TPU v7x, 128 devices: a whole 4x4x4 slice. The times are simulated.
128 devices in a mesh: row: 8 (over z, core), col: 16 (over x, y).
Axes of the slice: x: 4, y: 4, z: 4, core: 2. Of those that a mesh axis runs over, the one named last changes fastest.
Arguments:
- images: bfloat16 [8, 64, 65536], P(None, 'row', 'col'), may hold values from -6 to 6
- kernel: bfloat16 [3, 3, 1024, 1024], P(None, None, 'col', 'row'), may hold values from -0.09375 to 0.09375
- upstream: bfloat16 [8, 64, 65536], P(None, 'row', 'col'), may hold values from -6 to 6
Outputs:
- output_maps: bfloat16 [8, 64, 65536], P(None, 'row', 'col')
- input_grad: bfloat16 [8, 64, 65536], P(None, 'row', 'col')
- kernel_grad: float32 [3, 3, 1024, 1024], P(None, None, 'col', 'row')
All inputs are finite; a program needn't handle non-finite values.
Results may differ from a plain program's by a relative error of at most 0.001.
Values may be sent and summed in bfloat16 or wider, within the bound.
No kernel may reach another device: no remote copies, remote signals or barrier semaphores. Data moves between devices by JAX's collectives and lax.ppermute only.
A program may use at most 128 MiB of HBM per device.

v0:
```python
import functools

import jax
import jax.numpy as jnp
from jax import lax
from jax.experimental import pallas as pl
from jax.experimental.pallas import tpu as pltpu
from jax.sharding import Mesh, PartitionSpec as P


W = 64
LANES = 128
F32 = jnp.float32
BF16 = jnp.bfloat16
VMEM_LIMIT = 60 * 1024 * 1024

FIRST = [(0, 1), (1, 0), (2, 3), (3, 2)]
SECOND = [(1, 2), (2, 1), (3, 0), (0, 3)]
OPPOSITE = [(i, (i + 2) % 4) for i in range(4)]
SWAP = [(0, 1), (1, 0)]


def params():
    return pltpu.CompilerParams(vmem_limit_bytes=VMEM_LIMIT)


def lane_of(shape):
    return lax.broadcasted_iota(jnp.int32, shape, len(shape) - 1)


def row_of(shape):
    return lax.broadcasted_iota(jnp.int32, shape, len(shape) - 2)


def place_of(member, position):
    odd = lax.rem(position, 2)
    apart = lax.rem(member - position + 4, 4)
    return jnp.where(apart == 0, 0, jnp.where(apart == 2, 3, jnp.where(apart == 1, 1 + odd, 2 - odd)))


def pack_kernel(x_ref, o_ref, rows_ref, mix_ref):
    low = lane_of((32, LANES)) < W
    for q in range(4):
        for side in range(2):
            flat = x_ref[q + 4 * side].astype(F32)
            for p in range(32):
                rows_ref[side, :, p, :] = flat[:, p * LANES : (p + 1) * LANES]
        for h in range(8):
            first = rows_ref[0, h]
            second = rows_ref[1, h]
            mix_ref[h, pl.ds(0, 32, stride=2), :] = jnp.where(low, first, pltpu.roll(second, W, 1))
            mix_ref[h, pl.ds(1, 32, stride=2), :] = jnp.where(low, pltpu.roll(first, W, 1), second)
        for h in range(8):
            o_ref[q, :, h * LANES : (h + 1) * LANES] = mix_ref[h].astype(BF16)


def pack(x):
    return pl.pallas_call(
        pack_kernel,
        out_shape=jax.ShapeDtypeStruct((4, 64, 1024), BF16),
        in_specs=[pl.BlockSpec(memory_space=pltpu.VMEM)],
        out_specs=pl.BlockSpec(memory_space=pltpu.VMEM),
        scratch_shapes=[pltpu.VMEM((2, 8, 32, LANES), F32), pltpu.VMEM((8, 64, LANES), F32)],
        compiler_params=params(),
        name="pack",
    )(x)


ROWS = ((1, 2, 3, 4), (5, 6, 7, 0))


def finish_kernel(own_a, one_a, two_a, own_b, one_b, two_b, o_ref, mix_ref, rows_ref):
    low = lane_of((32, LANES)) < W
    for q in range(4):
        for rows, (own, one, two) in zip(ROWS, ((own_a, one_a, two_a), (own_b, one_b, two_b))):
            for j, h in enumerate(rows):
                lanes = slice(j * LANES, (j + 1) * LANES)
                mix_ref[h] = own[q, :, lanes] + one[0, q, :, lanes] + two[q, :, lanes]
        for h in range(8):
            even = mix_ref[h, pl.ds(0, 32, stride=2), :]
            odd = mix_ref[h, pl.ds(1, 32, stride=2), :]
            rows_ref[0, h] = jnp.where(low, even, pltpu.roll(odd, W, 1))
            rows_ref[1, h] = jnp.where(low, pltpu.roll(even, W, 1), odd)
        for side in range(2):
            for p in range(32):
                o_ref[q + 4 * side, :, p * LANES : (p + 1) * LANES] = rows_ref[side, :, p, :].astype(BF16)


def finish(*pieces):
    single = pl.BlockSpec((4, 64, 512), lambda i: (0, 0, 0))
    double = pl.BlockSpec((1, 4, 64, 512), lambda i: (0, 0, 0, 0))
    return pl.pallas_call(
        finish_kernel,
        out_shape=jax.ShapeDtypeStruct((8, 8, 4096), BF16),
        grid=(1,),
        in_specs=[single, double, single] * 2,
        out_specs=pl.BlockSpec((8, 8, 4096), lambda i: (0, 0, 0)),
        scratch_shapes=[pltpu.VMEM((8, 64, LANES), F32), pltpu.VMEM((2, 8, 32, LANES), F32)],
        compiler_params=params(),
        name="finish",
    )(*pieces)


def weights_kernel(at, mine, other, w_ref, wt_ref, whole):
    z, core, x, y = at[0], at[1], at[2], at[3]
    for ref, side in ((mine, core), (other, 1 - core)):
        for k in range(2):
            member = lax.rem(z + 8 - 2 * k - side, 4)
            rows = pl.ds(pl.multiple_of(place_of(member, x) * 64, 64), 64)
            for tap in range(9):
                for which, half in ((0, side), (1, 1 - side)):
                    lanes = pl.ds(pl.multiple_of(half * LANES, LANES), LANES)
                    whole[tap, rows, lanes] = ref[k, which, tap]
    listed, channel = row_of((256, 256)), lane_of((256, 256))
    order = jnp.where(
        (place_of(channel // 64, y) == listed // 64) & (channel % 64 == listed % 64), 1.0, 0.0
    ).astype(BF16)
    across = (((1,), (1,)), ((), ()))
    for tap in range(9):
        straight = lax.dot_general(whole[tap], order, across, preferred_element_type=F32).astype(BF16)
        turned = lax.dot_general(order, whole[tap], across, preferred_element_type=F32).astype(BF16)
        a, c = tap // 3, tap % 3
        w_ref[a, :, c * 256 : (c + 1) * 256] = straight
        wt_ref[2 - a, :, (2 - c) * 256 : (3 - c) * 256] = turned


def arrange_weights(at, mine, other):
    shape = jax.ShapeDtypeStruct((3, 256, 768), BF16)
    return pl.pallas_call(
        weights_kernel,
        out_shape=(shape, shape),
        in_specs=[pl.BlockSpec(memory_space=pltpu.SMEM)] + [pl.BlockSpec(memory_space=pltpu.VMEM)] * 2,
        out_specs=[pl.BlockSpec(memory_space=pltpu.VMEM)] * 2,
        scratch_shapes=[pltpu.VMEM((9, 256, 256), BF16)],
        compiler_params=params(),
        name="weights",
    )(at, mine, other)


def lay_shifted(chunks, top, bottom, rows, shifted):
    column = lane_of((64, LANES)) % W
    not_first = jnp.where(column == 0, 0.0, 1.0).astype(BF16)
    not_last = jnp.where(column == W - 1, 0.0, 1.0).astype(BF16)
    for k in range(4):
        at = k * 64
        for j, h in enumerate(rows):
            if h == -1:
                tile = top[k, 0]
            elif h == 8:
                tile = bottom[k, 0]
            else:
                tile = chunks[k][0, :, h * LANES : (h + 1) * LANES]
            lanes = slice(j * LANES, (j + 1) * LANES)
            shifted[at : at + 64, lanes] = pltpu.roll(tile, 1, 1) * not_first
            shifted[256 + at : 320 + at, lanes] = tile
            shifted[512 + at : 576 + at, lanes] = pltpu.roll(tile, LANES - 1, 1) * not_last


def conv_kernel(half, at, c0, c1, c2, c3, *refs):
    top, bottom = refs[:2] if half else (None, None)
    w_ref, own, following, send, shifted = refs[2 * half :]
    rows = (4, 5, 6, 7, 8, -1, 0, 1) if half else (0, 1, 2, 3, 4, 5)
    lay_shifted((c0, c1, c2, c3), top, bottom, rows, shifted)
    for n in range(2):
        part = None
        for a in range(3):
            first = 2 * n + a
            second = 5 + a if half and n else first + 1
            source = jnp.concatenate(
                [shifted[:, i * LANES : (i + 1) * LANES] for i in (first, second)], axis=1
            )
            term = jnp.dot(w_ref[a], source, preferred_element_type=F32)
            part = term if part is None else part + term
        lanes = slice(n * 256, (n + 1) * 256)
        own[0, :, lanes] = part[0:64]
        first_out, second_out = (following.at[0], send.at[0, 0]) if half else (send.at[0, 0], following.at[0])
        first_out[:, lanes] = part[64:128]
        second_out[:, lanes] = part[128:192]
        send[1, 0, :, lanes] = part[192:256]


def conv(half, at, chunks, sides, weights):
    single = jax.ShapeDtypeStruct((4, 64, 512), F32)
    double = jax.ShapeDtypeStruct((2, 4, 64, 512), F32)
    chunk = pl.BlockSpec((1, 64, 1024), lambda q: (q, 0, 0))
    edge = pl.BlockSpec((4, 1, 64, LANES), lambda q: (0, q, 0, 0))
    one = pl.BlockSpec((1, 64, 512), lambda q: (q, 0, 0))
    two = pl.BlockSpec((2, 1, 64, 512), lambda q: (0, q, 0, 0))
    sides = sides if half else ()
    return pl.pallas_call(
        functools.partial(conv_kernel, half),
        out_shape=(single, single, double),
        grid=(4,),
        in_specs=[pl.BlockSpec(memory_space=pltpu.SMEM)]
        + [chunk] * 4
        + [edge] * len(sides)
        + [pl.BlockSpec((3, 256, 768), lambda q: (0, 0, 0))],
        out_specs=[one, one, two],
        scratch_shapes=[pltpu.VMEM((768, 1024 if half else 768), BF16)],
        compiler_params=params(),
        cost_estimate=pl.CostEstimate(flops=2415919104, bytes_accessed=6000000, transcendentals=0),
    )(at, *chunks, *sides, weights)


def kernel_grad_kernel(at, x0, x1, x2, x3, top, bottom, g0, g1, g2, g3, mine, other, shifted, grads, total):
    z, core, x, y = at[0], at[1], at[2], at[3]
    q = pl.program_id(0)
    lay_shifted((x0, x1, x2, x3), top, bottom, range(-1, 9), shifted)
    for k, g_ref in enumerate((g0, g1, g2, g3)):
        grads[k * 64 : (k + 1) * 64, :] = g_ref[0]

    @pl.when(q == 0)
    def _():
        total[...] = jnp.zeros_like(total)

    for a in range(3):
        total[a] += lax.dot_general(
            grads[...],
            shifted[:, a * LANES : a * LANES + 1024],
            (((1,), (1,)), ((), ())),
            preferred_element_type=F32,
        )

    @pl.when(q == 3)
    def _():
        for half, o_ref in ((core, mine), (1 - core, other)):
            second = jnp.where(half == y // 2, 0, 1)
            straight = second == lax.rem(y, 2)
            for k in range(4):
                member = lax.rem(z + (0, 1, 3, 2)[k], 4)
                rows = pl.ds(pl.multiple_of(place_of(member, x) * 64, 64), 64)
                for a in range(3):
                    for c in range(3):
                        lanes = pl.ds(pl.multiple_of(c * 256 + second * LANES, LANES), LANES)
                        tile = total[a, rows, lanes]
                        o_ref[k, a * 3 + c] = jnp.where(straight, tile, pltpu.roll(tile, W, 1))


def weight_grads(at, chunks, top, bottom, grads):
    shape = jax.ShapeDtypeStruct((4, 9, 64, LANES), F32)
    chunk = pl.BlockSpec((1, 64, 1024), lambda q: (q, 0, 0))
    edge = pl.BlockSpec((4, 1, 64, LANES), lambda q: (0, q, 0, 0))
    whole = pl.BlockSpec((4, 9, 64, LANES), lambda q: (0, 0, 0, 0))
    return pl.pallas_call(
        kernel_grad_kernel,
        out_shape=(shape,) * 2,
        grid=(4,),
        in_specs=[pl.BlockSpec(memory_space=pltpu.SMEM)] + [chunk] * 4 + [edge] * 2 + [chunk] * 4,
        out_specs=[whole] * 2,
        scratch_shapes=[
            pltpu.VMEM((768, 1280), BF16),
            pltpu.VMEM((256, 1024), BF16),
            pltpu.VMEM((3, 256, 768), F32),
        ],
        compiler_params=params(),
        cost_estimate=pl.CostEstimate(flops=4831838208, bytes_accessed=9000000, transcendentals=0),
        name="weight_grads",
    )(at, *chunks, top, bottom, *grads)


def ring(step):
    return [(i, (i + step) % 4) for i in range(4)]


def after(value, *others):
    return lax.optimization_barrier((value, *others))[0]


def gather(block, axis):
    return (
        block, lax.ppermute(block, axis, FIRST), lax.ppermute(block, axis, SECOND), lax.ppermute(block, axis, OPPOSITE)
    )


def edges(chunks):
    forward = [(i, i + 1) for i in range(7)]
    backward = [(j, i) for i, j in forward]
    last = jnp.stack([chunk[:, :, -LANES:] for chunk in chunks])
    first = jnp.stack([chunk[:, :, :LANES] for chunk in chunks])
    return (lax.ppermute(last, ("z", "core"), forward), lax.ppermute(first, ("z", "core"), backward))


def reduce_second(a, b, one_a, one_b, axis):
    two_a = lax.ppermute(a[1] + one_a[1], axis, SECOND)
    two_b = lax.ppermute(b[1] + one_b[1], axis, FIRST)
    return finish(a[0], one_a, two_a, b[0], one_b, two_b)


def fetch_weights(at, block):
    both = jnp.stack([block, lax.ppermute(block, "core", SWAP)])
    got = []
    for k in range(2):
        pairs = [
            ((z * 2 + s) * 4 + x, (((x + 2 * k + s) % 4) * 2 + s) * 4 + z)
            for z in range(4)
            for s in range(2)
            for x in range(4)
        ]
        got.append(lax.ppermute(both, ("z", "core", "x"), pairs))
    got = jnp.stack(got)
    return arrange_weights(at, got, lax.ppermute(got, "core", SWAP))


def step(images, kernel, upstream):
    at = jnp.stack([lax.axis_index(n) for n in ("z", "core", "x", "y")]).astype(jnp.int32)
    weights, turned = fetch_weights(at, kernel.reshape(9, 64, LANES))
    x = pack(images)
    x_chunks = gather(x, "y")
    g = pack(upstream)
    g_chunks = gather(g, "x")

    x_sides = edges(x_chunks)
    g_sides = edges(g_chunks)
    out_a = conv(0, at, x_chunks, x_sides, weights)
    out_one_a = lax.ppermute(out_a[2], "x", FIRST)
    out_b = conv(1, after(at, out_a[0]), x_chunks, x_sides, weights)
    out_one_b = lax.ppermute(out_b[2], "x", SECOND)
    grad_a = conv(0, after(at, out_b[0]), g_chunks, g_sides, turned)
    grad_one_a = lax.ppermute(grad_a[2], "y", FIRST)
    grad_b = conv(1, after(at, grad_a[0]), g_chunks, g_sides, turned)
    grad_one_b = lax.ppermute(grad_b[2], "y", SECOND)

    near, far = weight_grads(after(at, grad_b[0]), x_chunks, *x_sides, g_chunks)
    near = near + lax.ppermute(far, "core", SWAP)
    output_maps = reduce_second(out_a, out_b, out_one_a, out_one_b, "x")
    input_grad = reduce_second(grad_a, grad_b, grad_one_a, grad_one_b, "y")
    total = near[0]
    for k, turn in ((1, 1), (2, 3), (3, 2)):
        total = total + lax.ppermute(near[k], "z", ring(turn))
    cross = [(z * 4 + x, x * 4 + z) for z in range(4) for x in range(4)]
    kernel_grad = lax.ppermute(total, ("z", "x"), cross).reshape(3, 3, 64, LANES)
    return output_maps, input_grad, kernel_grad


def solution(mesh):
    fine = Mesh(mesh.devices.reshape(4, 2, 4, 4), ("z", "core", "x", "y"))
    row, col = ("z", "core"), ("x", "y")
    flat = P(None, row, col)
    taps = P(None, None, col, row)
    return jax.shard_map(step, mesh=fine, in_specs=(flat, taps, flat), out_specs=(flat, flat, taps), check_vma=False)
```

profile of v0, /device:TPU:6, one launch (start us, length us, event | category | flops | bytes accessed | tf_op | source)
XLA Modules:
  0.0 174.7 jit_solution(7930374036594994851)
XLA Ops:
  0.6 3.1 %pack.2.c0.x0 = bf16[4,64,1024]{2,1,0:T(8,128)(2,1)} custom-call(bf16[8,8,4096]{2,1,0:T(8,128)(2,1)} %x_ref.2), custom_call_target="tpu_custom_call" | custom-call | tf_op jit(solution)/shard_map/pack/pallas_call | solution.py:58
  3.8 1.6 collective-permute-start
  5.3 2.2 %collective-permute-start.1 = (bf16[4,64,1024]{2,1,0:T(8,128)(2,1)}, bf16[4,64,1024]{2,1,0:T(8,128)(2,1)}, u32[]{:S(2)}, u32[]{:S(2)}) collective-permute-start(bf16[4,64,1024]{2,1,0:T(8,128)(2,1)} %pack.2.c0.x0), channel_id=1, source_target_pairs={{1,2},{2,1},{3,0},{0,3},{5,6},{6,5},{7,4},{4,7},{9,10},{10,9},{11,... | collective-permute-start | bytes 1572872 | tf_op jit(solution)/shard_map/ppermute | solution.py:271
  7.5 0.7 collective-permute-start.2
  8.3 3.1 %pack.3.c0.g0 = bf16[4,64,1024]{2,1,0:T(8,128)(2,1)} custom-call(bf16[8,8,4096]{2,1,0:T(8,128)(2,1)} %x_ref.3), custom_call_target="tpu_custom_call" | custom-call | tf_op jit(solution)/shard_map/pack/pallas_call | solution.py:58
  11.4 0.9 slice_bitcast_fusion.19
  12.4 1.9 %collective-permute-start.5 = (bf16[2,9,64,128]{3,2,1,0:T(8,128)(2,1)S(1)}, bf16[2,9,64,128]{3,2,1,0:T(8,128)(2,1)S(1)}, u32[]{:S(2)}, u32[]{:S(2)}) collective-permute-start(bf16[2,9,64,128]{3,2,1,0:T(8,128)(2,1)S(1)} %pad_maximum_fusion.1), channel_id=1, source_target_pairs={{0,64},{4,96},{8,0},{12,32},{16,112},{20,16},{24,48},{28,80},{32,6... | collective-permute-start | bytes 884744 | tf_op jit(solution)/shard_map/ppermute | solution.py:299
  14.3 6.6 %collective-permute-start.4 = (bf16[2,9,64,128]{3,2,1,0:T(8,128)(2,1)S(1)}, bf16[2,9,64,128]{3,2,1,0:T(8,128)(2,1)S(1)}, u32[]{:S(2)}, u32[]{:S(2)}) collective-permute-start(bf16[2,9,64,128]{3,2,1,0:T(8,128)(2,1)S(1)} %pad_maximum_fusion.1), channel_id=1, source_target_pairs={{0,0},{4,32},{8,64},{12,96},{16,48},{20,80},{24,112},{28,16},{32,4... | collective-permute-start | bytes 884744 | tf_op jit(solution)/shard_map/ppermute | solution.py:299
  20.9 0.9 slice_bitcast_fusion.11
  22.4 13.6 %collective-permute-done.5 = bf16[2,9,64,128]{3,2,1,0:T(8,128)(2,1)S(1)} collective-permute-done((bf16[2,9,64,128]{3,2,1,0:T(8,128)(2,1)S(1)}, bf16[2,9,64,128]{3,2,1,0:T(8,128)(2,1)S(1)}, u32[]{:S(2)}, u32[]{:S(2)}) %collective-permute-start.5) | collective-permute-done | bytes 294944 | tf_op jit(solution)/shard_map/ppermute | solution.py:299
  36.1 7.0 %collective-permute-start.13 = (bf16[4,64,1024]{2,1,0:T(8,128)(2,1)}, bf16[4,64,1024]{2,1,0:T(8,128)(2,1)S(1)}, u32[]{:S(2)}, u32[]{:S(2)}) collective-permute-start(bf16[4,64,1024]{2,1,0:T(8,128)(2,1)} %pack.3.c0.g0), channel_id=1, source_target_pairs={{0,4},{4,0},{8,12},{12,8},{1,5},{5,1},{9,13},{13,9},{2,6},{6,2},{1... | collective-permute-start | bytes 1572872 | tf_op jit(solution)/shard_map/ppermute | solution.py:271
  43.1 3.2 %collective-permute-done.4 = bf16[2,9,64,128]{3,2,1,0:T(8,128)(2,1)S(1)} collective-permute-done((bf16[2,9,64,128]{3,2,1,0:T(8,128)(2,1)S(1)}, bf16[2,9,64,128]{3,2,1,0:T(8,128)(2,1)S(1)}, u32[]{:S(2)}, u32[]{:S(2)}) %collective-permute-start.4) | collective-permute-done | bytes 294944 | tf_op jit(solution)/shard_map/ppermute | solution.py:299
  46.5 1.0 slice_bitcast_fusion.16
  47.6 0.9 slice_bitcast_fusion.17
  48.5 2.4 %collective-permute-start.9 = (bf16[4,4,64,128]{3,2,1,0:T(8,128)(2,1)S(1)}, bf16[4,4,64,128]{3,2,1,0:T(8,128)(2,1)S(1)}, u32[]{:S(2)}, u32[]{:S(2)}) collective-permute-start(bf16[4,4,64,128]{3,2,1,0:T(8,128)(2,1)S(1)} %pad_maximum_fusion.2), channel_id=1, source_target_pairs={{0,16},{16,32},{32,48},{48,64},{64,80},{80,96},{96,112},{1,17},{17... | collective-permute-start | bytes 786440 | tf_op jit(solution)/shard_map/ppermute | solution.py:280
  51.0 10.8 %collective-permute-done.15.c3.g3 = bf16[4,64,1024]{2,1,0:T(8,128)(2,1)S(1)} collective-permute-done((bf16[4,64,1024]{2,1,0:T(8,128)(2,1)S(1)}, bf16[4,64,1024]{2,1,0:T(8,128)(2,1)S(1)}, u32[]{:S(2)}, u32[]{:S(2)}) %collective-permute-start.15) | collective-permute-done | bytes 524320 | tf_op jit(solution)/shard_map/ppermute | solution.py:271
  61.8 1.3 collective-permute-start.10
  63.1 6.4 %collective-permute-done.14.c2.g2 = bf16[4,64,1024]{2,1,0:T(8,128)(2,1)S(1)} collective-permute-done((bf16[4,64,1024]{2,1,0:T(8,128)(2,1)}, bf16[4,64,1024]{2,1,0:T(8,128)(2,1)S(1)}, u32[]{:S(2)}, u32[]{:S(2)}) %collective-permute-start.14) | collective-permute-done | bytes 524320 | tf_op jit(solution)/shard_map/ppermute | solution.py:271
  69.7 2.0 %collective-permute-start.18 = (bf16[4,4,64,128]{3,2,1,0:T(8,128)(2,1)S(1)}, bf16[4,4,64,128]{3,2,1,0:T(8,128)(2,1)}, u32[]{:S(2)}, u32[]{:S(2)}) collective-permute-start(bf16[4,4,64,128]{3,2,1,0:T(8,128)(2,1)S(1)} %pad_maximum_fusion.4), channel_id=1, source_target_pairs={{0,16},{16,32},{32,48},{48,64},{64,80},{80,96},{96,112},{1,17},{17... | collective-permute-start | bytes 786440 | tf_op jit(solution)/shard_map/ppermute | solution.py:280
  71.7 1.3 collective-permute-start.19
  73.1 0.8 copy-done.7
  73.9 3.7 %weights.1 = (bf16[3,256,768]{2,1,0:T(8,128)(2,1)}, bf16[3,256,768]{2,1,0:T(8,128)(2,1)}) custom-call(s32[4]{0:T(128)} %pad_add_fusion.at, bf16[2,2,9,64,128]{4,3,2,1,0:T(8,128)(2,1)} %copy-done, bf16[2,2,9,64,128]{4,3,2,1,0:T(8,128)(2,1)} %copy-done.7), custom_call_target="tpu_custom_call" | custom-call | tf_op jit(solution)/shard_map/weights/pallas_call | solution.py:129
  77.5 6.5 %shard_map.58 = (f32[4,64,512]{2,1,0:T(8,128)}, f32[4,64,512]{2,1,0:T(8,128)}, f32[2,4,64,512]{3,2,1,0:T(8,128)}) custom-call(s32[4]{0:T(128)} %pad_add_fusion.at, bf16[4,64,1024]{2,1,0:T(8,128)(2,1)} %pack.2.c0.x0, bf16[4,64,1024]{2,1,0:T(8,128)(2,1)} %copy-done.17, bf16[4,64,1024]{2,1,0:T(8,128)(2,1)} %collective-permute-done.1.c2.x2, ...), custom_call_target="tpu_custom_call" | custom-call | flops 2415919104 | bytes 6000000 | tf_op jit(solution)/shard_map/pallas_call | solution.py:190
  84.7 6.6 %shard_map.59 = (f32[4,64,512]{2,1,0:T(8,128)}, f32[4,64,512]{2,1,0:T(8,128)}, f32[2,4,64,512]{3,2,1,0:T(8,128)}) custom-call(s32[4]{0:T(128)} %pad_add_fusion.at, bf16[4,64,1024]{2,1,0:T(8,128)(2,1)} %pack.2.c0.x0, bf16[4,64,1024]{2,1,0:T(8,128)(2,1)} %copy-done.17, bf16[4,64,1024]{2,1,0:T(8,128)(2,1)} %collective-permute-done.1.c2.x2, ...), custom_call_target="tpu_custom_call" | custom-call | flops 2415919104 | bytes 6000000 | tf_op jit(solution)/shard_map/pallas_call | solution.py:190
  91.3 3.2 %collective-permute-start.11 = (f32[2,4,64,512]{3,2,1,0:T(8,128)}, f32[2,4,64,512]{3,2,1,0:T(8,128)S(1)}, u32[]{:S(2)}, u32[]{:S(2)}) collective-permute-start(f32[2,4,64,512]{3,2,1,0:T(8,128)} %get-tuple-element.29), channel_id=1, source_target_pairs={{4,8},{8,4},{12,0},{0,12},{5,9},{9,5},{13,1},{1,13},{6,10},{10,6},... | collective-permute-start | bytes 3145736 | tf_op jit(solution)/shard_map/ppermute | solution.py:317
  94.5 6.5 %shard_map.60 = (f32[4,64,512]{2,1,0:T(8,128)}, f32[4,64,512]{2,1,0:T(8,128)}, f32[2,4,64,512]{3,2,1,0:T(8,128)}) custom-call(s32[4]{0:T(128)} %pad_add_fusion.at, bf16[4,64,1024]{2,1,0:T(8,128)(2,1)} %pack.3.c0.g0, bf16[4,64,1024]{2,1,0:T(8,128)(2,1)} %copy-done.18, bf16[4,64,1024]{2,1,0:T(8,128)(2,1)} %copy-done.19, bf16[4,64,1024]{2,1,0:T(8,128)(2,1)} %copy-done.20, ...), custom_call_target="tpu_custom_call" | custom-call | flops 2415919104 | bytes 6000000 | tf_op jit(solution)/shard_map/pallas_call | solution.py:190
  101.7 6.6 %shard_map.61 = (f32[4,64,512]{2,1,0:T(8,128)}, f32[4,64,512]{2,1,0:T(8,128)}, f32[2,4,64,512]{3,2,1,0:T(8,128)}) custom-call(s32[4]{0:T(128)} %pad_add_fusion.at, bf16[4,64,1024]{2,1,0:T(8,128)(2,1)} %pack.3.c0.g0, bf16[4,64,1024]{2,1,0:T(8,128)(2,1)} %copy-done.18, bf16[4,64,1024]{2,1,0:T(8,128)(2,1)} %copy-done.19, bf16[4,64,1024]{2,1,0:T(8,128)(2,1)} %copy-done.20, ...), custom_call_target="tpu_custom_call" | custom-call | flops 2415919104 | bytes 6000000 | tf_op jit(solution)/shard_map/pallas_call | solution.py:190
  108.3 11.3 %weight_grads.1 = (f32[4,9,64,128]{3,2,1,0:T(8,128)}, f32[4,9,64,128]{3,2,1,0:T(8,128)}) custom-call(s32[4]{0:T(128)} %pad_add_fusion.at, bf16[4,64,1024]{2,1,0:T(8,128)(2,1)} %pack.2.c0.x0, bf16[4,64,1024]{2,1,0:T(8,128)(2,1)} %copy-done.17, bf16[4,64,1024]{2,1,0:T(8,128)(2,1)} %collective-permute-done.1.c2.x2, ...), custom_call_target="tpu_custom_call" | custom-call | flops 4831838208 | bytes 9000000 | tf_op jit(solution)/shard_map/weight_grads/pallas_call | solution.py:244
  119.6 0.9 collective-permute-start.22
  120.5 1.2 collective-permute-start.16
  121.7 2.2 %collective-permute-start.20 = (f32[2,4,64,512]{3,2,1,0:T(8,128)}, f32[2,4,64,512]{3,2,1,0:T(8,128)S(1)}, u32[]{:S(2)}, u32[]{:S(2)}) collective-permute-start(f32[2,4,64,512]{3,2,1,0:T(8,128)} %get-tuple-element.38), channel_id=1, source_target_pairs={{1,2},{2,1},{3,0},{0,3},{5,6},{6,5},{7,4},{4,7},{9,10},{10,9},{11,... | collective-permute-start | bytes 3145736 | tf_op jit(solution)/shard_map/ppermute | solution.py:321
  124.9 1.0 copy-done.5
  126.2 1.6 collective-permute-start.25
  127.8 2.0 %collective-permute-start.24 = (f32[9,64,128]{2,1,0:T(8,128)S(1)}, f32[9,64,128]{2,1,0:T(8,128)S(1)}, u32[]{:S(2)}, u32[]{:S(2)}) collective-permute-start(f32[9,64,128]{2,1,0:T(8,128)S(1)} %get-tuple-element.45), channel_id=1, source_target_pairs={{0,96},{32,0},{64,32},{96,64},{1,97},{33,1},{65,33},{97,65},{2,98}... | collective-permute-start | bytes 884744 | tf_op jit(solution)/shard_map/ppermute | solution.py:329
  129.8 15.9 %collective-permute-done.16.one_a = f32[2,4,64,512]{3,2,1,0:T(8,128)S(1)} collective-permute-done((f32[2,4,64,512]{3,2,1,0:T(8,128)S(1)}, f32[2,4,64,512]{3,2,1,0:T(8,128)S(1)}, u32[]{:S(2)}, u32[]{:S(2)}) %collective-permute-start.16) | collective-permute-done | bytes 1048608 | tf_op jit(solution)/shard_map/ppermute | solution.py:319
  145.7 1.1 collective-permute-start.23
  146.8 1.1 collective-permute-done.20.one_b
  148.0 1.1 collective-permute-start.12
  149.2 2.3 %collective-permute-start.17 = (f32[4,64,512]{2,1,0:T(8,128)S(1)}, f32[4,64,512]{2,1,0:T(8,128)S(1)}, u32[]{:S(2)}, u32[]{:S(2)}) collective-permute-start(f32[4,64,512]{2,1,0:T(8,128)S(1)} %fusion.1), channel_id=1, source_target_pairs={{1,2},{2,1},{3,0},{0,3},{5,6},{6,5},{7,4},{4,7},{9,10},{10,9},{11,... | collective-permute-start | bytes 1572872 | tf_op jit(solution)/shard_map/ppermute | solution.py:284
  151.5 3.6 %collective-permute-done.23 = f32[9,64,128]{2,1,0:T(8,128)S(1)} collective-permute-done((f32[9,64,128]{2,1,0:T(8,128)S(1)}, f32[9,64,128]{2,1,0:T(8,128)S(1)}, u32[]{:S(2)}, u32[]{:S(2)}) %collective-permute-start.23) | collective-permute-done | bytes 294944 | tf_op jit(solution)/shard_map/ppermute | solution.py:329
  155.1 3.0 %collective-permute-start.26 = (f32[9,64,128]{2,1,0:T(8,128)S(1)}, f32[9,64,128]{2,1,0:T(8,128)S(1)}, u32[]{:S(2)}, u32[]{:S(2)}) collective-permute-start(f32[9,64,128]{2,1,0:T(8,128)S(1)} %fusion.6), channel_id=1, source_target_pairs={{0,0},{4,32},{8,64},{12,96},{32,4},{36,36},{40,68},{44,100},{64,8}... | collective-permute-start | bytes 884744 | tf_op jit(solution)/shard_map/ppermute | solution.py:331
  158.2 4.6 %collective-permute-done.12.two_b = f32[4,64,512]{2,1,0:T(8,128)S(1)} collective-permute-done((f32[4,64,512]{2,1,0:T(8,128)S(1)}, f32[4,64,512]{2,1,0:T(8,128)S(1)}, u32[]{:S(2)}, u32[]{:S(2)}) %collective-permute-start.12) | collective-permute-done | bytes 524320 | tf_op jit(solution)/shard_map/ppermute | solution.py:285
  162.8 0.8 copy-done.14
  163.6 4.0 %finish.2 = bf16[8,8,4096]{2,1,0:T(8,128)(2,1)} custom-call(f32[4,64,512]{2,1,0:T(8,128)} %get-tuple-element.24.own_a, f32[2,4,64,512]{3,2,1,0:T(8,128)} %copy-done.1, f32[4,64,512]{2,1,0:T(8,128)} %copy-done.8, f32[4,64,512]{2,1,0:T(8,128)} %get-tuple-element.28.own_b, f32[2,4,64,512]{3,2,1,0:T(8,128)} %copy-done.2, f32[4,64,512]{2,1,0:T(8,128)} %copy-done.14), custom_call_target="tpu_custom_call" | custom-call | tf_op jit(solution)/shard_map/finish/pallas_call | solution.py:92
  167.6 0.8 copy-done.13
  168.4 0.8 copy-done.15
  169.2 4.0 %finish.3 = bf16[8,8,4096]{2,1,0:T(8,128)(2,1)} custom-call(f32[4,64,512]{2,1,0:T(8,128)} %get-tuple-element.33.own_a, f32[2,4,64,512]{3,2,1,0:T(8,128)} %copy-done.3, f32[4,64,512]{2,1,0:T(8,128)} %copy-done.13, f32[4,64,512]{2,1,0:T(8,128)} %get-tuple-element.37.own_b, f32[2,4,64,512]{3,2,1,0:T(8,128)} %copy-done.4, f32[4,64,512]{2,1,0:T(8,128)} %copy-done.15), custom_call_target="tpu_custom_call" | custom-call | tf_op jit(solution)/shard_map/finish/pallas_call | solution.py:92
  173.2 0.7 collective-permute-done.26
  (87 shorter events, 4.9 us)
Async XLA Ops:
  0.6 11.7 %copy-start.16 = (bf16[3,3,64,128]{3,2,1,0:T(8,128)(2,1)S(1)}, bf16[3,3,64,128]{3,2,1,0:T(8,128)(2,1)}, u32[]{:S(2)}) copy-start(bf16[3,3,64,128]{3,2,1,0:T(8,128)(2,1)} %param.4) | copy-start | bytes 442372
  3.8 44.7 %collective-permute-start = (bf16[4,64,1024]{2,1,0:T(8,128)(2,1)}, bf16[4,64,1024]{2,1,0:T(8,128)(2,1)S(1)}, u32[]{:S(2)}, u32[]{:S(2)}) collective-permute-start(bf16[4,64,1024]{2,1,0:T(8,128)(2,1)} %pack.2.c0.x0), channel_id=1, source_target_pairs={{0,1},{1,0},{2,3},{3,2},{4,5},{5,4},{6,7},{7,6},{8,9},{9,8},{10,11... | collective-permute-start | bytes 1572872 | tf_op jit(solution)/shard_map/ppermute | solution.py:271
  5.3 42.1 %collective-permute-start.1 = (bf16[4,64,1024]{2,1,0:T(8,128)(2,1)}, bf16[4,64,1024]{2,1,0:T(8,128)(2,1)}, u32[]{:S(2)}, u32[]{:S(2)}) collective-permute-start(bf16[4,64,1024]{2,1,0:T(8,128)(2,1)} %pack.2.c0.x0), channel_id=1, source_target_pairs={{1,2},{2,1},{3,0},{0,3},{5,6},{6,5},{7,4},{4,7},{9,10},{10,9},{11,... | collective-permute-start | bytes 1572872 | tf_op jit(solution)/shard_map/ppermute | solution.py:271
  7.5 38.8 %collective-permute-start.2 = (bf16[4,64,1024]{2,1,0:T(8,128)(2,1)}, bf16[4,64,1024]{2,1,0:T(8,128)(2,1)}, u32[]{:S(2)}, u32[]{:S(2)}) collective-permute-start(bf16[4,64,1024]{2,1,0:T(8,128)(2,1)} %pack.2.c0.x0), channel_id=1, source_target_pairs={{0,2},{1,3},{2,0},{3,1},{4,6},{5,7},{6,4},{7,5},{8,10},{9,11},{10,... | collective-permute-start | bytes 1572872 | tf_op jit(solution)/shard_map/ppermute | solution.py:271
  8.2 4.0 %collective-permute-start.3 = (bf16[9,64,128]{2,1,0:T(8,128)(2,1)}, bf16[9,64,128]{2,1,0:T(8,128)(2,1)S(1)}, u32[]{:S(2)}, u32[]{:S(2)}) collective-permute-start(bf16[9,64,128]{2,1,0:T(8,128)(2,1)} %bitcast.75), channel_id=1, source_target_pairs={{0,16},{16,0},{1,17},{17,1},{2,18},{18,2},{3,19},{19,3},{4,20},{20... | collective-permute-start | bytes 442376 | tf_op jit(solution)/shard_map/ppermute | solution.py:290
  11.4 35.0 %copy-start.6 = (bf16[4,64,1024]{2,1,0:T(8,128)(2,1)S(1)}, bf16[4,64,1024]{2,1,0:T(8,128)(2,1)}, u32[]{:S(2)}) copy-start(bf16[4,64,1024]{2,1,0:T(8,128)(2,1)} %pack.3.c0.g0) | copy-start | bytes 1572868
  12.4 23.7 %collective-permute-start.5 = (bf16[2,9,64,128]{3,2,1,0:T(8,128)(2,1)S(1)}, bf16[2,9,64,128]{3,2,1,0:T(8,128)(2,1)S(1)}, u32[]{:S(2)}, u32[]{:S(2)}) collective-permute-start(bf16[2,9,64,128]{3,2,1,0:T(8,128)(2,1)S(1)} %pad_maximum_fusion.1), channel_id=1, source_target_pairs={{0,64},{4,96},{8,0},{12,32},{16,112},{20,16},{24,48},{28,80},{32,6... | collective-permute-start | bytes 884744 | tf_op jit(solution)/shard_map/ppermute | solution.py:299
  14.3 32.0 %collective-permute-start.4 = (bf16[2,9,64,128]{3,2,1,0:T(8,128)(2,1)S(1)}, bf16[2,9,64,128]{3,2,1,0:T(8,128)(2,1)S(1)}, u32[]{:S(2)}, u32[]{:S(2)}) collective-permute-start(bf16[2,9,64,128]{3,2,1,0:T(8,128)(2,1)S(1)} %pad_maximum_fusion.1), channel_id=1, source_target_pairs={{0,0},{4,32},{8,64},{12,96},{16,48},{20,80},{24,112},{28,16},{32,4... | collective-permute-start | bytes 884744 | tf_op jit(solution)/shard_map/ppermute | solution.py:299
  36.1 33.5 %collective-permute-start.13 = (bf16[4,64,1024]{2,1,0:T(8,128)(2,1)}, bf16[4,64,1024]{2,1,0:T(8,128)(2,1)S(1)}, u32[]{:S(2)}, u32[]{:S(2)}) collective-permute-start(bf16[4,64,1024]{2,1,0:T(8,128)(2,1)} %pack.3.c0.g0), channel_id=1, source_target_pairs={{0,4},{4,0},{8,12},{12,8},{1,5},{5,1},{9,13},{13,9},{2,6},{6,2},{1... | collective-permute-start | bytes 1572872 | tf_op jit(solution)/shard_map/ppermute | solution.py:271
  46.3 23.2 %collective-permute-start.14 = (bf16[4,64,1024]{2,1,0:T(8,128)(2,1)}, bf16[4,64,1024]{2,1,0:T(8,128)(2,1)S(1)}, u32[]{:S(2)}, u32[]{:S(2)}) collective-permute-start(bf16[4,64,1024]{2,1,0:T(8,128)(2,1)} %pack.3.c0.g0), channel_id=1, source_target_pairs={{4,8},{8,4},{12,0},{0,12},{5,9},{9,5},{13,1},{1,13},{6,10},{10,6},... | collective-permute-start | bytes 1572872 | tf_op jit(solution)/shard_map/ppermute | solution.py:271
  46.3 23.2 %copy-start = (bf16[2,2,9,64,128]{4,3,2,1,0:T(8,128)(2,1)}, bf16[2,2,9,64,128]{4,3,2,1,0:T(8,128)(2,1)S(1)}, u32[]{:S(2)}) copy-start(bf16[2,2,9,64,128]{4,3,2,1,0:T(8,128)(2,1)S(1)} %pad_maximum_fusion.mine) | copy-start | bytes 1769476
  46.4 15.4 %collective-permute-start.15 = (bf16[4,64,1024]{2,1,0:T(8,128)(2,1)S(1)}, bf16[4,64,1024]{2,1,0:T(8,128)(2,1)S(1)}, u32[]{:S(2)}, u32[]{:S(2)}) collective-permute-start(bf16[4,64,1024]{2,1,0:T(8,128)(2,1)S(1)} %copy-done.6), channel_id=1, source_target_pairs={{0,8},{4,12},{8,0},{12,4},{1,9},{5,13},{9,1},{13,5},{2,10},{6,14},... | collective-permute-start | bytes 1572872 | tf_op jit(solution)/shard_map/ppermute | solution.py:271
  47.5 25.6 %collective-permute-start.6 = (bf16[2,2,9,64,128]{4,3,2,1,0:T(8,128)(2,1)S(1)}, bf16[2,2,9,64,128]{4,3,2,1,0:T(8,128)(2,1)S(1)}, u32[]{:S(2)}, u32[]{:S(2)}) collective-permute-start(bf16[2,2,9,64,128]{4,3,2,1,0:T(8,128)(2,1)S(1)} %pad_maximum_fusion.mine), channel_id=1, source_target_pairs={{0,16},{16,0},{1,17},{17,1},{2,18},{18,2},{3,19},{19,3},{4,20},{20... | collective-permute-start | bytes 1769480 | tf_op jit(solution)/shard_map/ppermute | solution.py:301
  48.5 21.2 %copy-start.17 = (bf16[4,64,1024]{2,1,0:T(8,128)(2,1)}, bf16[4,64,1024]{2,1,0:T(8,128)(2,1)S(1)}, u32[]{:S(2)}) copy-start(bf16[4,64,1024]{2,1,0:T(8,128)(2,1)S(1)} %collective-permute-done.c1.x1) | copy-start | bytes 1572868
  48.5 35.5 %collective-permute-start.9 = (bf16[4,4,64,128]{3,2,1,0:T(8,128)(2,1)S(1)}, bf16[4,4,64,128]{3,2,1,0:T(8,128)(2,1)S(1)}, u32[]{:S(2)}, u32[]{:S(2)}) collective-permute-start(bf16[4,4,64,128]{3,2,1,0:T(8,128)(2,1)S(1)} %pad_maximum_fusion.2), channel_id=1, source_target_pairs={{0,16},{16,32},{32,48},{48,64},{64,80},{80,96},{96,112},{1,17},{17... | collective-permute-start | bytes 786440 | tf_op jit(solution)/shard_map/ppermute | solution.py:280
  61.8 11.2 %copy-start.20 = (bf16[4,64,1024]{2,1,0:T(8,128)(2,1)}, bf16[4,64,1024]{2,1,0:T(8,128)(2,1)S(1)}, u32[]{:S(2)}) copy-start(bf16[4,64,1024]{2,1,0:T(8,128)(2,1)S(1)} %collective-permute-done.15.c3.g3) | copy-start | bytes 1572868
  61.8 22.2 %collective-permute-start.10 = (bf16[4,4,64,128]{3,2,1,0:T(8,128)(2,1)S(1)}, bf16[4,4,64,128]{3,2,1,0:T(8,128)(2,1)}, u32[]{:S(2)}, u32[]{:S(2)}) collective-permute-start(bf16[4,4,64,128]{3,2,1,0:T(8,128)(2,1)S(1)} %pad_maximum_fusion.3), channel_id=1, source_target_pairs={{16,0},{32,16},{48,32},{64,48},{80,64},{96,80},{112,96},{17,1},{33... | collective-permute-start | bytes 786440 | tf_op jit(solution)/shard_map/ppermute | solution.py:280
  69.5 3.5 %copy-start.19 = (bf16[4,64,1024]{2,1,0:T(8,128)(2,1)}, bf16[4,64,1024]{2,1,0:T(8,128)(2,1)S(1)}, u32[]{:S(2)}) copy-start(bf16[4,64,1024]{2,1,0:T(8,128)(2,1)S(1)} %collective-permute-done.14.c2.g2) | copy-start | bytes 1572868
  69.6 3.5 %copy-start.18 = (bf16[4,64,1024]{2,1,0:T(8,128)(2,1)}, bf16[4,64,1024]{2,1,0:T(8,128)(2,1)S(1)}, u32[]{:S(2)}) copy-start(bf16[4,64,1024]{2,1,0:T(8,128)(2,1)S(1)} %collective-permute-done.13.c1.g1) | copy-start | bytes 1572868
  69.7 31.3 %collective-permute-start.18 = (bf16[4,4,64,128]{3,2,1,0:T(8,128)(2,1)S(1)}, bf16[4,4,64,128]{3,2,1,0:T(8,128)(2,1)}, u32[]{:S(2)}, u32[]{:S(2)}) collective-permute-start(bf16[4,4,64,128]{3,2,1,0:T(8,128)(2,1)S(1)} %pad_maximum_fusion.4), channel_id=1, source_target_pairs={{0,16},{16,32},{32,48},{48,64},{64,80},{80,96},{96,112},{1,17},{17... | collective-permute-start | bytes 786440 | tf_op jit(solution)/shard_map/ppermute | solution.py:280
  71.7 29.2 %collective-permute-start.19 = (bf16[4,4,64,128]{3,2,1,0:T(8,128)(2,1)S(1)}, bf16[4,4,64,128]{3,2,1,0:T(8,128)(2,1)S(1)}, u32[]{:S(2)}, u32[]{:S(2)}) collective-permute-start(bf16[4,4,64,128]{3,2,1,0:T(8,128)(2,1)S(1)} %pad_maximum_fusion.5), channel_id=1, source_target_pairs={{16,0},{32,16},{48,32},{64,48},{80,64},{96,80},{112,96},{17,1},{33... | collective-permute-start | bytes 786440 | tf_op jit(solution)/shard_map/ppermute | solution.py:280
  73.1 0.8 copy-start.7
  84.0 39.8 %collective-permute-start.7 = (f32[2,4,64,512]{3,2,1,0:T(8,128)}, f32[2,4,64,512]{3,2,1,0:T(8,128)S(1)}, u32[]{:S(2)}, u32[]{:S(2)}) collective-permute-start(f32[2,4,64,512]{3,2,1,0:T(8,128)} %get-tuple-element.25), channel_id=1, source_target_pairs={{0,4},{4,0},{8,12},{12,8},{1,5},{5,1},{9,13},{13,9},{2,6},{6,2},{1... | collective-permute-start | bytes 3145736 | tf_op jit(solution)/shard_map/ppermute | solution.py:315
  91.3 33.0 %collective-permute-start.11 = (f32[2,4,64,512]{3,2,1,0:T(8,128)}, f32[2,4,64,512]{3,2,1,0:T(8,128)S(1)}, u32[]{:S(2)}, u32[]{:S(2)}) collective-permute-start(f32[2,4,64,512]{3,2,1,0:T(8,128)} %get-tuple-element.29), channel_id=1, source_target_pairs={{4,8},{8,4},{12,0},{0,12},{5,9},{9,5},{13,1},{1,13},{6,10},{10,6},... | collective-permute-start | bytes 3145736 | tf_op jit(solution)/shard_map/ppermute | solution.py:317
  108.3 12.2 %copy-start.21 = (f32[2,4,64,512]{3,2,1,0:T(8,128)S(1)}, f32[2,4,64,512]{3,2,1,0:T(8,128)}, u32[]{:S(2)}) copy-start(f32[2,4,64,512]{3,2,1,0:T(8,128)} %get-tuple-element.34) | copy-start | bytes 3145732
  108.3 15.6 %copy-start.11 = (f32[4,64,512]{2,1,0:T(8,128)S(1)}, f32[4,64,512]{2,1,0:T(8,128)}, u32[]{:S(2)}) copy-start(f32[4,64,512]{2,1,0:T(8,128)} %get-tuple-element.26) | copy-start | bytes 1572868
  119.6 4.8 %copy-start.12 = (f32[4,64,512]{2,1,0:T(8,128)S(1)}, f32[4,64,512]{2,1,0:T(8,128)}, u32[]{:S(2)}) copy-start(f32[4,64,512]{2,1,0:T(8,128)} %get-tuple-element.30) | copy-start | bytes 1572868
  119.6 5.3 %collective-permute-start.22 = (f32[4,9,64,128]{3,2,1,0:T(8,128)}, f32[4,9,64,128]{3,2,1,0:T(8,128)S(1)}, u32[]{:S(2)}, u32[]{:S(2)}) collective-permute-start(f32[4,9,64,128]{3,2,1,0:T(8,128)} %get-tuple-element.42), channel_id=1, source_target_pairs={{0,16},{16,0},{1,17},{17,1},{2,18},{18,2},{3,19},{19,3},{4,20},{20... | collective-permute-start | bytes 3538952 | tf_op jit(solution)/shard_map/ppermute | solution.py:324
  120.5 25.2 %collective-permute-start.16 = (f32[2,4,64,512]{3,2,1,0:T(8,128)S(1)}, f32[2,4,64,512]{3,2,1,0:T(8,128)S(1)}, u32[]{:S(2)}, u32[]{:S(2)}) collective-permute-start(f32[2,4,64,512]{3,2,1,0:T(8,128)S(1)} %copy-done.21), channel_id=1, source_target_pairs={{0,1},{1,0},{2,3},{3,2},{4,5},{5,4},{6,7},{7,6},{8,9},{9,8},{10,11... | collective-permute-start | bytes 3145736 | tf_op jit(solution)/shard_map/ppermute | solution.py:319
  121.7 26.3 %collective-permute-start.20 = (f32[2,4,64,512]{3,2,1,0:T(8,128)}, f32[2,4,64,512]{3,2,1,0:T(8,128)S(1)}, u32[]{:S(2)}, u32[]{:S(2)}) collective-permute-start(f32[2,4,64,512]{3,2,1,0:T(8,128)} %get-tuple-element.38), channel_id=1, source_target_pairs={{1,2},{2,1},{3,0},{0,3},{5,6},{6,5},{7,4},{4,7},{9,10},{10,9},{11,... | collective-permute-start | bytes 3145736 | tf_op jit(solution)/shard_map/ppermute | solution.py:321
  123.9 1.0 copy-start.1
  123.9 2.0 %copy-start.5 = (f32[4,9,64,128]{3,2,1,0:T(8,128)S(1)}, f32[4,9,64,128]{3,2,1,0:T(8,128)}, u32[]{:S(2)}) copy-start(f32[4,9,64,128]{3,2,1,0:T(8,128)} %get-tuple-element.41) | copy-start | bytes 3538948
  124.0 34.2 %collective-permute-start.8 = (f32[4,64,512]{2,1,0:T(8,128)S(1)}, f32[4,64,512]{2,1,0:T(8,128)S(1)}, u32[]{:S(2)}, u32[]{:S(2)}) collective-permute-start(f32[4,64,512]{2,1,0:T(8,128)S(1)} %fusion.3), channel_id=1, source_target_pairs={{4,8},{8,4},{12,0},{0,12},{5,9},{9,5},{13,1},{1,13},{6,10},{10,6},... | collective-permute-start | bytes 1572872 | tf_op jit(solution)/shard_map/ppermute | solution.py:284
  124.3 1.8 %copy-start.2 = (f32[2,4,64,512]{3,2,1,0:T(8,128)}, f32[2,4,64,512]{3,2,1,0:T(8,128)S(1)}, u32[]{:S(2)}) copy-start(f32[2,4,64,512]{3,2,1,0:T(8,128)S(1)} %collective-permute-done.11.one_b) | copy-start | bytes 3145732
  126.1 20.6 %copy-start.9 = (f32[4,64,512]{2,1,0:T(8,128)S(1)}, f32[4,64,512]{2,1,0:T(8,128)}, u32[]{:S(2)}) copy-start(f32[4,64,512]{2,1,0:T(8,128)} %get-tuple-element.35) | copy-start | bytes 1572868
  126.2 22.9 %copy-start.10 = (f32[4,64,512]{2,1,0:T(8,128)S(1)}, f32[4,64,512]{2,1,0:T(8,128)}, u32[]{:S(2)}) copy-start(f32[4,64,512]{2,1,0:T(8,128)} %get-tuple-element.39) | copy-start | bytes 1572868
  126.2 22.9 %collective-permute-start.25 = (f32[9,64,128]{2,1,0:T(8,128)S(1)}, f32[9,64,128]{2,1,0:T(8,128)S(1)}, u32[]{:S(2)}, u32[]{:S(2)}) collective-permute-start(f32[9,64,128]{2,1,0:T(8,128)S(1)} %get-tuple-element.44), channel_id=1, source_target_pairs={{0,64},{32,96},{64,0},{96,32},{1,65},{33,97},{65,1},{97,33},{2,66}... | collective-permute-start | bytes 884744 | tf_op jit(solution)/shard_map/ppermute | solution.py:329
  127.8 23.7 %collective-permute-start.24 = (f32[9,64,128]{2,1,0:T(8,128)S(1)}, f32[9,64,128]{2,1,0:T(8,128)S(1)}, u32[]{:S(2)}, u32[]{:S(2)}) collective-permute-start(f32[9,64,128]{2,1,0:T(8,128)S(1)} %get-tuple-element.45), channel_id=1, source_target_pairs={{0,96},{32,0},{64,32},{96,64},{1,97},{33,1},{65,33},{97,65},{2,98}... | collective-permute-start | bytes 884744 | tf_op jit(solution)/shard_map/ppermute | solution.py:329
  145.7 3.5 %copy-start.3 = (f32[2,4,64,512]{3,2,1,0:T(8,128)}, f32[2,4,64,512]{3,2,1,0:T(8,128)S(1)}, u32[]{:S(2)}) copy-start(f32[2,4,64,512]{3,2,1,0:T(8,128)S(1)} %collective-permute-done.16.one_a) | copy-start | bytes 3145732
  145.7 9.4 %collective-permute-start.23 = (f32[9,64,128]{2,1,0:T(8,128)S(1)}, f32[9,64,128]{2,1,0:T(8,128)S(1)}, u32[]{:S(2)}, u32[]{:S(2)}) collective-permute-start(f32[9,64,128]{2,1,0:T(8,128)S(1)} %get-tuple-element.43), channel_id=1, source_target_pairs={{0,32},{32,64},{64,96},{96,0},{1,33},{33,65},{65,97},{97,1},{2,34}... | collective-permute-start | bytes 884744 | tf_op jit(solution)/shard_map/ppermute | solution.py:329
  148.0 7.1 %copy-start.4 = (f32[2,4,64,512]{3,2,1,0:T(8,128)}, f32[2,4,64,512]{3,2,1,0:T(8,128)S(1)}, u32[]{:S(2)}) copy-start(f32[2,4,64,512]{3,2,1,0:T(8,128)S(1)} %collective-permute-done.20.one_b) | copy-start | bytes 3145732
  148.0 14.8 %collective-permute-start.12 = (f32[4,64,512]{2,1,0:T(8,128)S(1)}, f32[4,64,512]{2,1,0:T(8,128)S(1)}, u32[]{:S(2)}, u32[]{:S(2)}) collective-permute-start(f32[4,64,512]{2,1,0:T(8,128)S(1)} %fusion.2), channel_id=1, source_target_pairs={{0,4},{4,0},{8,12},{12,8},{1,5},{5,1},{9,13},{13,9},{2,6},{6,2},{1... | collective-permute-start | bytes 1572872 | tf_op jit(solution)/shard_map/ppermute | solution.py:285
  149.2 18.4 %collective-permute-start.17 = (f32[4,64,512]{2,1,0:T(8,128)S(1)}, f32[4,64,512]{2,1,0:T(8,128)S(1)}, u32[]{:S(2)}, u32[]{:S(2)}) collective-permute-start(f32[4,64,512]{2,1,0:T(8,128)S(1)} %fusion.1), channel_id=1, source_target_pairs={{1,2},{2,1},{3,0},{0,3},{5,6},{6,5},{7,4},{4,7},{9,10},{10,9},{11,... | collective-permute-start | bytes 1572872 | tf_op jit(solution)/shard_map/ppermute | solution.py:284
  151.5 16.2 %collective-permute-start.21 = (f32[4,64,512]{2,1,0:T(8,128)S(1)}, f32[4,64,512]{2,1,0:T(8,128)S(1)}, u32[]{:S(2)}, u32[]{:S(2)}) collective-permute-start(f32[4,64,512]{2,1,0:T(8,128)S(1)} %fusion), channel_id=1, source_target_pairs={{0,1},{1,0},{2,3},{3,2},{4,5},{5,4},{6,7},{7,6},{8,9},{9,8},{10,11... | collective-permute-start | bytes 1572872 | tf_op jit(solution)/shard_map/ppermute | solution.py:285
  155.1 18.8 %collective-permute-start.26 = (f32[9,64,128]{2,1,0:T(8,128)S(1)}, f32[9,64,128]{2,1,0:T(8,128)S(1)}, u32[]{:S(2)}, u32[]{:S(2)}) collective-permute-start(f32[9,64,128]{2,1,0:T(8,128)S(1)} %fusion.6), channel_id=1, source_target_pairs={{0,0},{4,32},{8,64},{12,96},{32,4},{36,36},{40,68},{44,100},{64,8}... | collective-permute-start | bytes 884744 | tf_op jit(solution)/shard_map/ppermute | solution.py:331
  158.2 4.6 %copy-start.8 = (f32[4,64,512]{2,1,0:T(8,128)}, f32[4,64,512]{2,1,0:T(8,128)S(1)}, u32[]{:S(2)}) copy-start(f32[4,64,512]{2,1,0:T(8,128)S(1)} %collective-permute-done.8.two_a) | copy-start | bytes 1572868
  162.8 0.8 copy-start.14
  167.6 0.8 copy-start.13
  (3 other events, 2.2 us)
where the time goes:
time: 176 us; the launch traced here: 175 us
  waiting for transfers between devices  60 us (34%)
  Pallas kernels  55.3 us (31%)
  starting transfers between devices  46 us (26%)
  local copies, waits for them, and re-layouts  10.7 us (6%)
    pallas_call x4, Pallas kernels, conv(): pl.pallas_call(functools.partial(conv_kernel, half), out_shape=(single, s...  26.1 us
    ppermute x2, waiting for transfers between devices, fetch_weights(): got.append(lax.ppermute(both, ('z', 'core', 'x'), pairs))  16.8 us
    ppermute x1, waiting for transfers between devices, step(): grad_one_a = lax.ppermute(grad_a[2], 'y', FIRST)  15.9 us
    pallas_call x1, Pallas kernels, weight_grads(): pl.pallas_call(kernel_grad_kernel, out_shape=(shape,) * 2, grid=(4,), in_...  11.3 us
    ppermute x2, waiting for transfers between devices, gather(): lax.ppermute(block, axis, OPPOSITE)  10.8 us
    ppermute x2, starting transfers between devices, gather(): lax.ppermute(block, axis, FIRST)  8.59 us
    ppermute x2, starting transfers between devices, fetch_weights(): got.append(lax.ppermute(both, ('z', 'core', 'x'), pairs))  8.51 us
    pallas_call x2, Pallas kernels, finish(): pl.pallas_call(finish_kernel, out_shape=jax.ShapeDtypeStruct((8, 8, 4096)...  8.03 us
  transfers between devices with their start and end apart: 27, of which 9 were waited for; matrix products, arithmetic and copies ran while one was open for 3% of the time, Pallas kernels for 30%

commit v1 on v0

--- a/solution.py
+++ b/solution.py
@@ -12,7 +12,6 @@
 LANES = 128
 F32 = jnp.float32
 BF16 = jnp.bfloat16
-VMEM_LIMIT = 60 * 1024 * 1024
 
 FIRST = [(0, 1), (1, 0), (2, 3), (3, 2)]
 SECOND = [(1, 2), (2, 1), (3, 0), (0, 3)]
@@ -20,8 +19,8 @@
 SWAP = [(0, 1), (1, 0)]
 
 
-def params():
-    return pltpu.CompilerParams(vmem_limit_bytes=VMEM_LIMIT)
+def params(mib):
+    return pltpu.CompilerParams(vmem_limit_bytes=mib * 1024 * 1024)
 
 
 def lane_of(shape):
@@ -38,65 +37,117 @@
     return jnp.where(apart == 0, 0, jnp.where(apart == 2, 3, jnp.where(apart == 1, 1 + odd, 2 - odd)))
 
 
-def pack_kernel(x_ref, o_ref, rows_ref, mix_ref):
+def pack_kernel(x_hbm, g_hbm, x_out, g_out, taken, given, rows_ref, mix_ref, in_sem, out_sem):
     low = lane_of((32, LANES)) < W
+    pieces = [(t, q) for t in range(2) for q in range(4)]
+    ins, outs = (x_hbm, g_hbm), (x_out, g_out)
+
+    def fetch(t, q, side):
+        return pltpu.make_async_copy(ins[t].at[q + 4 * side], taken.at[t, q, side], in_sem.at[t, q, side])
+
+    def put(t, q):
+        return pltpu.make_async_copy(given.at[t, q], outs[t].at[q], out_sem.at[t, q])
+
+    for t, q in pieces:
+        for side in range(2):
+            fetch(t, q, side).start()
+    for t, q in pieces:
+        b = q % 2
+        for side in range(2):
+            fetch(t, q, side).wait()
+            flat = taken[t, q, side].astype(F32)
+            for p in range(32):
+                rows_ref[b, side, :, p, :] = flat[:, p * LANES : (p + 1) * LANES]
+        for h in range(8):
+            first = rows_ref[b, 0, h]
+            second = rows_ref[b, 1, h]
+            mix_ref[b, h, pl.ds(0, 32, stride=2), :] = jnp.where(low, first, pltpu.roll(second, W, 1))
+            mix_ref[b, h, pl.ds(1, 32, stride=2), :] = jnp.where(low, pltpu.roll(first, W, 1), second)
+        for h in range(8):
+            given[t, q, :, h * LANES : (h + 1) * LANES] = mix_ref[b, h].astype(BF16)
+        put(t, q).start()
+    for t, q in pieces:
+        put(t, q).wait()
+
+
+def pack(x, g):
+    shape = jax.ShapeDtypeStruct((4, 64, 1024), BF16)
+    anywhere = pl.BlockSpec(memory_space=pl.ANY)
+    return pl.pallas_call(
+        pack_kernel,
+        out_shape=(shape, shape),
+        in_specs=[pl.BlockSpec(memory_space=pltpu.HBM)] * 2,
+        out_specs=[anywhere] * 2,
+        scratch_shapes=[
+            pltpu.VMEM((2, 4, 2, 8, 4096), BF16),
+            pltpu.VMEM((2, 4, 64, 1024), BF16),
+            pltpu.VMEM((2, 2, 8, 32, LANES), F32),
+            pltpu.VMEM((2, 8, 64, LANES), F32),
+            pltpu.SemaphoreType.DMA((2, 4, 2)),
+            pltpu.SemaphoreType.DMA((2, 4)),
+        ],
+        compiler_params=params(8),
+        name="pack",
+    )(x, g)
+
+
+ROWS = ((1, 2, 3, 4), (5, 6, 7, 0))
+
+
+def finish_kernel(own_a, one_a, two_a, own_b, one_b, two_b, o_hbm, taken, given, mix_ref, rows_ref, in_sem, out_sem):
+    low = lane_of((32, LANES)) < W
+    pieces = ((own_a, one_a, two_a), (own_b, one_b, two_b))
+
+    def fetch(q, half, i):
+        ref = pieces[half][i]
+        source = ref.at[0, q] if i == 1 else ref.at[q]
+        return pltpu.make_async_copy(source, taken.at[q, half, i], in_sem.at[q, half, i])
+
+    def put(q, side):
+        return pltpu.make_async_copy(given.at[q, side], o_hbm.at[q + 4 * side], out_sem.at[q, side])
+
+    parts = [(half, i) for half in range(2) for i in range(3)]
+    for q in range(4):
+        for half, i in parts:
+            fetch(q, half, i).start()
+    for q in range(4):
+        b = q % 2
+        for half, i in parts:
+            fetch(q, half, i).wait()
+        for half, rows in enumerate(ROWS):
+            for j, h in enumerate(rows):
+                lanes = slice(j * LANES, (j + 1) * LANES)
+                mix_ref[b, h] = taken[q, half, 0, :, lanes] + taken[q, half, 1, :, lanes] + taken[q, half, 2, :, lanes]
+        for h in range(8):
+            even = mix_ref[b, h, pl.ds(0, 32, stride=2), :]
+            odd = mix_ref[b, h, pl.ds(1, 32, stride=2), :]
+            rows_ref[b, 0, h] = jnp.where(low, even, pltpu.roll(odd, W, 1))
+            rows_ref[b, 1, h] = jnp.where(low, pltpu.roll(even, W, 1), odd)
+        for side in range(2):
+            for p in range(32):
+                given[q, side, :, p * LANES : (p + 1) * LANES] = rows_ref[b, side, :, p, :].astype(BF16)
+            put(q, side).start()
     for q in range(4):
         for side in range(2):
-            flat = x_ref[q + 4 * side].astype(F32)
-            for p in range(32):
-                rows_ref[side, :, p, :] = flat[:, p * LANES : (p + 1) * LANES]
-        for h in range(8):
-            first = rows_ref[0, h]
-            second = rows_ref[1, h]
-            mix_ref[h, pl.ds(0, 32, stride=2), :] = jnp.where(low, first, pltpu.roll(second, W, 1))
-            mix_ref[h, pl.ds(1, 32, stride=2), :] = jnp.where(low, pltpu.roll(first, W, 1), second)
-        for h in range(8):
-            o_ref[q, :, h * LANES : (h + 1) * LANES] = mix_ref[h].astype(BF16)
-
-
-def pack(x):
-    return pl.pallas_call(
-        pack_kernel,
-        out_shape=jax.ShapeDtypeStruct((4, 64, 1024), BF16),
-        in_specs=[pl.BlockSpec(memory_space=pltpu.VMEM)],
-        out_specs=pl.BlockSpec(memory_space=pltpu.VMEM),
-        scratch_shapes=[pltpu.VMEM((2, 8, 32, LANES), F32), pltpu.VMEM((8, 64, LANES), F32)],
-        compiler_params=params(),
-        name="pack",
-    )(x)
-
-
-ROWS = ((1, 2, 3, 4), (5, 6, 7, 0))
-
-
-def finish_kernel(own_a, one_a, two_a, own_b, one_b, two_b, o_ref, mix_ref, rows_ref):
-    low = lane_of((32, LANES)) < W
-    for q in range(4):
-        for rows, (own, one, two) in zip(ROWS, ((own_a, one_a, two_a), (own_b, one_b, two_b))):
-            for j, h in enumerate(rows):
-                lanes = slice(j * LANES, (j + 1) * LANES)
-                mix_ref[h] = own[q, :, lanes] + one[0, q, :, lanes] + two[q, :, lanes]
-        for h in range(8):
-            even = mix_ref[h, pl.ds(0, 32, stride=2), :]
-            odd = mix_ref[h, pl.ds(1, 32, stride=2), :]
-            rows_ref[0, h] = jnp.where(low, even, pltpu.roll(odd, W, 1))
-            rows_ref[1, h] = jnp.where(low, pltpu.roll(even, W, 1), odd)
-        for side in range(2):
-            for p in range(32):
-                o_ref[q + 4 * side, :, p * LANES : (p + 1) * LANES] = rows_ref[side, :, p, :].astype(BF16)
+            put(q, side).wait()
 
 
 def finish(*pieces):
-    single = pl.BlockSpec((4, 64, 512), lambda i: (0, 0, 0))
-    double = pl.BlockSpec((1, 4, 64, 512), lambda i: (0, 0, 0, 0))
+    anywhere = pl.BlockSpec(memory_space=pl.ANY)
     return pl.pallas_call(
         finish_kernel,
         out_shape=jax.ShapeDtypeStruct((8, 8, 4096), BF16),
-        grid=(1,),
-        in_specs=[single, double, single] * 2,
-        out_specs=pl.BlockSpec((8, 8, 4096), lambda i: (0, 0, 0)),
-        scratch_shapes=[pltpu.VMEM((8, 64, LANES), F32), pltpu.VMEM((2, 8, 32, LANES), F32)],
-        compiler_params=params(),
+        in_specs=[anywhere] * 6,
+        out_specs=anywhere,
+        scratch_shapes=[
+            pltpu.VMEM((4, 2, 3, 64, 512), F32),
+            pltpu.VMEM((4, 2, 8, 4096), BF16),
+            pltpu.VMEM((2, 8, 64, LANES), F32),
+            pltpu.VMEM((2, 2, 8, 32, LANES), F32),
+            pltpu.SemaphoreType.DMA((4, 2, 3)),
+            pltpu.SemaphoreType.DMA((4, 2)),
+        ],
+        compiler_params=params(8),
         name="finish",
     )(*pieces)
 
@@ -132,7 +183,7 @@
         in_specs=[pl.BlockSpec(memory_space=pltpu.SMEM)] + [pl.BlockSpec(memory_space=pltpu.VMEM)] * 2,
         out_specs=[pl.BlockSpec(memory_space=pltpu.VMEM)] * 2,
         scratch_shapes=[pltpu.VMEM((9, 256, 256), BF16)],
-        compiler_params=params(),
+        compiler_params=params(20),
         name="weights",
     )(at, mine, other)
 
@@ -156,49 +207,52 @@
             shifted[512 + at : 576 + at, lanes] = pltpu.roll(tile, LANES - 1, 1) * not_last
 
 
-def conv_kernel(half, at, c0, c1, c2, c3, *refs):
-    top, bottom = refs[:2] if half else (None, None)
-    w_ref, own, following, send, shifted = refs[2 * half :]
-    rows = (4, 5, 6, 7, 8, -1, 0, 1) if half else (0, 1, 2, 3, 4, 5)
+def conv_kernel(halves, rows, at, c0, c1, c2, c3, *refs):
+    edged = 1 in halves
+    top, bottom = refs[:2] if edged else (None, None)
+    refs = refs[2 * edged :]
+    w_ref, shifted = refs[0], refs[-1]
     lay_shifted((c0, c1, c2, c3), top, bottom, rows, shifted)
-    for n in range(2):
-        part = None
-        for a in range(3):
-            first = 2 * n + a
-            second = 5 + a if half and n else first + 1
-            source = jnp.concatenate(
-                [shifted[:, i * LANES : (i + 1) * LANES] for i in (first, second)], axis=1
-            )
-            term = jnp.dot(w_ref[a], source, preferred_element_type=F32)
-            part = term if part is None else part + term
-        lanes = slice(n * 256, (n + 1) * 256)
-        own[0, :, lanes] = part[0:64]
-        first_out, second_out = (following.at[0], send.at[0, 0]) if half else (send.at[0, 0], following.at[0])
-        first_out[:, lanes] = part[64:128]
-        second_out[:, lanes] = part[128:192]
-        send[1, 0, :, lanes] = part[192:256]
-
-
-def conv(half, at, chunks, sides, weights):
+    for i, half in enumerate(halves):
+        own, following, send = refs[1 + 3 * i : 4 + 3 * i]
+        for n in range(2):
+            part = None
+            for a in range(3):
+                places = [rows.index(h - 1 + a) for h in ROWS[half][2 * n : 2 * n + 2]]
+                source = jnp.concatenate([shifted[:, j * LANES : (j + 1) * LANES] for j in places], axis=1)
+                term = jnp.dot(w_ref[a], source, preferred_element_type=F32)
+                part = term if part is None else part + term
+            lanes = slice(n * 256, (n + 1) * 256)
+            own[0, :, lanes] = part[0:64]
+            pair = (following.at[0], send.at[0, 0]) if half else (send.at[0, 0], following.at[0])
+            pair[0][:, lanes] = part[64:128]
+            pair[1][:, lanes] = part[128:192]
+            send[1, 0, :, lanes] = part[192:256]
+
+
+def conv(halves, at, chunks, sides, weights):
+    rows = {(0,): (0, 1, 2, 3, 4, 5), (1,): (4, 5, 6, 7, 8, -1, 0, 1)}.get(halves, tuple(range(-1, 9)))
     single = jax.ShapeDtypeStruct((4, 64, 512), F32)
     double = jax.ShapeDtypeStruct((2, 4, 64, 512), F32)
     chunk = pl.BlockSpec((1, 64, 1024), lambda q: (q, 0, 0))
     edge = pl.BlockSpec((4, 1, 64, LANES), lambda q: (0, q, 0, 0))
     one = pl.BlockSpec((1, 64, 512), lambda q: (q, 0, 0))
     two = pl.BlockSpec((2, 1, 64, 512), lambda q: (0, q, 0, 0))
-    sides = sides if half else ()
-    return pl.pallas_call(
-        functools.partial(conv_kernel, half),
-        out_shape=(single, single, double),
+    sides = sides if 1 in halves else ()
+    return pl.pallas_call(
+        functools.partial(conv_kernel, halves, rows),
+        out_shape=(single, single, double) * len(halves),
         grid=(4,),
         in_specs=[pl.BlockSpec(memory_space=pltpu.SMEM)]
         + [chunk] * 4
         + [edge] * len(sides)
         + [pl.BlockSpec((3, 256, 768), lambda q: (0, 0, 0))],
-        out_specs=[one, one, two],
-        scratch_shapes=[pltpu.VMEM((768, 1024 if half else 768), BF16)],
-        compiler_params=params(),
-        cost_estimate=pl.CostEstimate(flops=2415919104, bytes_accessed=6000000, transcendentals=0),
+        out_specs=[one, one, two] * len(halves),
+        scratch_shapes=[pltpu.VMEM((768, len(rows) * LANES), BF16)],
+        compiler_params=params(16),
+        cost_estimate=pl.CostEstimate(
+            flops=2415919104 * len(halves), bytes_accessed=6000000 * len(halves), transcendentals=0
+        ),
     )(at, *chunks, *sides, weights)
 
 
@@ -252,7 +306,7 @@
             pltpu.VMEM((256, 1024), BF16),
             pltpu.VMEM((3, 256, 768), F32),
         ],
-        compiler_params=params(),
+        compiler_params=params(20),
         cost_estimate=pl.CostEstimate(flops=4831838208, bytes_accessed=9000000, transcendentals=0),
         name="weight_grads",
     )(at, *chunks, top, bottom, *grads)
@@ -304,20 +358,19 @@
 def step(images, kernel, upstream):
     at = jnp.stack([lax.axis_index(n) for n in ("z", "core", "x", "y")]).astype(jnp.int32)
     weights, turned = fetch_weights(at, kernel.reshape(9, 64, LANES))
-    x = pack(images)
+    x, g = pack(images, upstream)
     x_chunks = gather(x, "y")
-    g = pack(upstream)
     g_chunks = gather(g, "x")
 
     x_sides = edges(x_chunks)
     g_sides = edges(g_chunks)
-    out_a = conv(0, at, x_chunks, x_sides, weights)
+    out = conv((0, 1), at, x_chunks, x_sides, weights)
+    out_a, out_b = out[:3], out[3:]
     out_one_a = lax.ppermute(out_a[2], "x", FIRST)
-    out_b = conv(1, after(at, out_a[0]), x_chunks, x_sides, weights)
     out_one_b = lax.ppermute(out_b[2], "x", SECOND)
-    grad_a = conv(0, after(at, out_b[0]), g_chunks, g_sides, turned)
+    grad_a = conv((0,), after(at, out_a[0]), g_chunks, g_sides, turned)
     grad_one_a = lax.ppermute(grad_a[2], "y", FIRST)
-    grad_b = conv(1, after(at, grad_a[0]), g_chunks, g_sides, turned)
+    grad_b = conv((1,), after(at, grad_a[0]), g_chunks, g_sides, turned)
     grad_one_b = lax.ppermute(grad_b[2], "y", SECOND)
 
     near, far = weight_grads(after(at, grad_b[0]), x_chunks, *x_sides, g_chunks)

time: 176 us -> 163 us (0.926)
  the two profiles are of different devices: /device:TPU:6 before, /device:TPU:1 now
where the time goes in v1:
time: 163 us; the launch traced here: 162 us
  waiting for transfers between devices  69.8 us (43%)
  Pallas kernels  45.2 us (28%)
  starting transfers between devices  40.3 us (25%)
  local copies, waits for them, and re-layouts  4.37 us (3%)
    ppermute x2, waiting for transfers between devices, fetch_weights(): got.append(lax.ppermute(both, ('z', 'core', 'x'), pairs))  24.2 us
    pallas_call x3, Pallas kernels, conv(): pl.pallas_call(functools.partial(conv_kernel, halves, rows), out_shape=(s...  16.3 us
    ppermute x1, waiting for transfers between devices, step(): grad_one_a = lax.ppermute(grad_a[2], 'y', FIRST)  14.3 us
    pallas_call x2, Pallas kernels, finish(): pl.pallas_call(finish_kernel, out_shape=jax.ShapeDtypeStruct((8, 8, 4096)...  13.1 us
    ppermute x2, waiting for transfers between devices, gather(): lax.ppermute(block, axis, OPPOSITE)  9.95 us
    pallas_call x1, Pallas kernels, weight_grads(): pl.pallas_call(kernel_grad_kernel, out_shape=(shape,) * 2, grid=(4,), in_...  9.01 us
    ppermute x2, starting transfers between devices, edges(): lax.ppermute(first, ('z', 'core'), backward)  7.78 us
    ppermute x2, starting transfers between devices, fetch_weights(): got.append(lax.ppermute(both, ('z', 'core', 'x'), pairs))  7.23 us
  transfers between devices with their start and end apart: 27, of which 12 were waited for; matrix products, arithmetic and copies ran while one was open for 2% of the time, Pallas kernels for 25%

profile of v1, /device:TPU:1, one launch (start us, length us, event | category | flops | bytes accessed | tf_op | source)
XLA Modules:
  0.0 161.6 jit_solution(5071812203050181214)
XLA Ops:
  0.6 1.0 copy-done
  1.7 1.0 copy-done.1
  2.7 5.3 %pack.1 = (bf16[4,64,1024]{2,1,0:T(8,128)(2,1)S(1)}, bf16[4,64,1024]{2,1,0:T(8,128)(2,1)S(1)}) custom-call(bf16[8,8,4096]{2,1,0:T(8,128)(2,1)S(1)} %copy-done, bf16[8,8,4096]{2,1,0:T(8,128)(2,1)S(1)} %copy-done.1), custom_call_target="tpu_custom_call" | custom-call | tf_op jit(solution)/shard_map/pack/pallas_call | solution.py:76
  8.0 2.2 %collective-permute-start = (bf16[4,64,1024]{2,1,0:T(8,128)(2,1)S(1)}, bf16[4,64,1024]{2,1,0:T(8,128)(2,1)S(1)}, u32[]{:S(2)}, u32[]{:S(2)}) collective-permute-start(bf16[4,64,1024]{2,1,0:T(8,128)(2,1)S(1)} %get-tuple-element.24.c0.x0), channel_id=1, source_target_pairs={{0,1},{1,0},{2,3},{3,2},{4,5},{5,4},{6,7},{7,6},{8,9},{9,8},{10,11... | collective-permute-start | bytes 1572872 | tf_op jit(solution)/shard_map/ppermute | solution.py:325
  10.2 1.9 %collective-permute-start.1 = (bf16[4,64,1024]{2,1,0:T(8,128)(2,1)S(1)}, bf16[4,64,1024]{2,1,0:T(8,128)(2,1)S(1)}, u32[]{:S(2)}, u32[]{:S(2)}) collective-permute-start(bf16[4,64,1024]{2,1,0:T(8,128)(2,1)S(1)} %get-tuple-element.24.c0.x0), channel_id=1, source_target_pairs={{1,2},{2,1},{3,0},{0,3},{5,6},{6,5},{7,4},{4,7},{9,10},{10,9},{11,... | collective-permute-start | bytes 1572872 | tf_op jit(solution)/shard_map/ppermute | solution.py:325
  12.1 0.7 collective-permute-start.2
  12.8 1.2 collective-permute-start.5
  14.0 0.7 slice_bitcast_fusion.22
  14.7 0.5 collective-permute-done.5
  15.3 3.8 %collective-permute-start.7 = (bf16[2,9,64,128]{3,2,1,0:T(8,128)(2,1)S(1)}, bf16[2,9,64,128]{3,2,1,0:T(8,128)(2,1)S(1)}, u32[]{:S(2)}, u32[]{:S(2)}) collective-permute-start(bf16[2,9,64,128]{3,2,1,0:T(8,128)(2,1)S(1)} %pad_maximum_fusion.1), channel_id=1, source_target_pairs={{0,64},{4,96},{8,0},{12,32},{16,112},{20,16},{24,48},{28,80},{32,6... | collective-permute-start | bytes 884744 | tf_op jit(solution)/shard_map/ppermute | solution.py:353
  19.1 3.4 %collective-permute-start.6 = (bf16[2,9,64,128]{3,2,1,0:T(8,128)(2,1)S(1)}, bf16[2,9,64,128]{3,2,1,0:T(8,128)(2,1)S(1)}, u32[]{:S(2)}, u32[]{:S(2)}) collective-permute-start(bf16[2,9,64,128]{3,2,1,0:T(8,128)(2,1)S(1)} %pad_maximum_fusion.1), channel_id=1, source_target_pairs={{0,0},{4,32},{8,64},{12,96},{16,48},{20,80},{24,112},{28,16},{32,4... | collective-permute-start | bytes 884744 | tf_op jit(solution)/shard_map/ppermute | solution.py:353
  22.5 0.7 slice_bitcast_fusion.20
  23.3 2.7 %collective-permute-done.7 = bf16[2,9,64,128]{3,2,1,0:T(8,128)(2,1)S(1)} collective-permute-done((bf16[2,9,64,128]{3,2,1,0:T(8,128)(2,1)S(1)}, bf16[2,9,64,128]{3,2,1,0:T(8,128)(2,1)S(1)}, u32[]{:S(2)}, u32[]{:S(2)}) %collective-permute-start.7) | collective-permute-done | bytes 294944 | tf_op jit(solution)/shard_map/ppermute | solution.py:353
  25.9 0.7 collective-permute-start.13
  26.6 21.5 %collective-permute-done.6 = bf16[2,9,64,128]{3,2,1,0:T(8,128)(2,1)S(1)} collective-permute-done((bf16[2,9,64,128]{3,2,1,0:T(8,128)(2,1)S(1)}, bf16[2,9,64,128]{3,2,1,0:T(8,128)(2,1)S(1)}, u32[]{:S(2)}, u32[]{:S(2)}) %collective-permute-start.6) | collective-permute-done | bytes 294944 | tf_op jit(solution)/shard_map/ppermute | solution.py:353
  48.2 0.1 collective-permute-start.15
  48.4 3.4 %collective-permute-start.8 = (bf16[2,2,9,64,128]{4,3,2,1,0:T(8,128)(2,1)S(1)}, bf16[2,2,9,64,128]{4,3,2,1,0:T(8,128)(2,1)S(1)}, u32[]{:S(2)}, u32[]{:S(2)}) collective-permute-start(bf16[2,2,9,64,128]{4,3,2,1,0:T(8,128)(2,1)S(1)} %pad_maximum_fusion.mine), channel_id=1, source_target_pairs={{0,16},{16,0},{1,17},{17,1},{2,18},{18,2},{3,19},{19,3},{4,20},{20... | collective-permute-start | bytes 1769480 | tf_op jit(solution)/shard_map/ppermute | solution.py:355
  51.8 1.9 %collective-permute-start.3 = (bf16[4,4,64,128]{3,2,1,0:T(8,128)(2,1)S(1)}, bf16[4,4,64,128]{3,2,1,0:T(8,128)(2,1)S(1)}, u32[]{:S(2)}, u32[]{:S(2)}) collective-permute-start(bf16[4,4,64,128]{3,2,1,0:T(8,128)(2,1)S(1)} %pad_maximum_fusion.2), channel_id=1, source_target_pairs={{0,16},{16,32},{32,48},{48,64},{64,80},{80,96},{96,112},{1,17},{17... | collective-permute-start | bytes 786440 | tf_op jit(solution)/shard_map/ppermute | solution.py:334
  53.8 9.9 %collective-permute-done.15.c3.g3 = bf16[4,64,1024]{2,1,0:T(8,128)(2,1)S(1)} collective-permute-done((bf16[4,64,1024]{2,1,0:T(8,128)(2,1)S(1)}, bf16[4,64,1024]{2,1,0:T(8,128)(2,1)S(1)}, u32[]{:S(2)}, u32[]{:S(2)}) %collective-permute-start.15) | collective-permute-done | bytes 524320 | tf_op jit(solution)/shard_map/ppermute | solution.py:325
  63.8 5.4 %collective-permute-start.4 = (bf16[4,4,64,128]{3,2,1,0:T(8,128)(2,1)S(1)}, bf16[4,4,64,128]{3,2,1,0:T(8,128)(2,1)S(1)}, u32[]{:S(2)}, u32[]{:S(2)}) collective-permute-start(bf16[4,4,64,128]{3,2,1,0:T(8,128)(2,1)S(1)} %pad_maximum_fusion.3), channel_id=1, source_target_pairs={{16,0},{32,16},{48,32},{64,48},{80,64},{96,80},{112,96},{17,1},{33... | collective-permute-start | bytes 786440 | tf_op jit(solution)/shard_map/ppermute | solution.py:334
  69.2 4.9 %collective-permute-done.14.c2.g2 = bf16[4,64,1024]{2,1,0:T(8,128)(2,1)S(1)} collective-permute-done((bf16[4,64,1024]{2,1,0:T(8,128)(2,1)S(1)}, bf16[4,64,1024]{2,1,0:T(8,128)(2,1)S(1)}, u32[]{:S(2)}, u32[]{:S(2)}) %collective-permute-start.14) | collective-permute-done | bytes 524320 | tf_op jit(solution)/shard_map/ppermute | solution.py:325
  74.2 1.9 %collective-permute-start.18 = (bf16[4,4,64,128]{3,2,1,0:T(8,128)(2,1)S(1)}, bf16[4,4,64,128]{3,2,1,0:T(8,128)(2,1)S(1)}, u32[]{:S(2)}, u32[]{:S(2)}) collective-permute-start(bf16[4,4,64,128]{3,2,1,0:T(8,128)(2,1)S(1)} %pad_maximum_fusion.4), channel_id=1, source_target_pairs={{0,16},{16,32},{32,48},{48,64},{64,80},{80,96},{96,112},{1,17},{17... | collective-permute-start | bytes 786440 | tf_op jit(solution)/shard_map/ppermute | solution.py:334
  76.1 2.4 %collective-permute-start.19 = (bf16[4,4,64,128]{3,2,1,0:T(8,128)(2,1)S(1)}, bf16[4,4,64,128]{3,2,1,0:T(8,128)(2,1)S(1)}, u32[]{:S(2)}, u32[]{:S(2)}) collective-permute-start(bf16[4,4,64,128]{3,2,1,0:T(8,128)(2,1)S(1)} %pad_maximum_fusion.5), channel_id=1, source_target_pairs={{16,0},{32,16},{48,32},{64,48},{80,64},{96,80},{112,96},{17,1},{33... | collective-permute-start | bytes 786440 | tf_op jit(solution)/shard_map/ppermute | solution.py:334
  78.6 1.6 weights.1
  80.2 7.1 %shard_map.58 = (f32[4,64,512]{2,1,0:T(8,128)S(1)}, f32[4,64,512]{2,1,0:T(8,128)S(1)}, f32[2,4,64,512]{3,2,1,0:T(8,128)S(1)}, f32[4,64,512]{2,1,0:T(8,128)S(1)},...) custom-call(s32[4]{0:T(128)S(1)} %pad_add_fusion.at, bf16[4,64,1024]{2,1,0:T(8,128)(2,1)S(1)} %get-tuple-element.24.c0.x0, ...), custom_call_target="tpu_custom_call" | custom-call | flops 4831838208 | bytes 12000000 | tf_op jit(solution)/shard_map/pallas_call | solution.py:242
  87.4 0.3 collective-permute-start.11
  87.6 4.5 %shard_map.59 = (f32[4,64,512]{2,1,0:T(8,128)S(1)}, f32[4,64,512]{2,1,0:T(8,128)S(1)}, f32[2,4,64,512]{3,2,1,0:T(8,128)S(1)}) custom-call(s32[4]{0:T(128)S(1)} %pad_add_fusion.at, bf16[4,64,1024]{2,1,0:T(8,128)(2,1)S(1)} %get-tuple-element.33.c0.g0, bf16[4,64,1024]{2,1,0:T(8,128)(2,1)S(1)} %collective-permute-done.13.c1.g1, ...), custom_call_target="tpu_custom_call" | custom-call | flops 2415919104 | bytes 6000000 | tf_op jit(solution)/shard_map/pallas_call | solution.py:242
  92.1 4.7 %shard_map.60 = (f32[4,64,512]{2,1,0:T(8,128)S(1)}, f32[4,64,512]{2,1,0:T(8,128)S(1)}, f32[2,4,64,512]{3,2,1,0:T(8,128)S(1)}) custom-call(s32[4]{0:T(128)S(1)} %pad_add_fusion.at, bf16[4,64,1024]{2,1,0:T(8,128)(2,1)S(1)} %get-tuple-element.33.c0.g0, bf16[4,64,1024]{2,1,0:T(8,128)(2,1)S(1)} %collective-permute-done.13.c1.g1, ...), custom_call_target="tpu_custom_call" | custom-call | flops 2415919104 | bytes 6000000 | tf_op jit(solution)/shard_map/pallas_call | solution.py:242
  96.9 9.0 %weight_grads.1 = (f32[4,9,64,128]{3,2,1,0:T(8,128)S(1)}, f32[4,9,64,128]{3,2,1,0:T(8,128)S(1)}) custom-call(s32[4]{0:T(128)S(1)} %pad_add_fusion.at, bf16[4,64,1024]{2,1,0:T(8,128)(2,1)S(1)} %get-tuple-element.24.c0.x0, bf16[4,64,1024]{2,1,0:T(8,128)(2,1)S(1)} %collective-permute-done.c1.x1, bf16[4,64,1024]{2,1,0:T(8,128)(2,1)S(1)} %collective-permute-done.1.c2.x2, ...), custom_call_target="tpu_custom_call" | custom-call | flops 4831838208 | bytes 9000000 | tf_op jit(solution)/shard_map/weight_grads/pallas_call | solution.py:298
  106.0 1.0 collective-permute-start.16
  107.0 1.9 %collective-permute-start.20 = (f32[2,4,64,512]{3,2,1,0:T(8,128)S(1)}, f32[2,4,64,512]{3,2,1,0:T(8,128)S(1)}, u32[]{:S(2)}, u32[]{:S(2)}) collective-permute-start(f32[2,4,64,512]{3,2,1,0:T(8,128)S(1)} %get-tuple-element.40), channel_id=1, source_target_pairs={{1,2},{2,1},{3,0},{0,3},{5,6},{6,5},{7,4},{4,7},{9,10},{10,9},{11,... | collective-permute-start | bytes 3145736 | tf_op jit(solution)/shard_map/ppermute | solution.py:374
  108.9 3.5 %collective-permute-done.9.one_a = f32[2,4,64,512]{3,2,1,0:T(8,128)S(1)} collective-permute-done((f32[2,4,64,512]{3,2,1,0:T(8,128)S(1)}, f32[2,4,64,512]{3,2,1,0:T(8,128)S(1)}, u32[]{:S(2)}, u32[]{:S(2)}) %collective-permute-start.9) | collective-permute-done | bytes 1048608 | tf_op jit(solution)/shard_map/ppermute | solution.py:369
  112.5 1.3 collective-permute-done.11.one_b
  113.9 0.2 add.28
  114.2 0.2 collective-permute-start.25
  114.3 1.7 %collective-permute-start.24 = (f32[9,64,128]{2,1,0:T(8,128)S(1)}, f32[9,64,128]{2,1,0:T(8,128)S(1)}, u32[]{:S(2)}, u32[]{:S(2)}) collective-permute-start(f32[9,64,128]{2,1,0:T(8,128)S(1)} %get-tuple-element.47), channel_id=1, source_target_pairs={{0,96},{32,0},{64,32},{96,64},{1,97},{33,1},{65,33},{97,65},{2,98}... | collective-permute-start | bytes 884744 | tf_op jit(solution)/shard_map/ppermute | solution.py:382
  116.0 14.3 %collective-permute-done.16.one_a = f32[2,4,64,512]{3,2,1,0:T(8,128)S(1)} collective-permute-done((f32[2,4,64,512]{3,2,1,0:T(8,128)S(1)}, f32[2,4,64,512]{3,2,1,0:T(8,128)S(1)}, u32[]{:S(2)}, u32[]{:S(2)}) %collective-permute-start.16) | collective-permute-done | bytes 1048608 | tf_op jit(solution)/shard_map/ppermute | solution.py:372
  130.4 1.6 collective-permute-start.23
  132.0 0.2 collective-permute-done.20.one_b
  132.2 1.4 collective-permute-start.12
  133.6 2.4 %collective-permute-start.17 = (f32[4,64,512]{2,1,0:T(8,128)S(1)}, f32[4,64,512]{2,1,0:T(8,128)S(1)}, u32[]{:S(2)}, u32[]{:S(2)}) collective-permute-start(f32[4,64,512]{2,1,0:T(8,128)S(1)} %fusion.1), channel_id=1, source_target_pairs={{1,2},{2,1},{3,0},{0,3},{5,6},{6,5},{7,4},{4,7},{9,10},{10,9},{11,... | collective-permute-start | bytes 1572872 | tf_op jit(solution)/shard_map/ppermute | solution.py:338
  136.1 2.8 %collective-permute-done.23 = f32[9,64,128]{2,1,0:T(8,128)S(1)} collective-permute-done((f32[9,64,128]{2,1,0:T(8,128)S(1)}, f32[9,64,128]{2,1,0:T(8,128)S(1)}, u32[]{:S(2)}, u32[]{:S(2)}) %collective-permute-start.23) | collective-permute-done | bytes 294944 | tf_op jit(solution)/shard_map/ppermute | solution.py:382
  138.9 0.7 collective-permute-start.26
  139.6 7.1 %collective-permute-done.17.two_a = f32[4,64,512]{2,1,0:T(8,128)S(1)} collective-permute-done((f32[4,64,512]{2,1,0:T(8,128)S(1)}, f32[4,64,512]{2,1,0:T(8,128)S(1)}, u32[]{:S(2)}, u32[]{:S(2)}) %collective-permute-start.17) | collective-permute-done | bytes 524320 | tf_op jit(solution)/shard_map/ppermute | solution.py:338
  146.8 1.0 collective-permute-done.21.two_b
  147.8 6.5 %finish.3 = bf16[8,8,4096]{2,1,0:T(8,128)(2,1)} custom-call(f32[4,64,512]{2,1,0:T(8,128)S(1)} %get-tuple-element.35.own_a, f32[2,4,64,512]{3,2,1,0:T(8,128)S(1)} %collective-permute-done.16.one_a, f32[4,64,512]{2,1,0:T(8,128)S(1)} %collective-permute-done.17.two_a, f32[4,64,512]{2,1,0:T(8,128)S(1)} %get-tuple-element.39.own_b, ...), custom_call_target="tpu_custom_call" | custom-call | tf_op jit(solution)/shard_map/finish/pallas_call | solution.py:137
  154.3 6.5 %finish.2 = bf16[8,8,4096]{2,1,0:T(8,128)(2,1)} custom-call(f32[4,64,512]{2,1,0:T(8,128)S(1)} %get-tuple-element.26.own_a, f32[2,4,64,512]{3,2,1,0:T(8,128)S(1)} %collective-permute-done.9.one_a, f32[4,64,512]{2,1,0:T(8,128)S(1)} %collective-permute-done.10.two_a, f32[4,64,512]{2,1,0:T(8,128)S(1)} %get-tuple-element.29.own_b, ...), custom_call_target="tpu_custom_call" | custom-call | tf_op jit(solution)/shard_map/finish/pallas_call | solution.py:137
  160.9 0.7 copy.7
  (51 shorter events, 1.2 us)
Async XLA Ops:
  0.6 1.0 copy-start
  1.7 1.0 copy-start.1
  2.7 12.5 %copy-start.6 = (bf16[3,3,64,128]{3,2,1,0:T(8,128)(2,1)S(1)}, bf16[3,3,64,128]{3,2,1,0:T(8,128)(2,1)}, u32[]{:S(2)}) copy-start(bf16[3,3,64,128]{3,2,1,0:T(8,128)(2,1)} %param.4) | copy-start | bytes 442372
  8.0 43.8 %collective-permute-start = (bf16[4,64,1024]{2,1,0:T(8,128)(2,1)S(1)}, bf16[4,64,1024]{2,1,0:T(8,128)(2,1)S(1)}, u32[]{:S(2)}, u32[]{:S(2)}) collective-permute-start(bf16[4,64,1024]{2,1,0:T(8,128)(2,1)S(1)} %get-tuple-element.24.c0.x0), channel_id=1, source_target_pairs={{0,1},{1,0},{2,3},{3,2},{4,5},{5,4},{6,7},{7,6},{8,9},{9,8},{10,11... | collective-permute-start | bytes 1572872 | tf_op jit(solution)/shard_map/ppermute | solution.py:325
  10.2 38.2 %collective-permute-start.1 = (bf16[4,64,1024]{2,1,0:T(8,128)(2,1)S(1)}, bf16[4,64,1024]{2,1,0:T(8,128)(2,1)S(1)}, u32[]{:S(2)}, u32[]{:S(2)}) collective-permute-start(bf16[4,64,1024]{2,1,0:T(8,128)(2,1)S(1)} %get-tuple-element.24.c0.x0), channel_id=1, source_target_pairs={{1,2},{2,1},{3,0},{0,3},{5,6},{6,5},{7,4},{4,7},{9,10},{10,9},{11,... | collective-permute-start | bytes 1572872 | tf_op jit(solution)/shard_map/ppermute | solution.py:325
  12.1 36.1 %collective-permute-start.2 = (bf16[4,64,1024]{2,1,0:T(8,128)(2,1)S(1)}, bf16[4,64,1024]{2,1,0:T(8,128)(2,1)S(1)}, u32[]{:S(2)}, u32[]{:S(2)}) collective-permute-start(bf16[4,64,1024]{2,1,0:T(8,128)(2,1)S(1)} %get-tuple-element.24.c0.x0), channel_id=1, source_target_pairs={{0,2},{1,3},{2,0},{3,1},{4,6},{5,7},{6,4},{7,5},{8,10},{9,11},{10,... | collective-permute-start | bytes 1572872 | tf_op jit(solution)/shard_map/ppermute | solution.py:325
  12.8 2.5 %collective-permute-start.5 = (bf16[9,64,128]{2,1,0:T(8,128)(2,1)}, bf16[9,64,128]{2,1,0:T(8,128)(2,1)S(1)}, u32[]{:S(2)}, u32[]{:S(2)}) collective-permute-start(bf16[9,64,128]{2,1,0:T(8,128)(2,1)} %bitcast.75), channel_id=1, source_target_pairs={{0,16},{16,0},{1,17},{17,1},{2,18},{18,2},{3,19},{19,3},{4,20},{20... | collective-permute-start | bytes 442376 | tf_op jit(solution)/shard_map/ppermute | solution.py:344
  15.3 10.7 %collective-permute-start.7 = (bf16[2,9,64,128]{3,2,1,0:T(8,128)(2,1)S(1)}, bf16[2,9,64,128]{3,2,1,0:T(8,128)(2,1)S(1)}, u32[]{:S(2)}, u32[]{:S(2)}) collective-permute-start(bf16[2,9,64,128]{3,2,1,0:T(8,128)(2,1)S(1)} %pad_maximum_fusion.1), channel_id=1, source_target_pairs={{0,64},{4,96},{8,0},{12,32},{16,112},{20,16},{24,48},{28,80},{32,6... | collective-permute-start | bytes 884744 | tf_op jit(solution)/shard_map/ppermute | solution.py:353
  19.1 29.0 %collective-permute-start.6 = (bf16[2,9,64,128]{3,2,1,0:T(8,128)(2,1)S(1)}, bf16[2,9,64,128]{3,2,1,0:T(8,128)(2,1)S(1)}, u32[]{:S(2)}, u32[]{:S(2)}) collective-permute-start(bf16[2,9,64,128]{3,2,1,0:T(8,128)(2,1)S(1)} %pad_maximum_fusion.1), channel_id=1, source_target_pairs={{0,0},{4,32},{8,64},{12,96},{16,48},{20,80},{24,112},{28,16},{32,4... | collective-permute-start | bytes 884744 | tf_op jit(solution)/shard_map/ppermute | solution.py:353
  23.2 28.6 %copy-start.5 = (bf16[1,4,64,128]{3,2,1,0:T(8,128)(2,1)S(1)}, bf16[1,4,64,128]{3,2,1,0:T(8,128)(2,1)}, u32[]{:S(2)}) copy-start(bf16[1,4,64,128]{3,2,1,0:T(8,128)(2,1)} %get-tuple-element.57) | copy-start | bytes 196612
  25.9 48.1 %collective-permute-start.13 = (bf16[4,64,1024]{2,1,0:T(8,128)(2,1)S(1)}, bf16[4,64,1024]{2,1,0:T(8,128)(2,1)S(1)}, u32[]{:S(2)}, u32[]{:S(2)}) collective-permute-start(bf16[4,64,1024]{2,1,0:T(8,128)(2,1)S(1)} %get-tuple-element.33.c0.g0), channel_id=1, source_target_pairs={{0,4},{4,0},{8,12},{12,8},{1,5},{5,1},{9,13},{13,9},{2,6},{6,2},{1... | collective-permute-start | bytes 1572872 | tf_op jit(solution)/shard_map/ppermute | solution.py:325
  48.1 25.9 %collective-permute-start.14 = (bf16[4,64,1024]{2,1,0:T(8,128)(2,1)S(1)}, bf16[4,64,1024]{2,1,0:T(8,128)(2,1)S(1)}, u32[]{:S(2)}, u32[]{:S(2)}) collective-permute-start(bf16[4,64,1024]{2,1,0:T(8,128)(2,1)S(1)} %get-tuple-element.33.c0.g0), channel_id=1, source_target_pairs={{4,8},{8,4},{12,0},{0,12},{5,9},{9,5},{13,1},{1,13},{6,10},{10,6},... | collective-permute-start | bytes 1572872 | tf_op jit(solution)/shard_map/ppermute | solution.py:325
  48.1 5.6 %copy-start.4 = (bf16[1,4,64,128]{3,2,1,0:T(8,128)(2,1)S(1)}, bf16[1,4,64,128]{3,2,1,0:T(8,128)(2,1)}, u32[]{:S(2)}) copy-start(bf16[1,4,64,128]{3,2,1,0:T(8,128)(2,1)} %get-tuple-element.56) | copy-start | bytes 196612
  48.2 15.6 %collective-permute-start.15 = (bf16[4,64,1024]{2,1,0:T(8,128)(2,1)S(1)}, bf16[4,64,1024]{2,1,0:T(8,128)(2,1)S(1)}, u32[]{:S(2)}, u32[]{:S(2)}) collective-permute-start(bf16[4,64,1024]{2,1,0:T(8,128)(2,1)S(1)} %get-tuple-element.33.c0.g0), channel_id=1, source_target_pairs={{0,8},{4,12},{8,0},{12,4},{1,9},{5,13},{9,1},{13,5},{2,10},{6,14},... | collective-permute-start | bytes 1572872 | tf_op jit(solution)/shard_map/ppermute | solution.py:325
  48.3 25.8 %copy-start.3 = (bf16[1,4,64,128]{3,2,1,0:T(8,128)(2,1)S(1)}, bf16[1,4,64,128]{3,2,1,0:T(8,128)(2,1)}, u32[]{:S(2)}) copy-start(bf16[1,4,64,128]{3,2,1,0:T(8,128)(2,1)} %get-tuple-element.49) | copy-start | bytes 196612
  48.4 30.2 %collective-permute-start.8 = (bf16[2,2,9,64,128]{4,3,2,1,0:T(8,128)(2,1)S(1)}, bf16[2,2,9,64,128]{4,3,2,1,0:T(8,128)(2,1)S(1)}, u32[]{:S(2)}, u32[]{:S(2)}) collective-permute-start(bf16[2,2,9,64,128]{4,3,2,1,0:T(8,128)(2,1)S(1)} %pad_maximum_fusion.mine), channel_id=1, source_target_pairs={{0,16},{16,0},{1,17},{17,1},{2,18},{18,2},{3,19},{19,3},{4,20},{20... | collective-permute-start | bytes 1769480 | tf_op jit(solution)/shard_map/ppermute | solution.py:355
  51.8 24.3 %copy-start.2 = (bf16[1,4,64,128]{3,2,1,0:T(8,128)(2,1)S(1)}, bf16[1,4,64,128]{3,2,1,0:T(8,128)(2,1)}, u32[]{:S(2)}) copy-start(bf16[1,4,64,128]{3,2,1,0:T(8,128)(2,1)} %get-tuple-element.48) | copy-start | bytes 196612
  51.8 28.3 %collective-permute-start.3 = (bf16[4,4,64,128]{3,2,1,0:T(8,128)(2,1)S(1)}, bf16[4,4,64,128]{3,2,1,0:T(8,128)(2,1)S(1)}, u32[]{:S(2)}, u32[]{:S(2)}) collective-permute-start(bf16[4,4,64,128]{3,2,1,0:T(8,128)(2,1)S(1)} %pad_maximum_fusion.2), channel_id=1, source_target_pairs={{0,16},{16,32},{32,48},{48,64},{64,80},{80,96},{96,112},{1,17},{17... | collective-permute-start | bytes 786440 | tf_op jit(solution)/shard_map/ppermute | solution.py:334
  63.8 16.4 %collective-permute-start.4 = (bf16[4,4,64,128]{3,2,1,0:T(8,128)(2,1)S(1)}, bf16[4,4,64,128]{3,2,1,0:T(8,128)(2,1)S(1)}, u32[]{:S(2)}, u32[]{:S(2)}) collective-permute-start(bf16[4,4,64,128]{3,2,1,0:T(8,128)(2,1)S(1)} %pad_maximum_fusion.3), channel_id=1, source_target_pairs={{16,0},{32,16},{48,32},{64,48},{80,64},{96,80},{112,96},{17,1},{33... | collective-permute-start | bytes 786440 | tf_op jit(solution)/shard_map/ppermute | solution.py:334
  74.2 17.9 %collective-permute-start.18 = (bf16[4,4,64,128]{3,2,1,0:T(8,128)(2,1)S(1)}, bf16[4,4,64,128]{3,2,1,0:T(8,128)(2,1)S(1)}, u32[]{:S(2)}, u32[]{:S(2)}) collective-permute-start(bf16[4,4,64,128]{3,2,1,0:T(8,128)(2,1)S(1)} %pad_maximum_fusion.4), channel_id=1, source_target_pairs={{0,16},{16,32},{32,48},{48,64},{64,80},{80,96},{96,112},{1,17},{17... | collective-permute-start | bytes 786440 | tf_op jit(solution)/shard_map/ppermute | solution.py:334
  76.1 16.0 %collective-permute-start.19 = (bf16[4,4,64,128]{3,2,1,0:T(8,128)(2,1)S(1)}, bf16[4,4,64,128]{3,2,1,0:T(8,128)(2,1)S(1)}, u32[]{:S(2)}, u32[]{:S(2)}) collective-permute-start(bf16[4,4,64,128]{3,2,1,0:T(8,128)(2,1)S(1)} %pad_maximum_fusion.5), channel_id=1, source_target_pairs={{16,0},{32,16},{48,32},{64,48},{80,64},{96,80},{112,96},{17,1},{33... | collective-permute-start | bytes 786440 | tf_op jit(solution)/shard_map/ppermute | solution.py:334
  87.3 25.1 %collective-permute-start.9 = (f32[2,4,64,512]{3,2,1,0:T(8,128)S(1)}, f32[2,4,64,512]{3,2,1,0:T(8,128)S(1)}, u32[]{:S(2)}, u32[]{:S(2)}) collective-permute-start(f32[2,4,64,512]{3,2,1,0:T(8,128)S(1)} %get-tuple-element.27), channel_id=1, source_target_pairs={{0,4},{4,0},{8,12},{12,8},{1,5},{5,1},{9,13},{13,9},{2,6},{6,2},{1... | collective-permute-start | bytes 3145736 | tf_op jit(solution)/shard_map/ppermute | solution.py:369
  87.4 26.5 %collective-permute-start.11 = (f32[2,4,64,512]{3,2,1,0:T(8,128)S(1)}, f32[2,4,64,512]{3,2,1,0:T(8,128)S(1)}, u32[]{:S(2)}, u32[]{:S(2)}) collective-permute-start(f32[2,4,64,512]{3,2,1,0:T(8,128)S(1)} %get-tuple-element.30), channel_id=1, source_target_pairs={{4,8},{8,4},{12,0},{0,12},{5,9},{9,5},{13,1},{1,13},{6,10},{10,6},... | collective-permute-start | bytes 3145736 | tf_op jit(solution)/shard_map/ppermute | solution.py:370
  105.9 8.0 %collective-permute-start.22 = (f32[4,9,64,128]{3,2,1,0:T(8,128)S(1)}, f32[4,9,64,128]{3,2,1,0:T(8,128)S(1)}, u32[]{:S(2)}, u32[]{:S(2)}) collective-permute-start(f32[4,9,64,128]{3,2,1,0:T(8,128)S(1)} %get-tuple-element.44), channel_id=1, source_target_pairs={{0,16},{16,0},{1,17},{17,1},{2,18},{18,2},{3,19},{19,3},{4,20},{20... | collective-permute-start | bytes 3538952 | tf_op jit(solution)/shard_map/ppermute | solution.py:377
  106.0 24.4 %collective-permute-start.16 = (f32[2,4,64,512]{3,2,1,0:T(8,128)S(1)}, f32[2,4,64,512]{3,2,1,0:T(8,128)S(1)}, u32[]{:S(2)}, u32[]{:S(2)}) collective-permute-start(f32[2,4,64,512]{3,2,1,0:T(8,128)S(1)} %get-tuple-element.36), channel_id=1, source_target_pairs={{0,1},{1,0},{2,3},{3,2},{4,5},{5,4},{6,7},{7,6},{8,9},{9,8},{10,11... | collective-permute-start | bytes 3145736 | tf_op jit(solution)/shard_map/ppermute | solution.py:372
  107.0 25.2 %collective-permute-start.20 = (f32[2,4,64,512]{3,2,1,0:T(8,128)S(1)}, f32[2,4,64,512]{3,2,1,0:T(8,128)S(1)}, u32[]{:S(2)}, u32[]{:S(2)}) collective-permute-start(f32[2,4,64,512]{3,2,1,0:T(8,128)S(1)} %get-tuple-element.40), channel_id=1, source_target_pairs={{1,2},{2,1},{3,0},{0,3},{5,6},{6,5},{7,4},{4,7},{9,10},{10,9},{11,... | collective-permute-start | bytes 3145736 | tf_op jit(solution)/shard_map/ppermute | solution.py:374
  112.4 41.9 %collective-permute-start.10 = (f32[4,64,512]{2,1,0:T(8,128)S(1)}, f32[4,64,512]{2,1,0:T(8,128)S(1)}, u32[]{:S(2)}, u32[]{:S(2)}) collective-permute-start(f32[4,64,512]{2,1,0:T(8,128)S(1)} %fusion.3), channel_id=1, source_target_pairs={{4,8},{8,4},{12,0},{0,12},{5,9},{9,5},{13,1},{1,13},{6,10},{10,6},... | collective-permute-start | bytes 1572872 | tf_op jit(solution)/shard_map/ppermute | solution.py:338
  114.2 19.5 %collective-permute-start.25 = (f32[9,64,128]{2,1,0:T(8,128)S(1)}, f32[9,64,128]{2,1,0:T(8,128)S(1)}, u32[]{:S(2)}, u32[]{:S(2)}) collective-permute-start(f32[9,64,128]{2,1,0:T(8,128)S(1)} %get-tuple-element.46), channel_id=1, source_target_pairs={{0,64},{32,96},{64,0},{96,32},{1,65},{33,97},{65,1},{97,33},{2,66}... | collective-permute-start | bytes 884744 | tf_op jit(solution)/shard_map/ppermute | solution.py:382
  114.3 21.7 %collective-permute-start.24 = (f32[9,64,128]{2,1,0:T(8,128)S(1)}, f32[9,64,128]{2,1,0:T(8,128)S(1)}, u32[]{:S(2)}, u32[]{:S(2)}) collective-permute-start(f32[9,64,128]{2,1,0:T(8,128)S(1)} %get-tuple-element.47), channel_id=1, source_target_pairs={{0,96},{32,0},{64,32},{96,64},{1,97},{33,1},{65,33},{97,65},{2,98}... | collective-permute-start | bytes 884744 | tf_op jit(solution)/shard_map/ppermute | solution.py:382
  130.4 8.5 %collective-permute-start.23 = (f32[9,64,128]{2,1,0:T(8,128)S(1)}, f32[9,64,128]{2,1,0:T(8,128)S(1)}, u32[]{:S(2)}, u32[]{:S(2)}) collective-permute-start(f32[9,64,128]{2,1,0:T(8,128)S(1)} %get-tuple-element.45), channel_id=1, source_target_pairs={{0,32},{32,64},{64,96},{96,0},{1,33},{33,65},{65,97},{97,1},{2,34}... | collective-permute-start | bytes 884744 | tf_op jit(solution)/shard_map/ppermute | solution.py:382
  132.2 22.1 %collective-permute-start.12 = (f32[4,64,512]{2,1,0:T(8,128)S(1)}, f32[4,64,512]{2,1,0:T(8,128)S(1)}, u32[]{:S(2)}, u32[]{:S(2)}) collective-permute-start(f32[4,64,512]{2,1,0:T(8,128)S(1)} %fusion.2), channel_id=1, source_target_pairs={{0,4},{4,0},{8,12},{12,8},{1,5},{5,1},{9,13},{13,9},{2,6},{6,2},{1... | collective-permute-start | bytes 1572872 | tf_op jit(solution)/shard_map/ppermute | solution.py:339
  133.6 13.1 %collective-permute-start.17 = (f32[4,64,512]{2,1,0:T(8,128)S(1)}, f32[4,64,512]{2,1,0:T(8,128)S(1)}, u32[]{:S(2)}, u32[]{:S(2)}) collective-permute-start(f32[4,64,512]{2,1,0:T(8,128)S(1)} %fusion.1), channel_id=1, source_target_pairs={{1,2},{2,1},{3,0},{0,3},{5,6},{6,5},{7,4},{4,7},{9,10},{10,9},{11,... | collective-permute-start | bytes 1572872 | tf_op jit(solution)/shard_map/ppermute | solution.py:338
  136.1 11.7 %collective-permute-start.21 = (f32[4,64,512]{2,1,0:T(8,128)S(1)}, f32[4,64,512]{2,1,0:T(8,128)S(1)}, u32[]{:S(2)}, u32[]{:S(2)}) collective-permute-start(f32[4,64,512]{2,1,0:T(8,128)S(1)} %fusion), channel_id=1, source_target_pairs={{0,1},{1,0},{2,3},{3,2},{4,5},{5,4},{6,7},{7,6},{8,9},{9,8},{10,11... | collective-permute-start | bytes 1572872 | tf_op jit(solution)/shard_map/ppermute | solution.py:339
  138.9 21.9 %collective-permute-start.26 = (f32[9,64,128]{2,1,0:T(8,128)S(1)}, f32[9,64,128]{2,1,0:T(8,128)S(1)}, u32[]{:S(2)}, u32[]{:S(2)}) collective-permute-start(f32[9,64,128]{2,1,0:T(8,128)S(1)} %fusion.6), channel_id=1, source_target_pairs={{0,0},{4,32},{8,64},{12,96},{32,4},{36,36},{40,68},{44,100},{64,8}... | collective-permute-start | bytes 884744 | tf_op jit(solution)/shard_map/ppermute | solution.py:384

commit v2 on v1

--- a/solution.py
+++ b/solution.py
@@ -37,25 +37,13 @@
     return jnp.where(apart == 0, 0, jnp.where(apart == 2, 3, jnp.where(apart == 1, 1 + odd, 2 - odd)))
 
 
-def pack_kernel(x_hbm, g_hbm, x_out, g_out, taken, given, rows_ref, mix_ref, in_sem, out_sem):
+def pack_kernel(x_ref, g_ref, x_out, g_out, rows_ref, mix_ref):
     low = lane_of((32, LANES)) < W
-    pieces = [(t, q) for t in range(2) for q in range(4)]
-    ins, outs = (x_hbm, g_hbm), (x_out, g_out)
-
-    def fetch(t, q, side):
-        return pltpu.make_async_copy(ins[t].at[q + 4 * side], taken.at[t, q, side], in_sem.at[t, q, side])
-
-    def put(t, q):
-        return pltpu.make_async_copy(given.at[t, q], outs[t].at[q], out_sem.at[t, q])
-
-    for t, q in pieces:
+    for i, (t, q) in enumerate((t, q) for t in range(2) for q in range(4)):
+        b = i % 2
+        source, target = ((x_ref, x_out), (g_ref, g_out))[t]
         for side in range(2):
-            fetch(t, q, side).start()
-    for t, q in pieces:
-        b = q % 2
-        for side in range(2):
-            fetch(t, q, side).wait()
-            flat = taken[t, q, side].astype(F32)
+            flat = source[q + 4 * side].astype(F32)
             for p in range(32):
                 rows_ref[b, side, :, p, :] = flat[:, p * LANES : (p + 1) * LANES]
         for h in range(8):
@@ -64,28 +52,18 @@
             mix_ref[b, h, pl.ds(0, 32, stride=2), :] = jnp.where(low, first, pltpu.roll(second, W, 1))
             mix_ref[b, h, pl.ds(1, 32, stride=2), :] = jnp.where(low, pltpu.roll(first, W, 1), second)
         for h in range(8):
-            given[t, q, :, h * LANES : (h + 1) * LANES] = mix_ref[b, h].astype(BF16)
-        put(t, q).start()
-    for t, q in pieces:
-        put(t, q).wait()
+            target[q, :, h * LANES : (h + 1) * LANES] = mix_ref[b, h].astype(BF16)
 
 
 def pack(x, g):
     shape = jax.ShapeDtypeStruct((4, 64, 1024), BF16)
-    anywhere = pl.BlockSpec(memory_space=pl.ANY)
+    near = pl.BlockSpec(memory_space=pltpu.VMEM)
     return pl.pallas_call(
         pack_kernel,
         out_shape=(shape, shape),
-        in_specs=[pl.BlockSpec(memory_space=pltpu.HBM)] * 2,
-        out_specs=[anywhere] * 2,
-        scratch_shapes=[
-            pltpu.VMEM((2, 4, 2, 8, 4096), BF16),
-            pltpu.VMEM((2, 4, 64, 1024), BF16),
-            pltpu.VMEM((2, 2, 8, 32, LANES), F32),
-            pltpu.VMEM((2, 8, 64, LANES), F32),
-            pltpu.SemaphoreType.DMA((2, 4, 2)),
-            pltpu.SemaphoreType.DMA((2, 4)),
-        ],
+        in_specs=[near] * 2,
+        out_specs=[near] * 2,
+        scratch_shapes=[pltpu.VMEM((2, 2, 8, 32, LANES), F32), pltpu.VMEM((2, 8, 64, LANES), F32)],
         compiler_params=params(8),
         name="pack",
     )(x, g)
@@ -94,30 +72,19 @@
 ROWS = ((1, 2, 3, 4), (5, 6, 7, 0))
 
 
-def finish_kernel(own_a, one_a, two_a, own_b, one_b, two_b, o_hbm, taken, given, mix_ref, rows_ref, in_sem, out_sem):
+def finish_kernel(own_a, one_a, two_a, own_b, one_b, two_b, o_hbm, given, mix_ref, rows_ref, out_sem):
     low = lane_of((32, LANES)) < W
     pieces = ((own_a, one_a, two_a), (own_b, one_b, two_b))
 
-    def fetch(q, half, i):
-        ref = pieces[half][i]
-        source = ref.at[0, q] if i == 1 else ref.at[q]
-        return pltpu.make_async_copy(source, taken.at[q, half, i], in_sem.at[q, half, i])
-
     def put(q, side):
         return pltpu.make_async_copy(given.at[q, side], o_hbm.at[q + 4 * side], out_sem.at[q, side])
 
-    parts = [(half, i) for half in range(2) for i in range(3)]
-    for q in range(4):
-        for half, i in parts:
-            fetch(q, half, i).start()
     for q in range(4):
         b = q % 2
-        for half, i in parts:
-            fetch(q, half, i).wait()
-        for half, rows in enumerate(ROWS):
+        for (own, one, two), rows in zip(pieces, ROWS):
             for j, h in enumerate(rows):
                 lanes = slice(j * LANES, (j + 1) * LANES)
-                mix_ref[b, h] = taken[q, half, 0, :, lanes] + taken[q, half, 1, :, lanes] + taken[q, half, 2, :, lanes]
+                mix_ref[b, h] = own[q, :, lanes] + one[0, q, :, lanes] + two[q, :, lanes]
         for h in range(8):
             even = mix_ref[b, h, pl.ds(0, 32, stride=2), :]
             odd = mix_ref[b, h, pl.ds(1, 32, stride=2), :]
@@ -133,21 +100,18 @@
 
 
 def finish(*pieces):
-    anywhere = pl.BlockSpec(memory_space=pl.ANY)
     return pl.pallas_call(
         finish_kernel,
         out_shape=jax.ShapeDtypeStruct((8, 8, 4096), BF16),
-        in_specs=[anywhere] * 6,
-        out_specs=anywhere,
+        in_specs=[pl.BlockSpec(memory_space=pltpu.VMEM)] * 6,
+        out_specs=pl.BlockSpec(memory_space=pl.ANY),
         scratch_shapes=[
-            pltpu.VMEM((4, 2, 3, 64, 512), F32),
             pltpu.VMEM((4, 2, 8, 4096), BF16),
             pltpu.VMEM((2, 8, 64, LANES), F32),
             pltpu.VMEM((2, 2, 8, 32, LANES), F32),
-            pltpu.SemaphoreType.DMA((4, 2, 3)),
             pltpu.SemaphoreType.DMA((4, 2)),
         ],
-        compiler_params=params(8),
+        compiler_params=params(12),
         name="finish",
     )(*pieces)
 

time: 163 us -> 157 us (0.963)
  the two profiles are of different devices: /device:TPU:1 before, /device:TPU:6 now
where the time goes in v2:
time: 157 us; the launch traced here: 156 us
  waiting for transfers between devices  69 us (44%)
  starting transfers between devices  47.6 us (30%)
  Pallas kernels  33.5 us (21%)
  local copies, waits for them, and re-layouts  4.37 us (3%)
    ppermute x1, waiting for transfers between devices, step(): grad_one_a = lax.ppermute(grad_a[2], 'y', FIRST)  17 us
    ppermute x2, waiting for transfers between devices, fetch_weights(): got.append(lax.ppermute(both, ('z', 'core', 'x'), pairs))  16.3 us
    pallas_call x3, Pallas kernels, conv(): pl.pallas_call(functools.partial(conv_kernel, halves, rows), out_shape=(s...  16.2 us
    ppermute x2, waiting for transfers between devices, gather(): lax.ppermute(block, axis, OPPOSITE)  13.3 us
    ppermute x2, starting transfers between devices, gather(): lax.ppermute(block, axis, FIRST)  9.02 us
    pallas_call x1, Pallas kernels, weight_grads(): pl.pallas_call(kernel_grad_kernel, out_shape=(shape,) * 2, grid=(4,), in_...  9.01 us
    ppermute x2, starting transfers between devices, fetch_weights(): got.append(lax.ppermute(both, ('z', 'core', 'x'), pairs))  8.51 us
    ppermute x2, waiting for transfers between devices, gather(): lax.ppermute(block, axis, SECOND)  6.23 us
  transfers between devices with their start and end apart: 27, of which 11 were waited for; matrix products, arithmetic and copies ran while one was open for 2% of the time, Pallas kernels for 20%

profile of v2, /device:TPU:6, one launch (start us, length us, event | category | flops | bytes accessed | tf_op | source)
XLA Modules:
  0.0 156.4 jit_solution(2192574628788200324)
XLA Ops:
  0.6 1.0 copy-done
  1.7 1.0 copy-done.1
  2.7 2.4 %pack.1 = (bf16[4,64,1024]{2,1,0:T(8,128)(2,1)S(1)}, bf16[4,64,1024]{2,1,0:T(8,128)(2,1)S(1)}) custom-call(bf16[8,8,4096]{2,1,0:T(8,128)(2,1)S(1)} %copy-done, bf16[8,8,4096]{2,1,0:T(8,128)(2,1)S(1)} %copy-done.1), custom_call_target="tpu_custom_call" | custom-call | tf_op jit(solution)/shard_map/pack/pallas_call | solution.py:61
  5.1 1.7 %collective-permute-start = (bf16[4,64,1024]{2,1,0:T(8,128)(2,1)S(1)}, bf16[4,64,1024]{2,1,0:T(8,128)(2,1)S(1)}, u32[]{:S(2)}, u32[]{:S(2)}) collective-permute-start(bf16[4,64,1024]{2,1,0:T(8,128)(2,1)S(1)} %get-tuple-element.24.c0.x0), channel_id=1, source_target_pairs={{0,1},{1,0},{2,3},{3,2},{4,5},{5,4},{6,7},{7,6},{8,9},{9,8},{10,11... | collective-permute-start | bytes 1572872 | tf_op jit(solution)/shard_map/ppermute | solution.py:289
  6.8 2.2 %collective-permute-start.1 = (bf16[4,64,1024]{2,1,0:T(8,128)(2,1)S(1)}, bf16[4,64,1024]{2,1,0:T(8,128)(2,1)S(1)}, u32[]{:S(2)}, u32[]{:S(2)}) collective-permute-start(bf16[4,64,1024]{2,1,0:T(8,128)(2,1)S(1)} %get-tuple-element.24.c0.x0), channel_id=1, source_target_pairs={{1,2},{2,1},{3,0},{0,3},{5,6},{6,5},{7,4},{4,7},{9,10},{10,9},{11,... | collective-permute-start | bytes 1572872 | tf_op jit(solution)/shard_map/ppermute | solution.py:289
  9.0 0.7 collective-permute-start.2
  9.7 0.7 slice_bitcast_fusion.22
  10.4 0.9 collective-permute-done.5
  11.3 1.9 %collective-permute-start.7 = (bf16[2,9,64,128]{3,2,1,0:T(8,128)(2,1)S(1)}, bf16[2,9,64,128]{3,2,1,0:T(8,128)(2,1)S(1)}, u32[]{:S(2)}, u32[]{:S(2)}) collective-permute-start(bf16[2,9,64,128]{3,2,1,0:T(8,128)(2,1)S(1)} %pad_maximum_fusion.1), channel_id=1, source_target_pairs={{0,64},{4,96},{8,0},{12,32},{16,112},{20,16},{24,48},{28,80},{32,6... | collective-permute-start | bytes 884744 | tf_op jit(solution)/shard_map/ppermute | solution.py:317
  13.2 6.6 %collective-permute-start.6 = (bf16[2,9,64,128]{3,2,1,0:T(8,128)(2,1)S(1)}, bf16[2,9,64,128]{3,2,1,0:T(8,128)(2,1)S(1)}, u32[]{:S(2)}, u32[]{:S(2)}) collective-permute-start(bf16[2,9,64,128]{3,2,1,0:T(8,128)(2,1)S(1)} %pad_maximum_fusion.1), channel_id=1, source_target_pairs={{0,0},{4,32},{8,64},{12,96},{16,48},{20,80},{24,112},{28,16},{32,4... | collective-permute-start | bytes 884744 | tf_op jit(solution)/shard_map/ppermute | solution.py:317
  19.8 0.7 slice_bitcast_fusion.20
  20.6 14.3 %collective-permute-done.7 = bf16[2,9,64,128]{3,2,1,0:T(8,128)(2,1)S(1)} collective-permute-done((bf16[2,9,64,128]{3,2,1,0:T(8,128)(2,1)S(1)}, bf16[2,9,64,128]{3,2,1,0:T(8,128)(2,1)S(1)}, u32[]{:S(2)}, u32[]{:S(2)}) %collective-permute-start.7) | collective-permute-done | bytes 294944 | tf_op jit(solution)/shard_map/ppermute | solution.py:317
  34.8 7.4 %collective-permute-start.13 = (bf16[4,64,1024]{2,1,0:T(8,128)(2,1)S(1)}, bf16[4,64,1024]{2,1,0:T(8,128)(2,1)S(1)}, u32[]{:S(2)}, u32[]{:S(2)}) collective-permute-start(bf16[4,64,1024]{2,1,0:T(8,128)(2,1)S(1)} %get-tuple-element.33.c0.g0), channel_id=1, source_target_pairs={{0,4},{4,0},{8,12},{12,8},{1,5},{5,1},{9,13},{13,9},{2,6},{6,2},{1... | collective-permute-start | bytes 1572872 | tf_op jit(solution)/shard_map/ppermute | solution.py:289
  42.2 2.1 %collective-permute-done.6 = bf16[2,9,64,128]{3,2,1,0:T(8,128)(2,1)S(1)} collective-permute-done((bf16[2,9,64,128]{3,2,1,0:T(8,128)(2,1)S(1)}, bf16[2,9,64,128]{3,2,1,0:T(8,128)(2,1)S(1)}, u32[]{:S(2)}, u32[]{:S(2)}) %collective-permute-start.6) | collective-permute-done | bytes 294944 | tf_op jit(solution)/shard_map/ppermute | solution.py:317
  44.5 0.3 collective-permute-start.8
  44.9 2.2 %collective-permute-start.3 = (bf16[4,4,64,128]{3,2,1,0:T(8,128)(2,1)S(1)}, bf16[4,4,64,128]{3,2,1,0:T(8,128)(2,1)S(1)}, u32[]{:S(2)}, u32[]{:S(2)}) collective-permute-start(bf16[4,4,64,128]{3,2,1,0:T(8,128)(2,1)S(1)} %pad_maximum_fusion.2), channel_id=1, source_target_pairs={{0,16},{16,32},{32,48},{48,64},{64,80},{80,96},{96,112},{1,17},{17... | collective-permute-start | bytes 786440 | tf_op jit(solution)/shard_map/ppermute | solution.py:298
  47.2 13.3 %collective-permute-done.15.c3.g3 = bf16[4,64,1024]{2,1,0:T(8,128)(2,1)S(1)} collective-permute-done((bf16[4,64,1024]{2,1,0:T(8,128)(2,1)S(1)}, bf16[4,64,1024]{2,1,0:T(8,128)(2,1)S(1)}, u32[]{:S(2)}, u32[]{:S(2)}) %collective-permute-start.15) | collective-permute-done | bytes 524320 | tf_op jit(solution)/shard_map/ppermute | solution.py:289
  60.5 1.3 collective-permute-start.4
  61.9 6.2 %collective-permute-done.14.c2.g2 = bf16[4,64,1024]{2,1,0:T(8,128)(2,1)S(1)} collective-permute-done((bf16[4,64,1024]{2,1,0:T(8,128)(2,1)S(1)}, bf16[4,64,1024]{2,1,0:T(8,128)(2,1)S(1)}, u32[]{:S(2)}, u32[]{:S(2)}) %collective-permute-start.14) | collective-permute-done | bytes 524320 | tf_op jit(solution)/shard_map/ppermute | solution.py:289
  68.2 1.3 collective-permute-start.18
  69.6 1.3 collective-permute-start.19
  70.9 1.6 %weights.1 = (bf16[3,256,768]{2,1,0:T(8,128)(2,1)S(1)}, bf16[3,256,768]{2,1,0:T(8,128)(2,1)S(1)}) custom-call(s32[4]{0:T(128)S(1)} %pad_add_fusion.at, bf16[2,2,9,64,128]{4,3,2,1,0:T(8,128)(2,1)S(1)} %pad_maximum_fusion.mine, bf16[2,2,9,64,128]{4,3,2,1,0:T(8,128)(2,1)S(1)} %collective-permute-done.8.other), custom_call_target="tpu_custom_call" | custom-call | tf_op jit(solution)/shard_map/weights/pallas_call | solution.py:144
  72.5 7.1 %shard_map.58 = (f32[4,64,512]{2,1,0:T(8,128)S(1)}, f32[4,64,512]{2,1,0:T(8,128)S(1)}, f32[2,4,64,512]{3,2,1,0:T(8,128)S(1)}, f32[4,64,512]{2,1,0:T(8,128)S(1)},...) custom-call(s32[4]{0:T(128)S(1)} %pad_add_fusion.at, bf16[4,64,1024]{2,1,0:T(8,128)(2,1)S(1)} %get-tuple-element.24.c0.x0, ...), custom_call_target="tpu_custom_call" | custom-call | flops 4831838208 | bytes 12000000 | tf_op jit(solution)/shard_map/pallas_call | solution.py:206
  79.7 3.5 %collective-permute-start.11 = (f32[2,4,64,512]{3,2,1,0:T(8,128)S(1)}, f32[2,4,64,512]{3,2,1,0:T(8,128)S(1)}, u32[]{:S(2)}, u32[]{:S(2)}) collective-permute-start(f32[2,4,64,512]{3,2,1,0:T(8,128)S(1)} %get-tuple-element.30), channel_id=1, source_target_pairs={{4,8},{8,4},{12,0},{0,12},{5,9},{9,5},{13,1},{1,13},{6,10},{10,6},... | collective-permute-start | bytes 3145736 | tf_op jit(solution)/shard_map/ppermute | solution.py:334
  83.1 4.4 %shard_map.59 = (f32[4,64,512]{2,1,0:T(8,128)S(1)}, f32[4,64,512]{2,1,0:T(8,128)S(1)}, f32[2,4,64,512]{3,2,1,0:T(8,128)S(1)}) custom-call(s32[4]{0:T(128)S(1)} %pad_add_fusion.at, bf16[4,64,1024]{2,1,0:T(8,128)(2,1)S(1)} %get-tuple-element.33.c0.g0, bf16[4,64,1024]{2,1,0:T(8,128)(2,1)S(1)} %collective-permute-done.13.c1.g1, ...), custom_call_target="tpu_custom_call" | custom-call | flops 2415919104 | bytes 6000000 | tf_op jit(solution)/shard_map/pallas_call | solution.py:206
  87.6 4.7 %shard_map.60 = (f32[4,64,512]{2,1,0:T(8,128)S(1)}, f32[4,64,512]{2,1,0:T(8,128)S(1)}, f32[2,4,64,512]{3,2,1,0:T(8,128)S(1)}) custom-call(s32[4]{0:T(128)S(1)} %pad_add_fusion.at, bf16[4,64,1024]{2,1,0:T(8,128)(2,1)S(1)} %get-tuple-element.33.c0.g0, bf16[4,64,1024]{2,1,0:T(8,128)(2,1)S(1)} %collective-permute-done.13.c1.g1, ...), custom_call_target="tpu_custom_call" | custom-call | flops 2415919104 | bytes 6000000 | tf_op jit(solution)/shard_map/pallas_call | solution.py:206
  92.3 9.0 %weight_grads.1 = (f32[4,9,64,128]{3,2,1,0:T(8,128)S(1)}, f32[4,9,64,128]{3,2,1,0:T(8,128)S(1)}) custom-call(s32[4]{0:T(128)S(1)} %pad_add_fusion.at, bf16[4,64,1024]{2,1,0:T(8,128)(2,1)S(1)} %get-tuple-element.24.c0.x0, bf16[4,64,1024]{2,1,0:T(8,128)(2,1)S(1)} %collective-permute-done.c1.x1, bf16[4,64,1024]{2,1,0:T(8,128)(2,1)S(1)} %collective-permute-done.1.c2.x2, ...), custom_call_target="tpu_custom_call" | custom-call | flops 4831838208 | bytes 9000000 | tf_op jit(solution)/shard_map/weight_grads/pallas_call | solution.py:262
  101.3 0.9 collective-permute-start.22
  102.3 1.2 collective-permute-start.16
  103.5 2.2 %collective-permute-start.20 = (f32[2,4,64,512]{3,2,1,0:T(8,128)S(1)}, f32[2,4,64,512]{3,2,1,0:T(8,128)S(1)}, u32[]{:S(2)}, u32[]{:S(2)}) collective-permute-start(f32[2,4,64,512]{3,2,1,0:T(8,128)S(1)} %get-tuple-element.40), channel_id=1, source_target_pairs={{1,2},{2,1},{3,0},{0,3},{5,6},{6,5},{7,4},{4,7},{9,10},{10,9},{11,... | collective-permute-start | bytes 3145736 | tf_op jit(solution)/shard_map/ppermute | solution.py:338
  105.7 3.1 %collective-permute-start.10 = (f32[4,64,512]{2,1,0:T(8,128)S(1)}, f32[4,64,512]{2,1,0:T(8,128)S(1)}, u32[]{:S(2)}, u32[]{:S(2)}) collective-permute-start(f32[4,64,512]{2,1,0:T(8,128)S(1)} %fusion.3), channel_id=1, source_target_pairs={{4,8},{8,4},{12,0},{0,12},{5,9},{9,5},{13,1},{1,13},{6,10},{10,6},... | collective-permute-start | bytes 1572872 | tf_op jit(solution)/shard_map/ppermute | solution.py:302
  109.0 0.2 add.28
  109.2 0.1 collective-permute-start.25
  109.3 1.2 collective-permute-start.24
  110.5 17.0 %collective-permute-done.16.one_a = f32[2,4,64,512]{3,2,1,0:T(8,128)S(1)} collective-permute-done((f32[2,4,64,512]{3,2,1,0:T(8,128)S(1)}, f32[2,4,64,512]{3,2,1,0:T(8,128)S(1)}, u32[]{:S(2)}, u32[]{:S(2)}) %collective-permute-start.16) | collective-permute-done | bytes 1048608 | tf_op jit(solution)/shard_map/ppermute | solution.py:336
  127.4 1.8 %collective-permute-start.23 = (f32[9,64,128]{2,1,0:T(8,128)S(1)}, f32[9,64,128]{2,1,0:T(8,128)S(1)}, u32[]{:S(2)}, u32[]{:S(2)}) collective-permute-start(f32[9,64,128]{2,1,0:T(8,128)S(1)} %get-tuple-element.45), channel_id=1, source_target_pairs={{0,32},{32,64},{64,96},{96,0},{1,33},{33,65},{65,97},{97,1},{2,34}... | collective-permute-start | bytes 884744 | tf_op jit(solution)/shard_map/ppermute | solution.py:346
  129.4 0.2 collective-permute-done.20.one_b
  129.6 1.0 collective-permute-start.12
  130.7 2.7 %collective-permute-start.17 = (f32[4,64,512]{2,1,0:T(8,128)S(1)}, f32[4,64,512]{2,1,0:T(8,128)S(1)}, u32[]{:S(2)}, u32[]{:S(2)}) collective-permute-start(f32[4,64,512]{2,1,0:T(8,128)S(1)} %fusion.1), channel_id=1, source_target_pairs={{1,2},{2,1},{3,0},{0,3},{5,6},{6,5},{7,4},{4,7},{9,10},{10,9},{11,... | collective-permute-start | bytes 1572872 | tf_op jit(solution)/shard_map/ppermute | solution.py:302
  133.4 0.2 collective-permute-start.21
  133.6 3.2 %collective-permute-done.23 = f32[9,64,128]{2,1,0:T(8,128)S(1)} collective-permute-done((f32[9,64,128]{2,1,0:T(8,128)S(1)}, f32[9,64,128]{2,1,0:T(8,128)S(1)}, u32[]{:S(2)}, u32[]{:S(2)}) %collective-permute-start.23) | collective-permute-done | bytes 294944 | tf_op jit(solution)/shard_map/ppermute | solution.py:346
  136.9 2.7 %collective-permute-start.26 = (f32[9,64,128]{2,1,0:T(8,128)S(1)}, f32[9,64,128]{2,1,0:T(8,128)S(1)}, u32[]{:S(2)}, u32[]{:S(2)}) collective-permute-start(f32[9,64,128]{2,1,0:T(8,128)S(1)} %fusion.6), channel_id=1, source_target_pairs={{0,0},{4,32},{8,64},{12,96},{32,4},{36,36},{40,68},{44,100},{64,8}... | collective-permute-start | bytes 884744 | tf_op jit(solution)/shard_map/ppermute | solution.py:348
  139.6 5.2 %collective-permute-done.17.two_a = f32[4,64,512]{2,1,0:T(8,128)S(1)} collective-permute-done((f32[4,64,512]{2,1,0:T(8,128)S(1)}, f32[4,64,512]{2,1,0:T(8,128)S(1)}, u32[]{:S(2)}, u32[]{:S(2)}) %collective-permute-start.17) | collective-permute-done | bytes 524320 | tf_op jit(solution)/shard_map/ppermute | solution.py:302
  144.8 1.1 collective-permute-done.21.two_b
  145.9 2.2 %finish.3 = bf16[8,8,4096]{2,1,0:T(8,128)(2,1)} custom-call(f32[4,64,512]{2,1,0:T(8,128)S(1)} %get-tuple-element.35.own_a, f32[2,4,64,512]{3,2,1,0:T(8,128)S(1)} %collective-permute-done.16.one_a, f32[4,64,512]{2,1,0:T(8,128)S(1)} %collective-permute-done.17.two_a, f32[4,64,512]{2,1,0:T(8,128)S(1)} %get-tuple-element.39.own_b, ...), custom_call_target="tpu_custom_call" | custom-call | tf_op jit(solution)/shard_map/finish/pallas_call | solution.py:103
  148.1 2.2 %finish.2 = bf16[8,8,4096]{2,1,0:T(8,128)(2,1)} custom-call(f32[4,64,512]{2,1,0:T(8,128)S(1)} %get-tuple-element.26.own_a, f32[2,4,64,512]{3,2,1,0:T(8,128)S(1)} %collective-permute-done.9.one_a, f32[4,64,512]{2,1,0:T(8,128)S(1)} %collective-permute-done.10.two_a, f32[4,64,512]{2,1,0:T(8,128)S(1)} %get-tuple-element.29.own_b, ...), custom_call_target="tpu_custom_call" | custom-call | tf_op jit(solution)/shard_map/finish/pallas_call | solution.py:103
  150.3 5.4 %collective-permute-done.26 = f32[9,64,128]{2,1,0:T(8,128)S(1)} collective-permute-done((f32[9,64,128]{2,1,0:T(8,128)S(1)}, f32[9,64,128]{2,1,0:T(8,128)S(1)}, u32[]{:S(2)}, u32[]{:S(2)}) %collective-permute-start.26) | collective-permute-done | bytes 294944 | tf_op jit(solution)/shard_map/ppermute | solution.py:348
  155.7 0.7 copy.7
  (51 shorter events, 1.2 us)
Async XLA Ops:
  0.6 1.0 copy-start
  1.7 1.0 copy-start.1
  2.7 8.6 %copy-start.6 = (bf16[3,3,64,128]{3,2,1,0:T(8,128)(2,1)S(1)}, bf16[3,3,64,128]{3,2,1,0:T(8,128)(2,1)}, u32[]{:S(2)}) copy-start(bf16[3,3,64,128]{3,2,1,0:T(8,128)(2,1)} %param.4) | copy-start | bytes 442372
  5.1 39.7 %collective-permute-start = (bf16[4,64,1024]{2,1,0:T(8,128)(2,1)S(1)}, bf16[4,64,1024]{2,1,0:T(8,128)(2,1)S(1)}, u32[]{:S(2)}, u32[]{:S(2)}) collective-permute-start(bf16[4,64,1024]{2,1,0:T(8,128)(2,1)S(1)} %get-tuple-element.24.c0.x0), channel_id=1, source_target_pairs={{0,1},{1,0},{2,3},{3,2},{4,5},{5,4},{6,7},{7,6},{8,9},{9,8},{10,11... | collective-permute-start | bytes 1572872 | tf_op jit(solution)/shard_map/ppermute | solution.py:289
  6.8 37.7 %collective-permute-start.1 = (bf16[4,64,1024]{2,1,0:T(8,128)(2,1)S(1)}, bf16[4,64,1024]{2,1,0:T(8,128)(2,1)S(1)}, u32[]{:S(2)}, u32[]{:S(2)}) collective-permute-start(bf16[4,64,1024]{2,1,0:T(8,128)(2,1)S(1)} %get-tuple-element.24.c0.x0), channel_id=1, source_target_pairs={{1,2},{2,1},{3,0},{0,3},{5,6},{6,5},{7,4},{4,7},{9,10},{10,9},{11,... | collective-permute-start | bytes 1572872 | tf_op jit(solution)/shard_map/ppermute | solution.py:289
  9.0 35.4 %collective-permute-start.2 = (bf16[4,64,1024]{2,1,0:T(8,128)(2,1)S(1)}, bf16[4,64,1024]{2,1,0:T(8,128)(2,1)S(1)}, u32[]{:S(2)}, u32[]{:S(2)}) collective-permute-start(bf16[4,64,1024]{2,1,0:T(8,128)(2,1)S(1)} %get-tuple-element.24.c0.x0), channel_id=1, source_target_pairs={{0,2},{1,3},{2,0},{3,1},{4,6},{5,7},{6,4},{7,5},{8,10},{9,11},{10,... | collective-permute-start | bytes 1572872 | tf_op jit(solution)/shard_map/ppermute | solution.py:289
  9.7 1.6 %collective-permute-start.5 = (bf16[9,64,128]{2,1,0:T(8,128)(2,1)}, bf16[9,64,128]{2,1,0:T(8,128)(2,1)S(1)}, u32[]{:S(2)}, u32[]{:S(2)}) collective-permute-start(bf16[9,64,128]{2,1,0:T(8,128)(2,1)} %bitcast.75), channel_id=1, source_target_pairs={{0,16},{16,0},{1,17},{17,1},{2,18},{18,2},{3,19},{19,3},{4,20},{20... | collective-permute-start | bytes 442376 | tf_op jit(solution)/shard_map/ppermute | solution.py:308
  11.3 23.5 %collective-permute-start.7 = (bf16[2,9,64,128]{3,2,1,0:T(8,128)(2,1)S(1)}, bf16[2,9,64,128]{3,2,1,0:T(8,128)(2,1)S(1)}, u32[]{:S(2)}, u32[]{:S(2)}) collective-permute-start(bf16[2,9,64,128]{3,2,1,0:T(8,128)(2,1)S(1)} %pad_maximum_fusion.1), channel_id=1, source_target_pairs={{0,64},{4,96},{8,0},{12,32},{16,112},{20,16},{24,48},{28,80},{32,6... | collective-permute-start | bytes 884744 | tf_op jit(solution)/shard_map/ppermute | solution.py:317
  13.2 31.1 %collective-permute-start.6 = (bf16[2,9,64,128]{3,2,1,0:T(8,128)(2,1)S(1)}, bf16[2,9,64,128]{3,2,1,0:T(8,128)(2,1)S(1)}, u32[]{:S(2)}, u32[]{:S(2)}) collective-permute-start(bf16[2,9,64,128]{3,2,1,0:T(8,128)(2,1)S(1)} %pad_maximum_fusion.1), channel_id=1, source_target_pairs={{0,0},{4,32},{8,64},{12,96},{16,48},{20,80},{24,112},{28,16},{32,4... | collective-permute-start | bytes 884744 | tf_op jit(solution)/shard_map/ppermute | solution.py:317
  20.5 24.4 %copy-start.5 = (bf16[1,4,64,128]{3,2,1,0:T(8,128)(2,1)S(1)}, bf16[1,4,64,128]{3,2,1,0:T(8,128)(2,1)}, u32[]{:S(2)}) copy-start(bf16[1,4,64,128]{3,2,1,0:T(8,128)(2,1)} %get-tuple-element.57) | copy-start | bytes 196612
  34.8 33.3 %collective-permute-start.13 = (bf16[4,64,1024]{2,1,0:T(8,128)(2,1)S(1)}, bf16[4,64,1024]{2,1,0:T(8,128)(2,1)S(1)}, u32[]{:S(2)}, u32[]{:S(2)}) collective-permute-start(bf16[4,64,1024]{2,1,0:T(8,128)(2,1)S(1)} %get-tuple-element.33.c0.g0), channel_id=1, source_target_pairs={{0,4},{4,0},{8,12},{12,8},{1,5},{5,1},{9,13},{13,9},{2,6},{6,2},{1... | collective-permute-start | bytes 1572872 | tf_op jit(solution)/shard_map/ppermute | solution.py:289
  44.3 23.8 %collective-permute-start.14 = (bf16[4,64,1024]{2,1,0:T(8,128)(2,1)S(1)}, bf16[4,64,1024]{2,1,0:T(8,128)(2,1)S(1)}, u32[]{:S(2)}, u32[]{:S(2)}) collective-permute-start(bf16[4,64,1024]{2,1,0:T(8,128)(2,1)S(1)} %get-tuple-element.33.c0.g0), channel_id=1, source_target_pairs={{4,8},{8,4},{12,0},{0,12},{5,9},{9,5},{13,1},{1,13},{6,10},{10,6},... | collective-permute-start | bytes 1572872 | tf_op jit(solution)/shard_map/ppermute | solution.py:289
  44.3 2.9 %copy-start.4 = (bf16[1,4,64,128]{3,2,1,0:T(8,128)(2,1)S(1)}, bf16[1,4,64,128]{3,2,1,0:T(8,128)(2,1)}, u32[]{:S(2)}) copy-start(bf16[1,4,64,128]{3,2,1,0:T(8,128)(2,1)} %get-tuple-element.56) | copy-start | bytes 196612
  44.4 16.2 %collective-permute-start.15 = (bf16[4,64,1024]{2,1,0:T(8,128)(2,1)S(1)}, bf16[4,64,1024]{2,1,0:T(8,128)(2,1)S(1)}, u32[]{:S(2)}, u32[]{:S(2)}) collective-permute-start(bf16[4,64,1024]{2,1,0:T(8,128)(2,1)S(1)} %get-tuple-element.33.c0.g0), channel_id=1, source_target_pairs={{0,8},{4,12},{8,0},{12,4},{1,9},{5,13},{9,1},{13,5},{2,10},{6,14},... | collective-permute-start | bytes 1572872 | tf_op jit(solution)/shard_map/ppermute | solution.py:289
  44.5 23.7 %copy-start.3 = (bf16[1,4,64,128]{3,2,1,0:T(8,128)(2,1)S(1)}, bf16[1,4,64,128]{3,2,1,0:T(8,128)(2,1)}, u32[]{:S(2)}) copy-start(bf16[1,4,64,128]{3,2,1,0:T(8,128)(2,1)} %get-tuple-element.49) | copy-start | bytes 196612
  44.5 26.4 %collective-permute-start.8 = (bf16[2,2,9,64,128]{4,3,2,1,0:T(8,128)(2,1)S(1)}, bf16[2,2,9,64,128]{4,3,2,1,0:T(8,128)(2,1)S(1)}, u32[]{:S(2)}, u32[]{:S(2)}) collective-permute-start(bf16[2,2,9,64,128]{4,3,2,1,0:T(8,128)(2,1)S(1)} %pad_maximum_fusion.mine), channel_id=1, source_target_pairs={{0,16},{16,0},{1,17},{17,1},{2,18},{18,2},{3,19},{19,3},{4,20},{20... | collective-permute-start | bytes 1769480 | tf_op jit(solution)/shard_map/ppermute | solution.py:319
  44.9 24.7 %copy-start.2 = (bf16[1,4,64,128]{3,2,1,0:T(8,128)(2,1)S(1)}, bf16[1,4,64,128]{3,2,1,0:T(8,128)(2,1)}, u32[]{:S(2)}) copy-start(bf16[1,4,64,128]{3,2,1,0:T(8,128)(2,1)} %get-tuple-element.48) | copy-start | bytes 196612
  44.9 27.6 %collective-permute-start.3 = (bf16[4,4,64,128]{3,2,1,0:T(8,128)(2,1)S(1)}, bf16[4,4,64,128]{3,2,1,0:T(8,128)(2,1)S(1)}, u32[]{:S(2)}, u32[]{:S(2)}) collective-permute-start(bf16[4,4,64,128]{3,2,1,0:T(8,128)(2,1)S(1)} %pad_maximum_fusion.2), channel_id=1, source_target_pairs={{0,16},{16,32},{32,48},{48,64},{64,80},{80,96},{96,112},{1,17},{17... | collective-permute-start | bytes 786440 | tf_op jit(solution)/shard_map/ppermute | solution.py:298
  60.5 11.9 %collective-permute-start.4 = (bf16[4,4,64,128]{3,2,1,0:T(8,128)(2,1)S(1)}, bf16[4,4,64,128]{3,2,1,0:T(8,128)(2,1)S(1)}, u32[]{:S(2)}, u32[]{:S(2)}) collective-permute-start(bf16[4,4,64,128]{3,2,1,0:T(8,128)(2,1)S(1)} %pad_maximum_fusion.3), channel_id=1, source_target_pairs={{16,0},{32,16},{48,32},{64,48},{80,64},{96,80},{112,96},{17,1},{33... | collective-permute-start | bytes 786440 | tf_op jit(solution)/shard_map/ppermute | solution.py:298
  68.2 19.4 %collective-permute-start.18 = (bf16[4,4,64,128]{3,2,1,0:T(8,128)(2,1)S(1)}, bf16[4,4,64,128]{3,2,1,0:T(8,128)(2,1)S(1)}, u32[]{:S(2)}, u32[]{:S(2)}) collective-permute-start(bf16[4,4,64,128]{3,2,1,0:T(8,128)(2,1)S(1)} %pad_maximum_fusion.4), channel_id=1, source_target_pairs={{0,16},{16,32},{32,48},{48,64},{64,80},{80,96},{96,112},{1,17},{17... | collective-permute-start | bytes 786440 | tf_op jit(solution)/shard_map/ppermute | solution.py:298
  69.6 18.0 %collective-permute-start.19 = (bf16[4,4,64,128]{3,2,1,0:T(8,128)(2,1)S(1)}, bf16[4,4,64,128]{3,2,1,0:T(8,128)(2,1)S(1)}, u32[]{:S(2)}, u32[]{:S(2)}) collective-permute-start(bf16[4,4,64,128]{3,2,1,0:T(8,128)(2,1)S(1)} %pad_maximum_fusion.5), channel_id=1, source_target_pairs={{16,0},{32,16},{48,32},{64,48},{80,64},{96,80},{112,96},{17,1},{33... | collective-permute-start | bytes 786440 | tf_op jit(solution)/shard_map/ppermute | solution.py:298
  79.6 26.1 %collective-permute-start.9 = (f32[2,4,64,512]{3,2,1,0:T(8,128)S(1)}, f32[2,4,64,512]{3,2,1,0:T(8,128)S(1)}, u32[]{:S(2)}, u32[]{:S(2)}) collective-permute-start(f32[2,4,64,512]{3,2,1,0:T(8,128)S(1)} %get-tuple-element.27), channel_id=1, source_target_pairs={{0,4},{4,0},{8,12},{12,8},{1,5},{5,1},{9,13},{13,9},{2,6},{6,2},{1... | collective-permute-start | bytes 3145736 | tf_op jit(solution)/shard_map/ppermute | solution.py:333
  79.7 29.2 %collective-permute-start.11 = (f32[2,4,64,512]{3,2,1,0:T(8,128)S(1)}, f32[2,4,64,512]{3,2,1,0:T(8,128)S(1)}, u32[]{:S(2)}, u32[]{:S(2)}) collective-permute-start(f32[2,4,64,512]{3,2,1,0:T(8,128)S(1)} %get-tuple-element.30), channel_id=1, source_target_pairs={{4,8},{8,4},{12,0},{0,12},{5,9},{9,5},{13,1},{1,13},{6,10},{10,6},... | collective-permute-start | bytes 3145736 | tf_op jit(solution)/shard_map/ppermute | solution.py:334
  101.3 7.6 %collective-permute-start.22 = (f32[4,9,64,128]{3,2,1,0:T(8,128)S(1)}, f32[4,9,64,128]{3,2,1,0:T(8,128)S(1)}, u32[]{:S(2)}, u32[]{:S(2)}) collective-permute-start(f32[4,9,64,128]{3,2,1,0:T(8,128)S(1)} %get-tuple-element.44), channel_id=1, source_target_pairs={{0,16},{16,0},{1,17},{17,1},{2,18},{18,2},{3,19},{19,3},{4,20},{20... | collective-permute-start | bytes 3538952 | tf_op jit(solution)/shard_map/ppermute | solution.py:341
  102.3 25.2 %collective-permute-start.16 = (f32[2,4,64,512]{3,2,1,0:T(8,128)S(1)}, f32[2,4,64,512]{3,2,1,0:T(8,128)S(1)}, u32[]{:S(2)}, u32[]{:S(2)}) collective-permute-start(f32[2,4,64,512]{3,2,1,0:T(8,128)S(1)} %get-tuple-element.36), channel_id=1, source_target_pairs={{0,1},{1,0},{2,3},{3,2},{4,5},{5,4},{6,7},{7,6},{8,9},{9,8},{10,11... | collective-permute-start | bytes 3145736 | tf_op jit(solution)/shard_map/ppermute | solution.py:336
  103.5 26.1 %collective-permute-start.20 = (f32[2,4,64,512]{3,2,1,0:T(8,128)S(1)}, f32[2,4,64,512]{3,2,1,0:T(8,128)S(1)}, u32[]{:S(2)}, u32[]{:S(2)}) collective-permute-start(f32[2,4,64,512]{3,2,1,0:T(8,128)S(1)} %get-tuple-element.40), channel_id=1, source_target_pairs={{1,2},{2,1},{3,0},{0,3},{5,6},{6,5},{7,4},{4,7},{9,10},{10,9},{11,... | collective-permute-start | bytes 3145736 | tf_op jit(solution)/shard_map/ppermute | solution.py:338
  105.7 42.4 %collective-permute-start.10 = (f32[4,64,512]{2,1,0:T(8,128)S(1)}, f32[4,64,512]{2,1,0:T(8,128)S(1)}, u32[]{:S(2)}, u32[]{:S(2)}) collective-permute-start(f32[4,64,512]{2,1,0:T(8,128)S(1)} %fusion.3), channel_id=1, source_target_pairs={{4,8},{8,4},{12,0},{0,12},{5,9},{9,5},{13,1},{1,13},{6,10},{10,6},... | collective-permute-start | bytes 1572872 | tf_op jit(solution)/shard_map/ppermute | solution.py:302
  109.2 21.4 %collective-permute-start.25 = (f32[9,64,128]{2,1,0:T(8,128)S(1)}, f32[9,64,128]{2,1,0:T(8,128)S(1)}, u32[]{:S(2)}, u32[]{:S(2)}) collective-permute-start(f32[9,64,128]{2,1,0:T(8,128)S(1)} %get-tuple-element.46), channel_id=1, source_target_pairs={{0,64},{32,96},{64,0},{96,32},{1,65},{33,97},{65,1},{97,33},{2,66}... | collective-permute-start | bytes 884744 | tf_op jit(solution)/shard_map/ppermute | solution.py:346
  109.3 24.1 %collective-permute-start.24 = (f32[9,64,128]{2,1,0:T(8,128)S(1)}, f32[9,64,128]{2,1,0:T(8,128)S(1)}, u32[]{:S(2)}, u32[]{:S(2)}) collective-permute-start(f32[9,64,128]{2,1,0:T(8,128)S(1)} %get-tuple-element.47), channel_id=1, source_target_pairs={{0,96},{32,0},{64,32},{96,64},{1,97},{33,1},{65,33},{97,65},{2,98}... | collective-permute-start | bytes 884744 | tf_op jit(solution)/shard_map/ppermute | solution.py:346
  127.4 9.4 %collective-permute-start.23 = (f32[9,64,128]{2,1,0:T(8,128)S(1)}, f32[9,64,128]{2,1,0:T(8,128)S(1)}, u32[]{:S(2)}, u32[]{:S(2)}) collective-permute-start(f32[9,64,128]{2,1,0:T(8,128)S(1)} %get-tuple-element.45), channel_id=1, source_target_pairs={{0,32},{32,64},{64,96},{96,0},{1,33},{33,65},{65,97},{97,1},{2,34}... | collective-permute-start | bytes 884744 | tf_op jit(solution)/shard_map/ppermute | solution.py:346
  129.6 18.6 %collective-permute-start.12 = (f32[4,64,512]{2,1,0:T(8,128)S(1)}, f32[4,64,512]{2,1,0:T(8,128)S(1)}, u32[]{:S(2)}, u32[]{:S(2)}) collective-permute-start(f32[4,64,512]{2,1,0:T(8,128)S(1)} %fusion.2), channel_id=1, source_target_pairs={{0,4},{4,0},{8,12},{12,8},{1,5},{5,1},{9,13},{13,9},{2,6},{6,2},{1... | collective-permute-start | bytes 1572872 | tf_op jit(solution)/shard_map/ppermute | solution.py:303
  130.7 14.1 %collective-permute-start.17 = (f32[4,64,512]{2,1,0:T(8,128)S(1)}, f32[4,64,512]{2,1,0:T(8,128)S(1)}, u32[]{:S(2)}, u32[]{:S(2)}) collective-permute-start(f32[4,64,512]{2,1,0:T(8,128)S(1)} %fusion.1), channel_id=1, source_target_pairs={{1,2},{2,1},{3,0},{0,3},{5,6},{6,5},{7,4},{4,7},{9,10},{10,9},{11,... | collective-permute-start | bytes 1572872 | tf_op jit(solution)/shard_map/ppermute | solution.py:302
  133.4 12.6 %collective-permute-start.21 = (f32[4,64,512]{2,1,0:T(8,128)S(1)}, f32[4,64,512]{2,1,0:T(8,128)S(1)}, u32[]{:S(2)}, u32[]{:S(2)}) collective-permute-start(f32[4,64,512]{2,1,0:T(8,128)S(1)} %fusion), channel_id=1, source_target_pairs={{0,1},{1,0},{2,3},{3,2},{4,5},{5,4},{6,7},{7,6},{8,9},{9,8},{10,11... | collective-permute-start | bytes 1572872 | tf_op jit(solution)/shard_map/ppermute | solution.py:303
  136.9 18.8 %collective-permute-start.26 = (f32[9,64,128]{2,1,0:T(8,128)S(1)}, f32[9,64,128]{2,1,0:T(8,128)S(1)}, u32[]{:S(2)}, u32[]{:S(2)}) collective-permute-start(f32[9,64,128]{2,1,0:T(8,128)S(1)} %fusion.6), channel_id=1, source_target_pairs={{0,0},{4,32},{8,64},{12,96},{32,4},{36,36},{40,68},{44,100},{64,8}... | collective-permute-start | bytes 884744 | tf_op jit(solution)/shard_map/ppermute | solution.py:348

commit v3 on v2

--- a/solution.py
+++ b/solution.py
@@ -116,19 +116,42 @@
     )(*pieces)
 
 
+def listed(position, k):
+    odd = lax.rem(position, 2)
+    return lax.rem(position + (0, 1 + 2 * odd, 3 - 2 * odd, 2)[k], 4)
+
+
+def route_kernel(at, b0, b1, b2, b3, o0, o1, o2, o3, held):
+    for k, ref in enumerate((b0, b1, b2, b3)):
+        held[k] = ref[...]
+    for k, ref in enumerate((o0, o1, o2, o3)):
+        ref[...] = held[place_of(listed(at[2], k), at[0])]
+
+
+def route_weights(at, blocks):
+    shape = jax.ShapeDtypeStruct((9, 64, LANES), BF16)
+    near = pl.BlockSpec(memory_space=pltpu.VMEM)
+    return pl.pallas_call(
+        route_kernel,
+        out_shape=(shape,) * 4,
+        in_specs=[pl.BlockSpec(memory_space=pltpu.SMEM)] + [near] * 4,
+        out_specs=[near] * 4,
+        scratch_shapes=[pltpu.VMEM((4, 9, 64, LANES), BF16)],
+        compiler_params=params(4),
+        name="route",
+    )(at, *blocks)
+
+
 def weights_kernel(at, mine, other, w_ref, wt_ref, whole):
-    z, core, x, y = at[0], at[1], at[2], at[3]
+    core, y = at[1], at[3]
     for ref, side in ((mine, core), (other, 1 - core)):
-        for k in range(2):
-            member = lax.rem(z + 8 - 2 * k - side, 4)
-            rows = pl.ds(pl.multiple_of(place_of(member, x) * 64, 64), 64)
+        lanes = pl.ds(pl.multiple_of(side * LANES, LANES), LANES)
+        for k in range(4):
             for tap in range(9):
-                for which, half in ((0, side), (1, 1 - side)):
-                    lanes = pl.ds(pl.multiple_of(half * LANES, LANES), LANES)
-                    whole[tap, rows, lanes] = ref[k, which, tap]
-    listed, channel = row_of((256, 256)), lane_of((256, 256))
+                whole[tap, k * 64 : (k + 1) * 64, lanes] = ref[k, tap]
+    place, channel = row_of((256, 256)), lane_of((256, 256))
     order = jnp.where(
-        (place_of(channel // 64, y) == listed // 64) & (channel % 64 == listed % 64), 1.0, 0.0
+        (place_of(channel // 64, y) == place // 64) & (channel % 64 == place % 64), 1.0, 0.0
     ).astype(BF16)
     across = (((1,), (1,)), ((), ()))
     for tap in range(9):
@@ -305,16 +328,9 @@
 
 
 def fetch_weights(at, block):
-    both = jnp.stack([block, lax.ppermute(block, "core", SWAP)])
-    got = []
-    for k in range(2):
-        pairs = [
-            ((z * 2 + s) * 4 + x, (((x + 2 * k + s) % 4) * 2 + s) * 4 + z)
-            for z in range(4)
-            for s in range(2)
-            for x in range(4)
-        ]
-        got.append(lax.ppermute(both, ("z", "core", "x"), pairs))
+    along_z = gather(block, "z")
+    own, first, second, far = route_weights(at, along_z)
+    got = (own, lax.ppermute(first, "x", FIRST), lax.ppermute(second, "x", SECOND), lax.ppermute(far, "x", OPPOSITE))
     got = jnp.stack(got)
     return arrange_weights(at, got, lax.ppermute(got, "core", SWAP))
 

time: 157 us -> 148 us (0.943)
  waiting for transfers between devices: 69 us -> 61.6 us
    ppermute x3, waiting for transfers between devices: 17.3 us -> 5.03 us  [the longest x1 4.49 us: fetch_weights(): lax.ppermute(far, 'x', OPPOSITE)]
    ppermute x2 -> x3, starting transfers between devices: 9.02 us -> 2.52 us  [gather(): lax.ppermute(block, axis, FIRST)]
    ppermute x2 -> x3, starting transfers between devices: 2.18 us -> 7.58 us  [gather(): lax.ppermute(block, axis, SECOND)]
    ppermute x3, starting transfers between devices: 8.52 us -> 3.58 us  [the longest x1 2.1 us: fetch_weights(): lax.ppermute(second, 'x', SECOND)]
    ppermute x2 -> x3, waiting for transfers between devices: 0.01 us -> 4.56 us  [gather(): lax.ppermute(block, axis, FIRST)]
    ppermute x2, waiting for transfers between devices: 5.19 us -> 1.51 us  [reduce_second(): two_a = lax.ppermute(a[1] + one_a[1], axis, SECOND)]
    ppermute x2 -> x3, starting transfers between devices: 0.81 us -> 3.9 us  [gather(): lax.ppermute(block, axis, OPPOSITE)]
    ppermute x1, waiting for transfers between devices: 5.44 us -> 8.29 us  [step(): lax.ppermute(total, ('z', 'x'), cross).reshape(3, 3, 64, LANES)]
  transfers between devices with their start and end apart: 27 -> 30, of which waited for: 11 -> 12; matrix products, arithmetic and copies ran while one was open for 2% -> 1% of each run, Pallas kernels for 20% -> 22%
where the time goes in v3:
time: 148 us
  waiting for transfers between devices  61.6 us (42%)
  starting transfers between devices  47.1 us (32%)
  Pallas kernels  34.2 us (23%)
  local copies, waits for them, and re-layouts  3.05 us (2%)
    pallas_call x3, Pallas kernels, conv(): pl.pallas_call(functools.partial(conv_kernel, halves, rows), out_shape=(s...  16.3 us
    ppermute x3, waiting for transfers between devices, gather(): lax.ppermute(block, axis, OPPOSITE)  16.1 us
    ppermute x1, waiting for transfers between devices, step(): grad_one_a = lax.ppermute(grad_a[2], 'y', FIRST)  14.4 us
    pallas_call x1, Pallas kernels, weight_grads(): pl.pallas_call(kernel_grad_kernel, out_shape=(shape,) * 2, grid=(4,), in_...  9.01 us
    ppermute x1, waiting for transfers between devices, step(): lax.ppermute(total, ('z', 'x'), cross).reshape(3, 3, 64, LANES)  8.29 us
    ppermute x3, starting transfers between devices, gather(): lax.ppermute(block, axis, SECOND)  7.58 us
    ppermute x3, starting transfers between devices, step(): total = total + lax.ppermute(near[k], 'z', ring(turn))  5.61 us
    ppermute x3, waiting for transfers between devices, step(): total = total + lax.ppermute(near[k], 'z', ring(turn))  5.27 us
  transfers between devices with their start and end apart: 30, of which 12 were waited for; matrix products, arithmetic and copies ran while one was open for 1% of the time, Pallas kernels for 22%

profile of v3, /device:TPU:6, one launch (start us, length us, event | category | flops | bytes accessed | tf_op | source)
XLA Modules:
  0.0 147.8 jit_solution(16734583114146745986)
XLA Ops:
  0.6 1.0 copy-done
  1.7 1.0 copy-done.1
  2.7 2.4 %pack.1 = (bf16[4,64,1024]{2,1,0:T(8,128)(2,1)S(1)}, bf16[4,64,1024]{2,1,0:T(8,128)(2,1)S(1)}) custom-call(bf16[8,8,4096]{2,1,0:T(8,128)(2,1)S(1)} %copy-done, bf16[8,8,4096]{2,1,0:T(8,128)(2,1)S(1)} %copy-done.1), custom_call_target="tpu_custom_call" | custom-call | tf_op jit(solution)/shard_map/pack/pallas_call | solution.py:61
  5.1 3.1 %collective-permute-start.1 = (bf16[4,64,1024]{2,1,0:T(8,128)(2,1)S(1)}, bf16[4,64,1024]{2,1,0:T(8,128)(2,1)S(1)}, u32[]{:S(2)}, u32[]{:S(2)}) collective-permute-start(bf16[4,64,1024]{2,1,0:T(8,128)(2,1)S(1)} %get-tuple-element.28.c0.x0), channel_id=1, source_target_pairs={{1,2},{2,1},{3,0},{0,3},{5,6},{6,5},{7,4},{4,7},{9,10},{10,9},{11,... | collective-permute-start | bytes 1572872 | tf_op jit(solution)/shard_map/ppermute | solution.py:312
  8.2 0.6 collective-permute-start.2
  8.9 1.9 %collective-permute-start.5 = (bf16[9,64,128]{2,1,0:T(8,128)(2,1)}, bf16[9,64,128]{2,1,0:T(8,128)(2,1)S(1)}, u32[]{:S(2)}, u32[]{:S(2)}) collective-permute-start(bf16[9,64,128]{2,1,0:T(8,128)(2,1)} %bitcast.73), channel_id=1, source_target_pairs={{0,32},{32,0},{64,96},{96,64},{1,33},{33,1},{65,97},{97,65},{2,34}... | collective-permute-start | bytes 442376 | tf_op jit(solution)/shard_map/ppermute | solution.py:312
  10.8 2.5 %collective-permute-start.6 = (bf16[9,64,128]{2,1,0:T(8,128)(2,1)}, bf16[9,64,128]{2,1,0:T(8,128)(2,1)S(1)}, u32[]{:S(2)}, u32[]{:S(2)}) collective-permute-start(bf16[9,64,128]{2,1,0:T(8,128)(2,1)} %bitcast.74), channel_id=1, source_target_pairs={{32,64},{64,32},{96,0},{0,96},{33,65},{65,33},{97,1},{1,97},{34,66... | collective-permute-start | bytes 442376 | tf_op jit(solution)/shard_map/ppermute | solution.py:312
  13.3 1.1 collective-permute-start.7
  14.5 4.6 %collective-permute-done.6.b2 = bf16[9,64,128]{2,1,0:T(8,128)(2,1)S(1)} collective-permute-done((bf16[9,64,128]{2,1,0:T(8,128)(2,1)}, bf16[9,64,128]{2,1,0:T(8,128)(2,1)S(1)}, u32[]{:S(2)}, u32[]{:S(2)}) %collective-permute-start.6) | collective-permute-done | bytes 147488 | tf_op jit(solution)/shard_map/ppermute | solution.py:312
  19.0 1.8 %collective-permute-done.7.b3 = bf16[9,64,128]{2,1,0:T(8,128)(2,1)S(1)} collective-permute-done((bf16[9,64,128]{2,1,0:T(8,128)(2,1)}, bf16[9,64,128]{2,1,0:T(8,128)(2,1)S(1)}, u32[]{:S(2)}, u32[]{:S(2)}) %collective-permute-start.7) | collective-permute-done | bytes 147488 | tf_op jit(solution)/shard_map/ppermute | solution.py:312
  20.8 0.6 route.1
  21.5 1.5 %collective-permute-start.10 = (bf16[9,64,128]{2,1,0:T(8,128)(2,1)S(1)}, bf16[9,64,128]{2,1,0:T(8,128)(2,1)S(1)}, u32[]{:S(2)}, u32[]{:S(2)}) collective-permute-start(bf16[9,64,128]{2,1,0:T(8,128)(2,1)S(1)} %get-tuple-element.32), channel_id=1, source_target_pairs={{0,8},{4,12},{8,0},{12,4},{1,9},{5,13},{9,1},{13,5},{2,10},{6,14},... | collective-permute-start | bytes 442376 | tf_op jit(solution)/shard_map/ppermute | solution.py:333
  23.0 2.1 %collective-permute-start.9 = (bf16[9,64,128]{2,1,0:T(8,128)(2,1)S(1)}, bf16[9,64,128]{2,1,0:T(8,128)(2,1)S(1)}, u32[]{:S(2)}, u32[]{:S(2)}) collective-permute-start(bf16[9,64,128]{2,1,0:T(8,128)(2,1)S(1)} %get-tuple-element.31), channel_id=1, source_target_pairs={{4,8},{8,4},{12,0},{0,12},{5,9},{9,5},{13,1},{1,13},{6,10},{10,6},... | collective-permute-start | bytes 442376 | tf_op jit(solution)/shard_map/ppermute | solution.py:333
  25.1 4.5 %collective-permute-done.10 = bf16[9,64,128]{2,1,0:T(8,128)(2,1)S(1)} collective-permute-done((bf16[9,64,128]{2,1,0:T(8,128)(2,1)S(1)}, bf16[9,64,128]{2,1,0:T(8,128)(2,1)S(1)}, u32[]{:S(2)}, u32[]{:S(2)}) %collective-permute-start.10) | collective-permute-done | bytes 147488 | tf_op jit(solution)/shard_map/ppermute | solution.py:333
  30.7 2.0 %collective-permute-start.17 = (bf16[4,64,1024]{2,1,0:T(8,128)(2,1)S(1)}, bf16[4,64,1024]{2,1,0:T(8,128)(2,1)S(1)}, u32[]{:S(2)}, u32[]{:S(2)}) collective-permute-start(bf16[4,64,1024]{2,1,0:T(8,128)(2,1)S(1)} %get-tuple-element.41.c0.g0), channel_id=1, source_target_pairs={{4,8},{8,4},{12,0},{0,12},{5,9},{9,5},{13,1},{1,13},{6,10},{10,6},... | collective-permute-start | bytes 1572872 | tf_op jit(solution)/shard_map/ppermute | solution.py:312
  32.8 2.2 %collective-permute-start.18 = (bf16[4,64,1024]{2,1,0:T(8,128)(2,1)S(1)}, bf16[4,64,1024]{2,1,0:T(8,128)(2,1)S(1)}, u32[]{:S(2)}, u32[]{:S(2)}) collective-permute-start(bf16[4,64,1024]{2,1,0:T(8,128)(2,1)S(1)} %get-tuple-element.41.c0.g0), channel_id=1, source_target_pairs={{0,8},{4,12},{8,0},{12,4},{1,9},{5,13},{9,1},{13,5},{2,10},{6,14},... | collective-permute-start | bytes 1572872 | tf_op jit(solution)/shard_map/ppermute | solution.py:312
  35.2 4.6 %collective-permute-done.c1.x1 = bf16[4,64,1024]{2,1,0:T(8,128)(2,1)S(1)} collective-permute-done((bf16[4,64,1024]{2,1,0:T(8,128)(2,1)S(1)}, bf16[4,64,1024]{2,1,0:T(8,128)(2,1)S(1)}, u32[]{:S(2)}, u32[]{:S(2)}) %collective-permute-start) | collective-permute-done | bytes 524320 | tf_op jit(solution)/shard_map/ppermute | solution.py:312
  39.8 1.3 collective-permute-start.3
  41.1 14.3 %collective-permute-done.18.c3.g3 = bf16[4,64,1024]{2,1,0:T(8,128)(2,1)S(1)} collective-permute-done((bf16[4,64,1024]{2,1,0:T(8,128)(2,1)S(1)}, bf16[4,64,1024]{2,1,0:T(8,128)(2,1)S(1)}, u32[]{:S(2)}, u32[]{:S(2)}) %collective-permute-start.18) | collective-permute-done | bytes 524320 | tf_op jit(solution)/shard_map/ppermute | solution.py:312
  55.4 1.3 collective-permute-start.4
  56.9 3.0 %collective-permute-start.21 = (bf16[4,4,64,128]{3,2,1,0:T(8,128)(2,1)S(1)}, bf16[4,4,64,128]{3,2,1,0:T(8,128)(2,1)S(1)}, u32[]{:S(2)}, u32[]{:S(2)}) collective-permute-start(bf16[4,4,64,128]{3,2,1,0:T(8,128)(2,1)S(1)} %pad_maximum_fusion.3), channel_id=1, source_target_pairs={{0,16},{16,32},{32,48},{48,64},{64,80},{80,96},{96,112},{1,17},{17... | collective-permute-start | bytes 786440 | tf_op jit(solution)/shard_map/ppermute | solution.py:321
  60.0 1.3 collective-permute-start.22
  61.3 1.6 %weights.1 = (bf16[3,256,768]{2,1,0:T(8,128)(2,1)S(1)}, bf16[3,256,768]{2,1,0:T(8,128)(2,1)S(1)}) custom-call(s32[4]{0:T(128)S(1)} %pad_add_fusion.at, bf16[4,9,64,128]{3,2,1,0:T(8,128)(2,1)S(1)} %pad_maximum_fusion.mine, bf16[4,9,64,128]{3,2,1,0:T(8,128)(2,1)S(1)} %collective-permute-done.11.other), custom_call_target="tpu_custom_call" | custom-call | tf_op jit(solution)/shard_map/weights/pallas_call | solution.py:167
  62.9 7.1 %shard_map.58 = (f32[4,64,512]{2,1,0:T(8,128)S(1)}, f32[4,64,512]{2,1,0:T(8,128)S(1)}, f32[2,4,64,512]{3,2,1,0:T(8,128)S(1)}, f32[4,64,512]{2,1,0:T(8,128)S(1)},...) custom-call(s32[4]{0:T(128)S(1)} %pad_add_fusion.at, bf16[4,64,1024]{2,1,0:T(8,128)(2,1)S(1)} %get-tuple-element.28.c0.x0, ...), custom_call_target="tpu_custom_call" | custom-call | flops 4831838208 | bytes 12000000 | tf_op jit(solution)/shard_map/pallas_call | solution.py:229
  70.5 1.6 %collective-permute-start.14 = (f32[2,4,64,512]{3,2,1,0:T(8,128)S(1)}, f32[2,4,64,512]{3,2,1,0:T(8,128)S(1)}, u32[]{:S(2)}, u32[]{:S(2)}) collective-permute-start(f32[2,4,64,512]{3,2,1,0:T(8,128)S(1)} %get-tuple-element.38), channel_id=1, source_target_pairs={{4,8},{8,4},{12,0},{0,12},{5,9},{9,5},{13,1},{1,13},{6,10},{10,6},... | collective-permute-start | bytes 3145736 | tf_op jit(solution)/shard_map/ppermute | solution.py:350
  72.1 4.4 %shard_map.59 = (f32[4,64,512]{2,1,0:T(8,128)S(1)}, f32[4,64,512]{2,1,0:T(8,128)S(1)}, f32[2,4,64,512]{3,2,1,0:T(8,128)S(1)}) custom-call(s32[4]{0:T(128)S(1)} %pad_add_fusion.at, bf16[4,64,1024]{2,1,0:T(8,128)(2,1)S(1)} %get-tuple-element.41.c0.g0, bf16[4,64,1024]{2,1,0:T(8,128)(2,1)S(1)} %collective-permute-done.16.c1.g1, ...), custom_call_target="tpu_custom_call" | custom-call | flops 2415919104 | bytes 6000000 | tf_op jit(solution)/shard_map/pallas_call | solution.py:229
  76.6 4.8 %shard_map.60 = (f32[4,64,512]{2,1,0:T(8,128)S(1)}, f32[4,64,512]{2,1,0:T(8,128)S(1)}, f32[2,4,64,512]{3,2,1,0:T(8,128)S(1)}) custom-call(s32[4]{0:T(128)S(1)} %pad_add_fusion.at, bf16[4,64,1024]{2,1,0:T(8,128)(2,1)S(1)} %get-tuple-element.41.c0.g0, bf16[4,64,1024]{2,1,0:T(8,128)(2,1)S(1)} %collective-permute-done.16.c1.g1, ...), custom_call_target="tpu_custom_call" | custom-call | flops 2415919104 | bytes 6000000 | tf_op jit(solution)/shard_map/pallas_call | solution.py:229
  81.3 9.0 %weight_grads.1 = (f32[4,9,64,128]{3,2,1,0:T(8,128)S(1)}, f32[4,9,64,128]{3,2,1,0:T(8,128)S(1)}) custom-call(s32[4]{0:T(128)S(1)} %pad_add_fusion.at, bf16[4,64,1024]{2,1,0:T(8,128)(2,1)S(1)} %get-tuple-element.28.c0.x0, bf16[4,64,1024]{2,1,0:T(8,128)(2,1)S(1)} %collective-permute-done.c1.x1, bf16[4,64,1024]{2,1,0:T(8,128)(2,1)S(1)} %collective-permute-done.1.c2.x2, ...), custom_call_target="tpu_custom_call" | custom-call | flops 4831838208 | bytes 9000000 | tf_op jit(solution)/shard_map/weight_grads/pallas_call | solution.py:285
  90.4 0.9 collective-permute-start.25
  91.3 1.0 collective-permute-start.19
  92.3 2.5 %collective-permute-start.23 = (f32[2,4,64,512]{3,2,1,0:T(8,128)S(1)}, f32[2,4,64,512]{3,2,1,0:T(8,128)S(1)}, u32[]{:S(2)}, u32[]{:S(2)}) collective-permute-start(f32[2,4,64,512]{3,2,1,0:T(8,128)S(1)} %get-tuple-element.48), channel_id=1, source_target_pairs={{1,2},{2,1},{3,0},{0,3},{5,6},{6,5},{7,4},{4,7},{9,10},{10,9},{11,... | collective-permute-start | bytes 3145736 | tf_op jit(solution)/shard_map/ppermute | solution.py:354
  94.8 1.1 collective-permute-done.12.one_a
  96.0 1.9 %collective-permute-start.13 = (f32[4,64,512]{2,1,0:T(8,128)S(1)}, f32[4,64,512]{2,1,0:T(8,128)S(1)}, u32[]{:S(2)}, u32[]{:S(2)}) collective-permute-start(f32[4,64,512]{2,1,0:T(8,128)S(1)} %fusion.3), channel_id=1, source_target_pairs={{4,8},{8,4},{12,0},{0,12},{5,9},{9,5},{13,1},{1,13},{6,10},{10,6},... | collective-permute-start | bytes 1572872 | tf_op jit(solution)/shard_map/ppermute | solution.py:325
  98.2 2.0 %collective-permute-start.28 = (f32[9,64,128]{2,1,0:T(8,128)S(1)}, f32[9,64,128]{2,1,0:T(8,128)S(1)}, u32[]{:S(2)}, u32[]{:S(2)}) collective-permute-start(f32[9,64,128]{2,1,0:T(8,128)S(1)} %get-tuple-element.54), channel_id=1, source_target_pairs={{0,64},{32,96},{64,0},{96,32},{1,65},{33,97},{65,1},{97,33},{2,66}... | collective-permute-start | bytes 884744 | tf_op jit(solution)/shard_map/ppermute | solution.py:362
  100.2 1.8 %collective-permute-start.27 = (f32[9,64,128]{2,1,0:T(8,128)S(1)}, f32[9,64,128]{2,1,0:T(8,128)S(1)}, u32[]{:S(2)}, u32[]{:S(2)}) collective-permute-start(f32[9,64,128]{2,1,0:T(8,128)S(1)} %get-tuple-element.55), channel_id=1, source_target_pairs={{0,96},{32,0},{64,32},{96,64},{1,97},{33,1},{65,33},{97,65},{2,98}... | collective-permute-start | bytes 884744 | tf_op jit(solution)/shard_map/ppermute | solution.py:362
  102.0 14.4 %collective-permute-done.19.one_a = f32[2,4,64,512]{3,2,1,0:T(8,128)S(1)} collective-permute-done((f32[2,4,64,512]{3,2,1,0:T(8,128)S(1)}, f32[2,4,64,512]{3,2,1,0:T(8,128)S(1)}, u32[]{:S(2)}, u32[]{:S(2)}) %collective-permute-start.19) | collective-permute-done | bytes 1048608 | tf_op jit(solution)/shard_map/ppermute | solution.py:352
  116.4 1.8 %collective-permute-start.26 = (f32[9,64,128]{2,1,0:T(8,128)S(1)}, f32[9,64,128]{2,1,0:T(8,128)S(1)}, u32[]{:S(2)}, u32[]{:S(2)}) collective-permute-start(f32[9,64,128]{2,1,0:T(8,128)S(1)} %get-tuple-element.53), channel_id=1, source_target_pairs={{0,32},{32,64},{64,96},{96,0},{1,33},{33,65},{65,97},{97,1},{2,34}... | collective-permute-start | bytes 884744 | tf_op jit(solution)/shard_map/ppermute | solution.py:362
  118.4 1.2 collective-permute-start.15
  119.7 2.3 %collective-permute-start.20 = (f32[4,64,512]{2,1,0:T(8,128)S(1)}, f32[4,64,512]{2,1,0:T(8,128)S(1)}, u32[]{:S(2)}, u32[]{:S(2)}) collective-permute-start(f32[4,64,512]{2,1,0:T(8,128)S(1)} %fusion.1), channel_id=1, source_target_pairs={{1,2},{2,1},{3,0},{0,3},{5,6},{6,5},{7,4},{4,7},{9,10},{10,9},{11,... | collective-permute-start | bytes 1572872 | tf_op jit(solution)/shard_map/ppermute | solution.py:325
  121.9 0.7 collective-permute-start.24
  122.6 5.3 %collective-permute-done.26 = f32[9,64,128]{2,1,0:T(8,128)S(1)} collective-permute-done((f32[9,64,128]{2,1,0:T(8,128)S(1)}, f32[9,64,128]{2,1,0:T(8,128)S(1)}, u32[]{:S(2)}, u32[]{:S(2)}) %collective-permute-start.26) | collective-permute-done | bytes 294944 | tf_op jit(solution)/shard_map/ppermute | solution.py:362
  128.0 4.3 %collective-permute-start.29 = (f32[9,64,128]{2,1,0:T(8,128)S(1)}, f32[9,64,128]{2,1,0:T(8,128)S(1)}, u32[]{:S(2)}, u32[]{:S(2)}) collective-permute-start(f32[9,64,128]{2,1,0:T(8,128)S(1)} %fusion.6), channel_id=1, source_target_pairs={{0,0},{4,32},{8,64},{12,96},{32,4},{36,36},{40,68},{44,100},{64,8}... | collective-permute-start | bytes 884744 | tf_op jit(solution)/shard_map/ppermute | solution.py:364
  132.3 1.5 %collective-permute-done.20.two_a = f32[4,64,512]{2,1,0:T(8,128)S(1)} collective-permute-done((f32[4,64,512]{2,1,0:T(8,128)S(1)}, f32[4,64,512]{2,1,0:T(8,128)S(1)}, u32[]{:S(2)}, u32[]{:S(2)}) %collective-permute-start.20) | collective-permute-done | bytes 524320 | tf_op jit(solution)/shard_map/ppermute | solution.py:325
  133.8 0.7 collective-permute-done.24.two_b
  134.5 2.2 %finish.3 = bf16[8,8,4096]{2,1,0:T(8,128)(2,1)} custom-call(f32[4,64,512]{2,1,0:T(8,128)S(1)} %get-tuple-element.43.own_a, f32[2,4,64,512]{3,2,1,0:T(8,128)S(1)} %collective-permute-done.19.one_a, f32[4,64,512]{2,1,0:T(8,128)S(1)} %collective-permute-done.20.two_a, f32[4,64,512]{2,1,0:T(8,128)S(1)} %get-tuple-element.47.own_b, ...), custom_call_target="tpu_custom_call" | custom-call | tf_op jit(solution)/shard_map/finish/pallas_call | solution.py:103
  136.7 2.2 %finish.2 = bf16[8,8,4096]{2,1,0:T(8,128)(2,1)} custom-call(f32[4,64,512]{2,1,0:T(8,128)S(1)} %get-tuple-element.34.own_a, f32[2,4,64,512]{3,2,1,0:T(8,128)S(1)} %collective-permute-done.12.one_a, f32[4,64,512]{2,1,0:T(8,128)S(1)} %collective-permute-done.13.two_a, f32[4,64,512]{2,1,0:T(8,128)S(1)} %get-tuple-element.37.own_b, ...), custom_call_target="tpu_custom_call" | custom-call | tf_op jit(solution)/shard_map/finish/pallas_call | solution.py:103
  138.8 8.3 %collective-permute-done.29 = f32[9,64,128]{2,1,0:T(8,128)S(1)} collective-permute-done((f32[9,64,128]{2,1,0:T(8,128)S(1)}, f32[9,64,128]{2,1,0:T(8,128)S(1)}, u32[]{:S(2)}, u32[]{:S(2)}) %collective-permute-start.29) | collective-permute-done | bytes 294944 | tf_op jit(solution)/shard_map/ppermute | solution.py:364
  147.1 0.7 copy.7
  (49 shorter events, 3.0 us)
Async XLA Ops:
  0.6 1.0 copy-start
  1.7 1.0 copy-start.1
  2.7 18.1 %copy-start.2 = (bf16[3,3,64,128]{3,2,1,0:T(8,128)(2,1)S(1)}, bf16[3,3,64,128]{3,2,1,0:T(8,128)(2,1)}, u32[]{:S(2)}) copy-start(bf16[3,3,64,128]{3,2,1,0:T(8,128)(2,1)} %param.4) | copy-start | bytes 442372
  5.1 29.9 %collective-permute-start.1 = (bf16[4,64,1024]{2,1,0:T(8,128)(2,1)S(1)}, bf16[4,64,1024]{2,1,0:T(8,128)(2,1)S(1)}, u32[]{:S(2)}, u32[]{:S(2)}) collective-permute-start(bf16[4,64,1024]{2,1,0:T(8,128)(2,1)S(1)} %get-tuple-element.28.c0.x0), channel_id=1, source_target_pairs={{1,2},{2,1},{3,0},{0,3},{5,6},{6,5},{7,4},{4,7},{9,10},{10,9},{11,... | collective-permute-start | bytes 1572872 | tf_op jit(solution)/shard_map/ppermute | solution.py:312
  8.2 24.6 %collective-permute-start.2 = (bf16[4,64,1024]{2,1,0:T(8,128)(2,1)S(1)}, bf16[4,64,1024]{2,1,0:T(8,128)(2,1)S(1)}, u32[]{:S(2)}, u32[]{:S(2)}) collective-permute-start(bf16[4,64,1024]{2,1,0:T(8,128)(2,1)S(1)} %get-tuple-element.28.c0.x0), channel_id=1, source_target_pairs={{0,2},{1,3},{2,0},{3,1},{4,6},{5,7},{6,4},{7,5},{8,10},{9,11},{10,... | collective-permute-start | bytes 1572872 | tf_op jit(solution)/shard_map/ppermute | solution.py:312
  8.9 5.6 %collective-permute-start.5 = (bf16[9,64,128]{2,1,0:T(8,128)(2,1)}, bf16[9,64,128]{2,1,0:T(8,128)(2,1)S(1)}, u32[]{:S(2)}, u32[]{:S(2)}) collective-permute-start(bf16[9,64,128]{2,1,0:T(8,128)(2,1)} %bitcast.73), channel_id=1, source_target_pairs={{0,32},{32,0},{64,96},{96,64},{1,33},{33,1},{65,97},{97,65},{2,34}... | collective-permute-start | bytes 442376 | tf_op jit(solution)/shard_map/ppermute | solution.py:312
  10.8 8.3 %collective-permute-start.6 = (bf16[9,64,128]{2,1,0:T(8,128)(2,1)}, bf16[9,64,128]{2,1,0:T(8,128)(2,1)S(1)}, u32[]{:S(2)}, u32[]{:S(2)}) collective-permute-start(bf16[9,64,128]{2,1,0:T(8,128)(2,1)} %bitcast.74), channel_id=1, source_target_pairs={{32,64},{64,32},{96,0},{0,96},{33,65},{65,33},{97,1},{1,97},{34,66... | collective-permute-start | bytes 442376 | tf_op jit(solution)/shard_map/ppermute | solution.py:312
  13.3 7.5 %collective-permute-start.7 = (bf16[9,64,128]{2,1,0:T(8,128)(2,1)}, bf16[9,64,128]{2,1,0:T(8,128)(2,1)S(1)}, u32[]{:S(2)}, u32[]{:S(2)}) collective-permute-start(bf16[9,64,128]{2,1,0:T(8,128)(2,1)} %bitcast.75), channel_id=1, source_target_pairs={{0,64},{32,96},{64,0},{96,32},{1,65},{33,97},{65,1},{97,33},{2,66}... | collective-permute-start | bytes 442376 | tf_op jit(solution)/shard_map/ppermute | solution.py:312
  21.5 8.1 %collective-permute-start.10 = (bf16[9,64,128]{2,1,0:T(8,128)(2,1)S(1)}, bf16[9,64,128]{2,1,0:T(8,128)(2,1)S(1)}, u32[]{:S(2)}, u32[]{:S(2)}) collective-permute-start(bf16[9,64,128]{2,1,0:T(8,128)(2,1)S(1)} %get-tuple-element.32), channel_id=1, source_target_pairs={{0,8},{4,12},{8,0},{12,4},{1,9},{5,13},{9,1},{13,5},{2,10},{6,14},... | collective-permute-start | bytes 442376 | tf_op jit(solution)/shard_map/ppermute | solution.py:333
  23.0 7.8 %collective-permute-start.9 = (bf16[9,64,128]{2,1,0:T(8,128)(2,1)S(1)}, bf16[9,64,128]{2,1,0:T(8,128)(2,1)S(1)}, u32[]{:S(2)}, u32[]{:S(2)}) collective-permute-start(bf16[9,64,128]{2,1,0:T(8,128)(2,1)S(1)} %get-tuple-element.31), channel_id=1, source_target_pairs={{4,8},{8,4},{12,0},{0,12},{5,9},{9,5},{13,1},{1,13},{6,10},{10,6},... | collective-permute-start | bytes 442376 | tf_op jit(solution)/shard_map/ppermute | solution.py:333
  25.1 5.7 %collective-permute-start.8 = (bf16[9,64,128]{2,1,0:T(8,128)(2,1)S(1)}, bf16[9,64,128]{2,1,0:T(8,128)(2,1)S(1)}, u32[]{:S(2)}, u32[]{:S(2)}) collective-permute-start(bf16[9,64,128]{2,1,0:T(8,128)(2,1)S(1)} %get-tuple-element.30), channel_id=1, source_target_pairs={{0,4},{4,0},{8,12},{12,8},{1,5},{5,1},{9,13},{13,9},{2,6},{6,2},{1... | collective-permute-start | bytes 442376 | tf_op jit(solution)/shard_map/ppermute | solution.py:333
  29.6 10.1 %collective-permute-start = (bf16[4,64,1024]{2,1,0:T(8,128)(2,1)S(1)}, bf16[4,64,1024]{2,1,0:T(8,128)(2,1)S(1)}, u32[]{:S(2)}, u32[]{:S(2)}) collective-permute-start(bf16[4,64,1024]{2,1,0:T(8,128)(2,1)S(1)} %get-tuple-element.28.c0.x0), channel_id=1, source_target_pairs={{0,1},{1,0},{2,3},{3,2},{4,5},{5,4},{6,7},{7,6},{8,9},{9,8},{10,11... | collective-permute-start | bytes 1572872 | tf_op jit(solution)/shard_map/ppermute | solution.py:312
  30.7 26.0 %collective-permute-start.16 = (bf16[4,64,1024]{2,1,0:T(8,128)(2,1)S(1)}, bf16[4,64,1024]{2,1,0:T(8,128)(2,1)S(1)}, u32[]{:S(2)}, u32[]{:S(2)}) collective-permute-start(bf16[4,64,1024]{2,1,0:T(8,128)(2,1)S(1)} %get-tuple-element.41.c0.g0), channel_id=1, source_target_pairs={{0,4},{4,0},{8,12},{12,8},{1,5},{5,1},{9,13},{13,9},{2,6},{6,2},{1... | collective-permute-start | bytes 1572872 | tf_op jit(solution)/shard_map/ppermute | solution.py:312
  30.7 26.0 %collective-permute-start.17 = (bf16[4,64,1024]{2,1,0:T(8,128)(2,1)S(1)}, bf16[4,64,1024]{2,1,0:T(8,128)(2,1)S(1)}, u32[]{:S(2)}, u32[]{:S(2)}) collective-permute-start(bf16[4,64,1024]{2,1,0:T(8,128)(2,1)S(1)} %get-tuple-element.41.c0.g0), channel_id=1, source_target_pairs={{4,8},{8,4},{12,0},{0,12},{5,9},{9,5},{13,1},{1,13},{6,10},{10,6},... | collective-permute-start | bytes 1572872 | tf_op jit(solution)/shard_map/ppermute | solution.py:312
  32.8 22.6 %collective-permute-start.18 = (bf16[4,64,1024]{2,1,0:T(8,128)(2,1)S(1)}, bf16[4,64,1024]{2,1,0:T(8,128)(2,1)S(1)}, u32[]{:S(2)}, u32[]{:S(2)}) collective-permute-start(bf16[4,64,1024]{2,1,0:T(8,128)(2,1)S(1)} %get-tuple-element.41.c0.g0), channel_id=1, source_target_pairs={{0,8},{4,12},{8,0},{12,4},{1,9},{5,13},{9,1},{13,5},{2,10},{6,14},... | collective-permute-start | bytes 1572872 | tf_op jit(solution)/shard_map/ppermute | solution.py:312
  35.0 26.2 %collective-permute-start.11 = (bf16[4,9,64,128]{3,2,1,0:T(8,128)(2,1)S(1)}, bf16[4,9,64,128]{3,2,1,0:T(8,128)(2,1)S(1)}, u32[]{:S(2)}, u32[]{:S(2)}) collective-permute-start(bf16[4,9,64,128]{3,2,1,0:T(8,128)(2,1)S(1)} %pad_maximum_fusion.mine), channel_id=1, source_target_pairs={{0,16},{16,0},{1,17},{17,1},{2,18},{18,2},{3,19},{19,3},{4,20},{20... | collective-permute-start | bytes 1769480 | tf_op jit(solution)/shard_map/ppermute | solution.py:335
  39.8 23.1 %collective-permute-start.3 = (bf16[4,4,64,128]{3,2,1,0:T(8,128)(2,1)S(1)}, bf16[4,4,64,128]{3,2,1,0:T(8,128)(2,1)S(1)}, u32[]{:S(2)}, u32[]{:S(2)}) collective-permute-start(bf16[4,4,64,128]{3,2,1,0:T(8,128)(2,1)S(1)} %pad_maximum_fusion.1), channel_id=1, source_target_pairs={{0,16},{16,32},{32,48},{48,64},{64,80},{80,96},{96,112},{1,17},{17... | collective-permute-start | bytes 786440 | tf_op jit(solution)/shard_map/ppermute | solution.py:321
  55.4 7.4 %collective-permute-start.4 = (bf16[4,4,64,128]{3,2,1,0:T(8,128)(2,1)S(1)}, bf16[4,4,64,128]{3,2,1,0:T(8,128)(2,1)S(1)}, u32[]{:S(2)}, u32[]{:S(2)}) collective-permute-start(bf16[4,4,64,128]{3,2,1,0:T(8,128)(2,1)S(1)} %pad_maximum_fusion.2), channel_id=1, source_target_pairs={{16,0},{32,16},{48,32},{64,48},{80,64},{96,80},{112,96},{17,1},{33... | collective-permute-start | bytes 786440 | tf_op jit(solution)/shard_map/ppermute | solution.py:321
  56.9 19.7 %collective-permute-start.21 = (bf16[4,4,64,128]{3,2,1,0:T(8,128)(2,1)S(1)}, bf16[4,4,64,128]{3,2,1,0:T(8,128)(2,1)S(1)}, u32[]{:S(2)}, u32[]{:S(2)}) collective-permute-start(bf16[4,4,64,128]{3,2,1,0:T(8,128)(2,1)S(1)} %pad_maximum_fusion.3), channel_id=1, source_target_pairs={{0,16},{16,32},{32,48},{48,64},{64,80},{80,96},{96,112},{1,17},{17... | collective-permute-start | bytes 786440 | tf_op jit(solution)/shard_map/ppermute | solution.py:321
  60.0 16.6 %collective-permute-start.22 = (bf16[4,4,64,128]{3,2,1,0:T(8,128)(2,1)S(1)}, bf16[4,4,64,128]{3,2,1,0:T(8,128)(2,1)S(1)}, u32[]{:S(2)}, u32[]{:S(2)}) collective-permute-start(bf16[4,4,64,128]{3,2,1,0:T(8,128)(2,1)S(1)} %pad_maximum_fusion.4), channel_id=1, source_target_pairs={{16,0},{32,16},{48,32},{64,48},{80,64},{96,80},{112,96},{17,1},{33... | collective-permute-start | bytes 786440 | tf_op jit(solution)/shard_map/ppermute | solution.py:321
  69.9 26.0 %collective-permute-start.12 = (f32[2,4,64,512]{3,2,1,0:T(8,128)S(1)}, f32[2,4,64,512]{3,2,1,0:T(8,128)S(1)}, u32[]{:S(2)}, u32[]{:S(2)}) collective-permute-start(f32[2,4,64,512]{3,2,1,0:T(8,128)S(1)} %get-tuple-element.35), channel_id=1, source_target_pairs={{0,4},{4,0},{8,12},{12,8},{1,5},{5,1},{9,13},{13,9},{2,6},{6,2},{1... | collective-permute-start | bytes 3145736 | tf_op jit(solution)/shard_map/ppermute | solution.py:349
  70.5 27.4 %collective-permute-start.14 = (f32[2,4,64,512]{3,2,1,0:T(8,128)S(1)}, f32[2,4,64,512]{3,2,1,0:T(8,128)S(1)}, u32[]{:S(2)}, u32[]{:S(2)}) collective-permute-start(f32[2,4,64,512]{3,2,1,0:T(8,128)S(1)} %get-tuple-element.38), channel_id=1, source_target_pairs={{4,8},{8,4},{12,0},{0,12},{5,9},{9,5},{13,1},{1,13},{6,10},{10,6},... | collective-permute-start | bytes 3145736 | tf_op jit(solution)/shard_map/ppermute | solution.py:350
  90.4 7.6 %collective-permute-start.25 = (f32[4,9,64,128]{3,2,1,0:T(8,128)S(1)}, f32[4,9,64,128]{3,2,1,0:T(8,128)S(1)}, u32[]{:S(2)}, u32[]{:S(2)}) collective-permute-start(f32[4,9,64,128]{3,2,1,0:T(8,128)S(1)} %get-tuple-element.52), channel_id=1, source_target_pairs={{0,16},{16,0},{1,17},{17,1},{2,18},{18,2},{3,19},{19,3},{4,20},{20... | collective-permute-start | bytes 3538952 | tf_op jit(solution)/shard_map/ppermute | solution.py:357
  91.3 25.2 %collective-permute-start.19 = (f32[2,4,64,512]{3,2,1,0:T(8,128)S(1)}, f32[2,4,64,512]{3,2,1,0:T(8,128)S(1)}, u32[]{:S(2)}, u32[]{:S(2)}) collective-permute-start(f32[2,4,64,512]{3,2,1,0:T(8,128)S(1)} %get-tuple-element.44), channel_id=1, source_target_pairs={{0,1},{1,0},{2,3},{3,2},{4,5},{5,4},{6,7},{7,6},{8,9},{9,8},{10,11... | collective-permute-start | bytes 3145736 | tf_op jit(solution)/shard_map/ppermute | solution.py:352
  92.3 26.1 %collective-permute-start.23 = (f32[2,4,64,512]{3,2,1,0:T(8,128)S(1)}, f32[2,4,64,512]{3,2,1,0:T(8,128)S(1)}, u32[]{:S(2)}, u32[]{:S(2)}) collective-permute-start(f32[2,4,64,512]{3,2,1,0:T(8,128)S(1)} %get-tuple-element.48), channel_id=1, source_target_pairs={{1,2},{2,1},{3,0},{0,3},{5,6},{6,5},{7,4},{4,7},{9,10},{10,9},{11,... | collective-permute-start | bytes 3145736 | tf_op jit(solution)/shard_map/ppermute | solution.py:354
  96.0 40.7 %collective-permute-start.13 = (f32[4,64,512]{2,1,0:T(8,128)S(1)}, f32[4,64,512]{2,1,0:T(8,128)S(1)}, u32[]{:S(2)}, u32[]{:S(2)}) collective-permute-start(f32[4,64,512]{2,1,0:T(8,128)S(1)} %fusion.3), channel_id=1, source_target_pairs={{4,8},{8,4},{12,0},{0,12},{5,9},{9,5},{13,1},{1,13},{6,10},{10,6},... | collective-permute-start | bytes 1572872 | tf_op jit(solution)/shard_map/ppermute | solution.py:325
  98.2 21.4 %collective-permute-start.28 = (f32[9,64,128]{2,1,0:T(8,128)S(1)}, f32[9,64,128]{2,1,0:T(8,128)S(1)}, u32[]{:S(2)}, u32[]{:S(2)}) collective-permute-start(f32[9,64,128]{2,1,0:T(8,128)S(1)} %get-tuple-element.54), channel_id=1, source_target_pairs={{0,64},{32,96},{64,0},{96,32},{1,65},{33,97},{65,1},{97,33},{2,66}... | collective-permute-start | bytes 884744 | tf_op jit(solution)/shard_map/ppermute | solution.py:362
  100.2 21.7 %collective-permute-start.27 = (f32[9,64,128]{2,1,0:T(8,128)S(1)}, f32[9,64,128]{2,1,0:T(8,128)S(1)}, u32[]{:S(2)}, u32[]{:S(2)}) collective-permute-start(f32[9,64,128]{2,1,0:T(8,128)S(1)} %get-tuple-element.55), channel_id=1, source_target_pairs={{0,96},{32,0},{64,32},{96,64},{1,97},{33,1},{65,33},{97,65},{2,98}... | collective-permute-start | bytes 884744 | tf_op jit(solution)/shard_map/ppermute | solution.py:362
  116.4 11.4 %collective-permute-start.26 = (f32[9,64,128]{2,1,0:T(8,128)S(1)}, f32[9,64,128]{2,1,0:T(8,128)S(1)}, u32[]{:S(2)}, u32[]{:S(2)}) collective-permute-start(f32[9,64,128]{2,1,0:T(8,128)S(1)} %get-tuple-element.53), channel_id=1, source_target_pairs={{0,32},{32,64},{64,96},{96,0},{1,33},{33,65},{65,97},{97,1},{2,34}... | collective-permute-start | bytes 884744 | tf_op jit(solution)/shard_map/ppermute | solution.py:362
  118.4 18.3 %collective-permute-start.15 = (f32[4,64,512]{2,1,0:T(8,128)S(1)}, f32[4,64,512]{2,1,0:T(8,128)S(1)}, u32[]{:S(2)}, u32[]{:S(2)}) collective-permute-start(f32[4,64,512]{2,1,0:T(8,128)S(1)} %fusion.2), channel_id=1, source_target_pairs={{0,4},{4,0},{8,12},{12,8},{1,5},{5,1},{9,13},{13,9},{2,6},{6,2},{1... | collective-permute-start | bytes 1572872 | tf_op jit(solution)/shard_map/ppermute | solution.py:326
  119.7 14.1 %collective-permute-start.20 = (f32[4,64,512]{2,1,0:T(8,128)S(1)}, f32[4,64,512]{2,1,0:T(8,128)S(1)}, u32[]{:S(2)}, u32[]{:S(2)}) collective-permute-start(f32[4,64,512]{2,1,0:T(8,128)S(1)} %fusion.1), channel_id=1, source_target_pairs={{1,2},{2,1},{3,0},{0,3},{5,6},{6,5},{7,4},{4,7},{9,10},{10,9},{11,... | collective-permute-start | bytes 1572872 | tf_op jit(solution)/shard_map/ppermute | solution.py:325
  121.9 12.6 %collective-permute-start.24 = (f32[4,64,512]{2,1,0:T(8,128)S(1)}, f32[4,64,512]{2,1,0:T(8,128)S(1)}, u32[]{:S(2)}, u32[]{:S(2)}) collective-permute-start(f32[4,64,512]{2,1,0:T(8,128)S(1)} %fusion), channel_id=1, source_target_pairs={{0,1},{1,0},{2,3},{3,2},{4,5},{5,4},{6,7},{7,6},{8,9},{9,8},{10,11... | collective-permute-start | bytes 1572872 | tf_op jit(solution)/shard_map/ppermute | solution.py:326
  128.0 19.2 %collective-permute-start.29 = (f32[9,64,128]{2,1,0:T(8,128)S(1)}, f32[9,64,128]{2,1,0:T(8,128)S(1)}, u32[]{:S(2)}, u32[]{:S(2)}) collective-permute-start(f32[9,64,128]{2,1,0:T(8,128)S(1)} %fusion.6), channel_id=1, source_target_pairs={{0,0},{4,32},{8,64},{12,96},{32,4},{36,36},{40,68},{44,100},{64,8}... | collective-permute-start | bytes 884744 | tf_op jit(solution)/shard_map/ppermute | solution.py:364

commit v4 on v3

--- a/solution.py
+++ b/solution.py
@@ -72,7 +72,12 @@
 ROWS = ((1, 2, 3, 4), (5, 6, 7, 0))
 
 
-def finish_kernel(own_a, one_a, two_a, own_b, one_b, two_b, o_hbm, given, mix_ref, rows_ref, out_sem):
+def finish_kernel(own_a, one_a, two_a, own_b, one_b, two_b, *refs):
+    given, mix_ref, rows_ref, out_sem, more_sem = refs[-5:]
+    o_hbm = refs[-6] if len(refs) == 6 else refs[1]
+    more = pltpu.make_async_copy(refs[0], refs[2], more_sem) if len(refs) == 8 else None
+    if more is not None:
+        more.start()
     low = lane_of((32, LANES)) < W
     pieces = ((own_a, one_a, two_a), (own_b, one_b, two_b))
 
@@ -97,19 +102,25 @@
     for q in range(4):
         for side in range(2):
             put(q, side).wait()
+    if more is not None:
+        more.wait()
 
 
 def finish(*pieces):
+    shapes = [jax.ShapeDtypeStruct((8, 8, 4096), BF16)]
+    shapes += [jax.ShapeDtypeStruct(piece.shape, piece.dtype) for piece in pieces[6:]]
+    specs = [pl.BlockSpec(memory_space=pl.ANY)] * len(shapes)
     return pl.pallas_call(
         finish_kernel,
-        out_shape=jax.ShapeDtypeStruct((8, 8, 4096), BF16),
-        in_specs=[pl.BlockSpec(memory_space=pltpu.VMEM)] * 6,
-        out_specs=pl.BlockSpec(memory_space=pl.ANY),
+        out_shape=shapes if len(shapes) > 1 else shapes[0],
+        in_specs=[pl.BlockSpec(memory_space=pltpu.VMEM)] * len(pieces),
+        out_specs=specs if len(shapes) > 1 else specs[0],
         scratch_shapes=[
             pltpu.VMEM((4, 2, 8, 4096), BF16),
             pltpu.VMEM((2, 8, 64, LANES), F32),
             pltpu.VMEM((2, 2, 8, 32, LANES), F32),
             pltpu.SemaphoreType.DMA((4, 2)),
+            pltpu.SemaphoreType.DMA,
         ],
         compiler_params=params(12),
         name="finish",
@@ -324,7 +335,7 @@
 def reduce_second(a, b, one_a, one_b, axis):
     two_a = lax.ppermute(a[1] + one_a[1], axis, SECOND)
     two_b = lax.ppermute(b[1] + one_b[1], axis, FIRST)
-    return finish(a[0], one_a, two_a, b[0], one_b, two_b)
+    return a[0], one_a, two_a, b[0], one_b, two_b
 
 
 def fetch_weights(at, block):
@@ -348,21 +359,22 @@
     out_a, out_b = out[:3], out[3:]
     out_one_a = lax.ppermute(out_a[2], "x", FIRST)
     out_one_b = lax.ppermute(out_b[2], "x", SECOND)
-    grad_a = conv((0,), after(at, out_a[0]), g_chunks, g_sides, turned)
+    grad = conv((0, 1), after(at, out_a[0]), g_chunks, g_sides, turned)
+    grad_a, grad_b = grad[:3], grad[3:]
     grad_one_a = lax.ppermute(grad_a[2], "y", FIRST)
-    grad_b = conv((1,), after(at, grad_a[0]), g_chunks, g_sides, turned)
     grad_one_b = lax.ppermute(grad_b[2], "y", SECOND)
 
     near, far = weight_grads(after(at, grad_b[0]), x_chunks, *x_sides, g_chunks)
     near = near + lax.ppermute(far, "core", SWAP)
-    output_maps = reduce_second(out_a, out_b, out_one_a, out_one_b, "x")
-    input_grad = reduce_second(grad_a, grad_b, grad_one_a, grad_one_b, "y")
+    output_maps = finish(*reduce_second(out_a, out_b, out_one_a, out_one_b, "x"))
+    grad_pieces = reduce_second(grad_a, grad_b, grad_one_a, grad_one_b, "y")
     total = near[0]
     for k, turn in ((1, 1), (2, 3), (3, 2)):
         total = total + lax.ppermute(near[k], "z", ring(turn))
     cross = [(z * 4 + x, x * 4 + z) for z in range(4) for x in range(4)]
-    kernel_grad = lax.ppermute(total, ("z", "x"), cross).reshape(3, 3, 64, LANES)
-    return output_maps, input_grad, kernel_grad
+    home = lax.ppermute(total, ("z", "x"), cross)
+    input_grad, kernel_grad = finish(*grad_pieces, home)
+    return output_maps, input_grad, kernel_grad.reshape(3, 3, 64, LANES)
 
 
 def solution(mesh):

time: 148 us -> 138 us (0.932)
  the two profiles are of different devices: /device:TPU:6 before, /device:TPU:97 now
where the time goes in v4:
time: 138 us
  waiting for transfers between devices  53.3 us (39%)
  starting transfers between devices  48.4 us (35%)
  Pallas kernels  32.1 us (23%)
  local copies, waits for them, and re-layouts  2.36 us (2%)
    ppermute x1, waiting for transfers between devices, step(): grad_one_a = lax.ppermute(grad_a[2], 'y', FIRST)  16.8 us
    pallas_call x2, Pallas kernels, conv(): pl.pallas_call(functools.partial(conv_kernel, halves, rows), out_shape=(s...  14.1 us
    ppermute x2, starting transfers between devices, edges(): lax.ppermute(first, ('z', 'core'), backward)  13.6 us
    ppermute x1, waiting for transfers between devices, step(): home = lax.ppermute(total, ('z', 'x'), cross)  12.4 us
    ppermute x3, waiting for transfers between devices, gather(): lax.ppermute(block, axis, SECOND)  11 us
    pallas_call x1, Pallas kernels, weight_grads(): pl.pallas_call(kernel_grad_kernel, out_shape=(shape,) * 2, grid=(4,), in_...  9.04 us
    ppermute x3, starting transfers between devices, gather(): lax.ppermute(block, axis, OPPOSITE)  5.06 us
    pallas_call x2, Pallas kernels, finish(): pl.pallas_call(finish_kernel, out_shape=shapes if len(shapes) > 1 else sh...  4.32 us
  transfers between devices with their start and end apart: 30, of which 9 were waited for; matrix products, arithmetic and copies ran while one was open for 1% of the time, Pallas kernels for 22%

profile of v4, /device:TPU:97, one launch (start us, length us, event | category | flops | bytes accessed | tf_op | source)
XLA Modules:
  0.0 138.2 jit_solution(8159372471843633951)
XLA Ops:
  0.6 0.4 collective-permute-start.7
  1.0 2.2 %collective-permute-start.6 = (bf16[9,64,128]{2,1,0:T(8,128)(2,1)}, bf16[9,64,128]{2,1,0:T(8,128)(2,1)S(1)}, u32[]{:S(2)}, u32[]{:S(2)}) collective-permute-start(bf16[9,64,128]{2,1,0:T(8,128)(2,1)} %bitcast.74), channel_id=1, source_target_pairs={{32,64},{64,32},{96,0},{0,96},{33,65},{65,33},{97,1},{1,97},{34,66... | collective-permute-start | bytes 442376 | tf_op jit(solution)/shard_map/ppermute | solution.py:323
  3.2 0.1 collective-permute-start.5
  3.4 1.0 copy-done
  4.4 1.0 copy-done.1
  5.4 2.4 %pack.1 = (bf16[4,64,1024]{2,1,0:T(8,128)(2,1)S(1)}, bf16[4,64,1024]{2,1,0:T(8,128)(2,1)S(1)}) custom-call(bf16[8,8,4096]{2,1,0:T(8,128)(2,1)S(1)} %copy-done, bf16[8,8,4096]{2,1,0:T(8,128)(2,1)S(1)} %copy-done.1), custom_call_target="tpu_custom_call" | custom-call | tf_op jit(solution)/shard_map/pack/pallas_call | solution.py:61
  7.9 3.0 %collective-permute-start.2 = (bf16[4,64,1024]{2,1,0:T(8,128)(2,1)S(1)}, bf16[4,64,1024]{2,1,0:T(8,128)(2,1)S(1)}, u32[]{:S(2)}, u32[]{:S(2)}) collective-permute-start(bf16[4,64,1024]{2,1,0:T(8,128)(2,1)S(1)} %get-tuple-element.29.c0.x0), channel_id=1, source_target_pairs={{0,2},{1,3},{2,0},{3,1},{4,6},{5,7},{6,4},{7,5},{8,10},{9,11},{10,... | collective-permute-start | bytes 1572872 | tf_op jit(solution)/shard_map/ppermute | solution.py:323
  10.9 0.8 collective-permute-start.1
  11.8 0.6 route.1
  12.4 1.3 collective-permute-start.8
  13.7 1.8 %collective-permute-start.9 = (bf16[9,64,128]{2,1,0:T(8,128)(2,1)S(1)}, bf16[9,64,128]{2,1,0:T(8,128)(2,1)S(1)}, u32[]{:S(2)}, u32[]{:S(2)}) collective-permute-start(bf16[9,64,128]{2,1,0:T(8,128)(2,1)S(1)} %get-tuple-element.32), channel_id=1, source_target_pairs={{4,8},{8,4},{12,0},{0,12},{5,9},{9,5},{13,1},{1,13},{6,10},{10,6},... | collective-permute-start | bytes 442376 | tf_op jit(solution)/shard_map/ppermute | solution.py:344
  15.5 0.6 collective-permute-start.10
  16.2 0.6 collective-permute-done.8
  16.8 1.4 %collective-permute-start = (bf16[4,64,1024]{2,1,0:T(8,128)(2,1)S(1)}, bf16[4,64,1024]{2,1,0:T(8,128)(2,1)S(1)}, u32[]{:S(2)}, u32[]{:S(2)}) collective-permute-start(bf16[4,64,1024]{2,1,0:T(8,128)(2,1)S(1)} %get-tuple-element.29.c0.x0), channel_id=1, source_target_pairs={{0,1},{1,0},{2,3},{3,2},{4,5},{5,4},{6,7},{7,6},{8,9},{9,8},{10,11... | collective-permute-start | bytes 1572872 | tf_op jit(solution)/shard_map/ppermute | solution.py:323
  18.2 1.0 collective-permute-done.9
  19.2 1.7 %collective-permute-start.18 = (bf16[4,64,1024]{2,1,0:T(8,128)(2,1)S(1)}, bf16[4,64,1024]{2,1,0:T(8,128)(2,1)S(1)}, u32[]{:S(2)}, u32[]{:S(2)}) collective-permute-start(bf16[4,64,1024]{2,1,0:T(8,128)(2,1)S(1)} %get-tuple-element.42.c0.g0), channel_id=1, source_target_pairs={{0,8},{4,12},{8,0},{12,4},{1,9},{5,13},{9,1},{13,5},{2,10},{6,14},... | collective-permute-start | bytes 1572872 | tf_op jit(solution)/shard_map/ppermute | solution.py:323
  20.9 1.8 %collective-permute-done.10 = bf16[9,64,128]{2,1,0:T(8,128)(2,1)S(1)} collective-permute-done((bf16[9,64,128]{2,1,0:T(8,128)(2,1)S(1)}, bf16[9,64,128]{2,1,0:T(8,128)(2,1)S(1)}, u32[]{:S(2)}, u32[]{:S(2)}) %collective-permute-start.10) | collective-permute-done | bytes 147488 | tf_op jit(solution)/shard_map/ppermute | solution.py:344
  22.7 0.6 collective-permute-start.17
  23.4 0.1 collective-permute-start.16
  23.5 11.0 %collective-permute-done.1.c2.x2 = bf16[4,64,1024]{2,1,0:T(8,128)(2,1)S(1)} collective-permute-done((bf16[4,64,1024]{2,1,0:T(8,128)(2,1)S(1)}, bf16[4,64,1024]{2,1,0:T(8,128)(2,1)S(1)}, u32[]{:S(2)}, u32[]{:S(2)}) %collective-permute-start.1) | collective-permute-done | bytes 524320 | tf_op jit(solution)/shard_map/ppermute | solution.py:323
  34.5 0.5 collective-permute-start.11
  35.1 1.3 collective-permute-start.3
  36.5 7.3 %collective-permute-start.4 = (bf16[4,4,64,128]{3,2,1,0:T(8,128)(2,1)S(1)}, bf16[4,4,64,128]{3,2,1,0:T(8,128)(2,1)S(1)}, u32[]{:S(2)}, u32[]{:S(2)}) collective-permute-start(bf16[4,4,64,128]{3,2,1,0:T(8,128)(2,1)S(1)} %pad_maximum_fusion.2), channel_id=1, source_target_pairs={{16,0},{32,16},{48,32},{64,48},{80,64},{96,80},{112,96},{17,1},{33... | collective-permute-start | bytes 786440 | tf_op jit(solution)/shard_map/ppermute | solution.py:332
  43.9 1.3 collective-permute-start.19
  45.3 6.3 %collective-permute-start.20 = (bf16[4,4,64,128]{3,2,1,0:T(8,128)(2,1)S(1)}, bf16[4,4,64,128]{3,2,1,0:T(8,128)(2,1)S(1)}, u32[]{:S(2)}, u32[]{:S(2)}) collective-permute-start(bf16[4,4,64,128]{3,2,1,0:T(8,128)(2,1)S(1)} %pad_maximum_fusion.4), channel_id=1, source_target_pairs={{16,0},{32,16},{48,32},{64,48},{80,64},{96,80},{112,96},{17,1},{33... | collective-permute-start | bytes 786440 | tf_op jit(solution)/shard_map/ppermute | solution.py:332
  51.6 1.6 %weights.1 = (bf16[3,256,768]{2,1,0:T(8,128)(2,1)S(1)}, bf16[3,256,768]{2,1,0:T(8,128)(2,1)S(1)}) custom-call(s32[4]{0:T(128)S(1)} %pad_add_fusion.at, bf16[4,9,64,128]{3,2,1,0:T(8,128)(2,1)S(1)} %pad_maximum_fusion.mine, bf16[4,9,64,128]{3,2,1,0:T(8,128)(2,1)S(1)} %collective-permute-done.11.other), custom_call_target="tpu_custom_call" | custom-call | tf_op jit(solution)/shard_map/weights/pallas_call | solution.py:178
  53.2 7.1 %shard_map.58 = (f32[4,64,512]{2,1,0:T(8,128)S(1)}, f32[4,64,512]{2,1,0:T(8,128)S(1)}, f32[2,4,64,512]{3,2,1,0:T(8,128)S(1)}, f32[4,64,512]{2,1,0:T(8,128)S(1)},...) custom-call(s32[4]{0:T(128)S(1)} %pad_add_fusion.at, bf16[4,64,1024]{2,1,0:T(8,128)(2,1)S(1)} %get-tuple-element.29.c0.x0, ...), custom_call_target="tpu_custom_call" | custom-call | flops 4831838208 | bytes 12000000 | tf_op jit(solution)/shard_map/pallas_call | solution.py:240
  60.3 0.1 collective-permute-start.12
  60.4 1.7 %collective-permute-start.14 = (f32[2,4,64,512]{3,2,1,0:T(8,128)S(1)}, f32[2,4,64,512]{3,2,1,0:T(8,128)S(1)}, u32[]{:S(2)}, u32[]{:S(2)}) collective-permute-start(f32[2,4,64,512]{3,2,1,0:T(8,128)S(1)} %get-tuple-element.39), channel_id=1, source_target_pairs={{4,8},{8,4},{12,0},{0,12},{5,9},{9,5},{13,1},{1,13},{6,10},{10,6},... | collective-permute-start | bytes 3145736 | tf_op jit(solution)/shard_map/ppermute | solution.py:361
  62.1 7.0 %shard_map.59 = (f32[4,64,512]{2,1,0:T(8,128)S(1)}, f32[4,64,512]{2,1,0:T(8,128)S(1)}, f32[2,4,64,512]{3,2,1,0:T(8,128)S(1)}, f32[4,64,512]{2,1,0:T(8,128)S(1)},...) custom-call(s32[4]{0:T(128)S(1)} %pad_add_fusion.at, bf16[4,64,1024]{2,1,0:T(8,128)(2,1)S(1)} %get-tuple-element.42.c0.g0, ...), custom_call_target="tpu_custom_call" | custom-call | flops 4831838208 | bytes 12000000 | tf_op jit(solution)/shard_map/pallas_call | solution.py:240
  69.1 9.0 %weight_grads.1 = (f32[4,9,64,128]{3,2,1,0:T(8,128)S(1)}, f32[4,9,64,128]{3,2,1,0:T(8,128)S(1)}) custom-call(s32[4]{0:T(128)S(1)} %pad_add_fusion.at, bf16[4,64,1024]{2,1,0:T(8,128)(2,1)S(1)} %get-tuple-element.29.c0.x0, bf16[4,64,1024]{2,1,0:T(8,128)(2,1)S(1)} %collective-permute-done.c1.x1, bf16[4,64,1024]{2,1,0:T(8,128)(2,1)S(1)} %collective-permute-done.1.c2.x2, ...), custom_call_target="tpu_custom_call" | custom-call | flops 4831838208 | bytes 9000000 | tf_op jit(solution)/shard_map/weight_grads/pallas_call | solution.py:296
  78.2 2.1 %collective-permute-start.25 = (f32[4,9,64,128]{3,2,1,0:T(8,128)S(1)}, f32[4,9,64,128]{3,2,1,0:T(8,128)S(1)}, u32[]{:S(2)}, u32[]{:S(2)}) collective-permute-start(f32[4,9,64,128]{3,2,1,0:T(8,128)S(1)} %get-tuple-element.52), channel_id=1, source_target_pairs={{0,16},{16,0},{1,17},{17,1},{2,18},{18,2},{3,19},{19,3},{4,20},{20... | collective-permute-start | bytes 3538952 | tf_op jit(solution)/shard_map/ppermute | solution.py:368
  80.3 3.1 %collective-permute-start.21 = (f32[2,4,64,512]{3,2,1,0:T(8,128)S(1)}, f32[2,4,64,512]{3,2,1,0:T(8,128)S(1)}, u32[]{:S(2)}, u32[]{:S(2)}) collective-permute-start(f32[2,4,64,512]{3,2,1,0:T(8,128)S(1)} %get-tuple-element.45), channel_id=1, source_target_pairs={{0,1},{1,0},{2,3},{3,2},{4,5},{5,4},{6,7},{7,6},{8,9},{9,8},{10,11... | collective-permute-start | bytes 3145736 | tf_op jit(solution)/shard_map/ppermute | solution.py:364
  83.4 1.7 %collective-permute-start.23 = (f32[2,4,64,512]{3,2,1,0:T(8,128)S(1)}, f32[2,4,64,512]{3,2,1,0:T(8,128)S(1)}, u32[]{:S(2)}, u32[]{:S(2)}) collective-permute-start(f32[2,4,64,512]{3,2,1,0:T(8,128)S(1)} %get-tuple-element.48), channel_id=1, source_target_pairs={{1,2},{2,1},{3,0},{0,3},{5,6},{6,5},{7,4},{4,7},{9,10},{10,9},{11,... | collective-permute-start | bytes 3145736 | tf_op jit(solution)/shard_map/ppermute | solution.py:365
  85.2 0.6 collective-permute-start.13
  85.9 0.2 add.28
  86.2 1.0 collective-permute-start.26
  87.3 2.7 %collective-permute-start.28 = (f32[9,64,128]{2,1,0:T(8,128)S(1)}, f32[9,64,128]{2,1,0:T(8,128)S(1)}, u32[]{:S(2)}, u32[]{:S(2)}) collective-permute-start(f32[9,64,128]{2,1,0:T(8,128)S(1)} %get-tuple-element.56), channel_id=1, source_target_pairs={{0,64},{32,96},{64,0},{96,32},{1,65},{33,97},{65,1},{97,33},{2,66}... | collective-permute-start | bytes 884744 | tf_op jit(solution)/shard_map/ppermute | solution.py:373
  90.0 16.8 %collective-permute-done.21.one_a = f32[2,4,64,512]{3,2,1,0:T(8,128)S(1)} collective-permute-done((f32[2,4,64,512]{3,2,1,0:T(8,128)S(1)}, f32[2,4,64,512]{3,2,1,0:T(8,128)S(1)}, u32[]{:S(2)}, u32[]{:S(2)}) %collective-permute-start.21) | collective-permute-done | bytes 1048608 | tf_op jit(solution)/shard_map/ppermute | solution.py:364
  106.9 2.0 %collective-permute-done.23.one_b = f32[2,4,64,512]{3,2,1,0:T(8,128)S(1)} collective-permute-done((f32[2,4,64,512]{3,2,1,0:T(8,128)S(1)}, f32[2,4,64,512]{3,2,1,0:T(8,128)S(1)}, u32[]{:S(2)}, u32[]{:S(2)}) %collective-permute-start.23) | collective-permute-done | bytes 1048608 | tf_op jit(solution)/shard_map/ppermute | solution.py:365
  109.0 0.8 collective-permute-start.15
  109.9 1.8 %collective-permute-start.22 = (f32[4,64,512]{2,1,0:T(8,128)S(1)}, f32[4,64,512]{2,1,0:T(8,128)S(1)}, u32[]{:S(2)}, u32[]{:S(2)}) collective-permute-start(f32[4,64,512]{2,1,0:T(8,128)S(1)} %fusion.1), channel_id=1, source_target_pairs={{1,2},{2,1},{3,0},{0,3},{5,6},{6,5},{7,4},{4,7},{9,10},{10,9},{11,... | collective-permute-start | bytes 1572872 | tf_op jit(solution)/shard_map/ppermute | solution.py:336
  111.7 4.2 %collective-permute-done.27 = f32[9,64,128]{2,1,0:T(8,128)S(1)} collective-permute-done((f32[9,64,128]{2,1,0:T(8,128)S(1)}, f32[9,64,128]{2,1,0:T(8,128)S(1)}, u32[]{:S(2)}, u32[]{:S(2)}) %collective-permute-start.27) | collective-permute-done | bytes 294944 | tf_op jit(solution)/shard_map/ppermute | solution.py:373
  116.0 1.9 %collective-permute-start.29 = (f32[9,64,128]{2,1,0:T(8,128)S(1)}, f32[9,64,128]{2,1,0:T(8,128)S(1)}, u32[]{:S(2)}, u32[]{:S(2)}) collective-permute-start(f32[9,64,128]{2,1,0:T(8,128)S(1)} %fusion.6), channel_id=1, source_target_pairs={{0,0},{4,32},{8,64},{12,96},{32,4},{36,36},{40,68},{44,100},{64,8}... | collective-permute-start | bytes 884744 | tf_op jit(solution)/shard_map/ppermute | solution.py:375
  117.9 3.3 %collective-permute-done.15.two_b = f32[4,64,512]{2,1,0:T(8,128)S(1)} collective-permute-done((f32[4,64,512]{2,1,0:T(8,128)S(1)}, f32[4,64,512]{2,1,0:T(8,128)S(1)}, u32[]{:S(2)}, u32[]{:S(2)}) %collective-permute-start.15) | collective-permute-done | bytes 524320 | tf_op jit(solution)/shard_map/ppermute | solution.py:337
  121.2 2.2 %finish.2 = bf16[8,8,4096]{2,1,0:T(8,128)(2,1)} custom-call(f32[4,64,512]{2,1,0:T(8,128)S(1)} %get-tuple-element.35.own_a, f32[2,4,64,512]{3,2,1,0:T(8,128)S(1)} %collective-permute-done.12.one_a, f32[4,64,512]{2,1,0:T(8,128)S(1)} %collective-permute-done.13.two_a, f32[4,64,512]{2,1,0:T(8,128)S(1)} %get-tuple-element.38.own_b, ...), custom_call_target="tpu_custom_call" | custom-call | tf_op jit(solution)/shard_map/finish/pallas_call | solution.py:113
  123.4 12.4 %collective-permute-done.29.refs_0_ = f32[9,64,128]{2,1,0:T(8,128)S(1)} collective-permute-done((f32[9,64,128]{2,1,0:T(8,128)S(1)}, f32[9,64,128]{2,1,0:T(8,128)S(1)}, u32[]{:S(2)}, u32[]{:S(2)}) %collective-permute-start.29) | collective-permute-done | bytes 294944 | tf_op jit(solution)/shard_map/ppermute | solution.py:375
  135.8 2.2 %finish.3 = (bf16[8,8,4096]{2,1,0:T(8,128)(2,1)}, f32[9,64,128]{2,1,0:T(8,128)}) custom-call(f32[4,64,512]{2,1,0:T(8,128)S(1)} %get-tuple-element.44.own_a, f32[2,4,64,512]{3,2,1,0:T(8,128)S(1)} %collective-permute-done.21.one_a, f32[4,64,512]{2,1,0:T(8,128)S(1)} %collective-permute-done.22.two_a, f32[4,64,512]{2,1,0:T(8,128)S(1)} %get-tuple-element.47.own_b, ...), custom_call_target="tpu_custom_call" | custom-call | tf_op jit(solution)/shard_map/finish/pallas_call | solution.py:113
  (47 shorter events, 1.1 us)
Async XLA Ops:
  0.6 11.1 %collective-permute-start.7 = (bf16[9,64,128]{2,1,0:T(8,128)(2,1)}, bf16[9,64,128]{2,1,0:T(8,128)(2,1)S(1)}, u32[]{:S(2)}, u32[]{:S(2)}) collective-permute-start(bf16[9,64,128]{2,1,0:T(8,128)(2,1)} %bitcast.73), channel_id=1, source_target_pairs={{0,64},{32,96},{64,0},{96,32},{1,65},{33,97},{65,1},{97,33},{2,66}... | collective-permute-start | bytes 442376 | tf_op jit(solution)/shard_map/ppermute | solution.py:323
  1.0 10.8 %collective-permute-start.6 = (bf16[9,64,128]{2,1,0:T(8,128)(2,1)}, bf16[9,64,128]{2,1,0:T(8,128)(2,1)S(1)}, u32[]{:S(2)}, u32[]{:S(2)}) collective-permute-start(bf16[9,64,128]{2,1,0:T(8,128)(2,1)} %bitcast.74), channel_id=1, source_target_pairs={{32,64},{64,32},{96,0},{0,96},{33,65},{65,33},{97,1},{1,97},{34,66... | collective-permute-start | bytes 442376 | tf_op jit(solution)/shard_map/ppermute | solution.py:323
  3.2 8.5 %collective-permute-start.5 = (bf16[9,64,128]{2,1,0:T(8,128)(2,1)}, bf16[9,64,128]{2,1,0:T(8,128)(2,1)S(1)}, u32[]{:S(2)}, u32[]{:S(2)}) collective-permute-start(bf16[9,64,128]{2,1,0:T(8,128)(2,1)} %bitcast.75), channel_id=1, source_target_pairs={{0,32},{32,0},{64,96},{96,64},{1,33},{33,1},{65,97},{97,65},{2,34}... | collective-permute-start | bytes 442376 | tf_op jit(solution)/shard_map/ppermute | solution.py:323
  3.4 1.0 copy-start
  4.4 1.0 copy-start.1
  5.4 6.3 %copy-start.2 = (bf16[3,3,64,128]{3,2,1,0:T(8,128)(2,1)S(1)}, bf16[3,3,64,128]{3,2,1,0:T(8,128)(2,1)}, u32[]{:S(2)}) copy-start(bf16[3,3,64,128]{3,2,1,0:T(8,128)(2,1)} %param.4) | copy-start | bytes 442372
  7.9 15.5 %collective-permute-start.2 = (bf16[4,64,1024]{2,1,0:T(8,128)(2,1)S(1)}, bf16[4,64,1024]{2,1,0:T(8,128)(2,1)S(1)}, u32[]{:S(2)}, u32[]{:S(2)}) collective-permute-start(bf16[4,64,1024]{2,1,0:T(8,128)(2,1)S(1)} %get-tuple-element.29.c0.x0), channel_id=1, source_target_pairs={{0,2},{1,3},{2,0},{3,1},{4,6},{5,7},{6,4},{7,5},{8,10},{9,11},{10,... | collective-permute-start | bytes 1572872 | tf_op jit(solution)/shard_map/ppermute | solution.py:323
  10.9 23.7 %collective-permute-start.1 = (bf16[4,64,1024]{2,1,0:T(8,128)(2,1)S(1)}, bf16[4,64,1024]{2,1,0:T(8,128)(2,1)S(1)}, u32[]{:S(2)}, u32[]{:S(2)}) collective-permute-start(bf16[4,64,1024]{2,1,0:T(8,128)(2,1)S(1)} %get-tuple-element.29.c0.x0), channel_id=1, source_target_pairs={{1,2},{2,1},{3,0},{0,3},{5,6},{6,5},{7,4},{4,7},{9,10},{10,9},{11,... | collective-permute-start | bytes 1572872 | tf_op jit(solution)/shard_map/ppermute | solution.py:323
  12.4 4.4 %collective-permute-start.8 = (bf16[9,64,128]{2,1,0:T(8,128)(2,1)S(1)}, bf16[9,64,128]{2,1,0:T(8,128)(2,1)S(1)}, u32[]{:S(2)}, u32[]{:S(2)}) collective-permute-start(bf16[9,64,128]{2,1,0:T(8,128)(2,1)S(1)} %get-tuple-element.31), channel_id=1, source_target_pairs={{0,4},{4,0},{8,12},{12,8},{1,5},{5,1},{9,13},{13,9},{2,6},{6,2},{1... | collective-permute-start | bytes 442376 | tf_op jit(solution)/shard_map/ppermute | solution.py:344
  13.7 5.5 %collective-permute-start.9 = (bf16[9,64,128]{2,1,0:T(8,128)(2,1)S(1)}, bf16[9,64,128]{2,1,0:T(8,128)(2,1)S(1)}, u32[]{:S(2)}, u32[]{:S(2)}) collective-permute-start(bf16[9,64,128]{2,1,0:T(8,128)(2,1)S(1)} %get-tuple-element.32), channel_id=1, source_target_pairs={{4,8},{8,4},{12,0},{0,12},{5,9},{9,5},{13,1},{1,13},{6,10},{10,6},... | collective-permute-start | bytes 442376 | tf_op jit(solution)/shard_map/ppermute | solution.py:344
  15.5 7.2 %collective-permute-start.10 = (bf16[9,64,128]{2,1,0:T(8,128)(2,1)S(1)}, bf16[9,64,128]{2,1,0:T(8,128)(2,1)S(1)}, u32[]{:S(2)}, u32[]{:S(2)}) collective-permute-start(bf16[9,64,128]{2,1,0:T(8,128)(2,1)S(1)} %get-tuple-element.33), channel_id=1, source_target_pairs={{0,8},{4,12},{8,0},{12,4},{1,9},{5,13},{9,1},{13,5},{2,10},{6,14},... | collective-permute-start | bytes 442376 | tf_op jit(solution)/shard_map/ppermute | solution.py:344
  16.8 18.3 %collective-permute-start = (bf16[4,64,1024]{2,1,0:T(8,128)(2,1)S(1)}, bf16[4,64,1024]{2,1,0:T(8,128)(2,1)S(1)}, u32[]{:S(2)}, u32[]{:S(2)}) collective-permute-start(bf16[4,64,1024]{2,1,0:T(8,128)(2,1)S(1)} %get-tuple-element.29.c0.x0), channel_id=1, source_target_pairs={{0,1},{1,0},{2,3},{3,2},{4,5},{5,4},{6,7},{7,6},{8,9},{9,8},{10,11... | collective-permute-start | bytes 1572872 | tf_op jit(solution)/shard_map/ppermute | solution.py:323
  19.2 17.3 %collective-permute-start.18 = (bf16[4,64,1024]{2,1,0:T(8,128)(2,1)S(1)}, bf16[4,64,1024]{2,1,0:T(8,128)(2,1)S(1)}, u32[]{:S(2)}, u32[]{:S(2)}) collective-permute-start(bf16[4,64,1024]{2,1,0:T(8,128)(2,1)S(1)} %get-tuple-element.42.c0.g0), channel_id=1, source_target_pairs={{0,8},{4,12},{8,0},{12,4},{1,9},{5,13},{9,1},{13,5},{2,10},{6,14},... | collective-permute-start | bytes 1572872 | tf_op jit(solution)/shard_map/ppermute | solution.py:323
  22.7 21.1 %collective-permute-start.17 = (bf16[4,64,1024]{2,1,0:T(8,128)(2,1)S(1)}, bf16[4,64,1024]{2,1,0:T(8,128)(2,1)S(1)}, u32[]{:S(2)}, u32[]{:S(2)}) collective-permute-start(bf16[4,64,1024]{2,1,0:T(8,128)(2,1)S(1)} %get-tuple-element.42.c0.g0), channel_id=1, source_target_pairs={{4,8},{8,4},{12,0},{0,12},{5,9},{9,5},{13,1},{1,13},{6,10},{10,6},... | collective-permute-start | bytes 1572872 | tf_op jit(solution)/shard_map/ppermute | solution.py:323
  23.4 20.5 %collective-permute-start.16 = (bf16[4,64,1024]{2,1,0:T(8,128)(2,1)S(1)}, bf16[4,64,1024]{2,1,0:T(8,128)(2,1)S(1)}, u32[]{:S(2)}, u32[]{:S(2)}) collective-permute-start(bf16[4,64,1024]{2,1,0:T(8,128)(2,1)S(1)} %get-tuple-element.42.c0.g0), channel_id=1, source_target_pairs={{0,4},{4,0},{8,12},{12,8},{1,5},{5,1},{9,13},{13,9},{2,6},{6,2},{1... | collective-permute-start | bytes 1572872 | tf_op jit(solution)/shard_map/ppermute | solution.py:323
  34.5 17.1 %collective-permute-start.11 = (bf16[4,9,64,128]{3,2,1,0:T(8,128)(2,1)S(1)}, bf16[4,9,64,128]{3,2,1,0:T(8,128)(2,1)S(1)}, u32[]{:S(2)}, u32[]{:S(2)}) collective-permute-start(bf16[4,9,64,128]{3,2,1,0:T(8,128)(2,1)S(1)} %pad_maximum_fusion.mine), channel_id=1, source_target_pairs={{0,16},{16,0},{1,17},{17,1},{2,18},{18,2},{3,19},{19,3},{4,20},{20... | collective-permute-start | bytes 1769480 | tf_op jit(solution)/shard_map/ppermute | solution.py:346
  35.1 18.0 %collective-permute-start.3 = (bf16[4,4,64,128]{3,2,1,0:T(8,128)(2,1)S(1)}, bf16[4,4,64,128]{3,2,1,0:T(8,128)(2,1)S(1)}, u32[]{:S(2)}, u32[]{:S(2)}) collective-permute-start(bf16[4,4,64,128]{3,2,1,0:T(8,128)(2,1)S(1)} %pad_maximum_fusion.1), channel_id=1, source_target_pairs={{0,16},{16,32},{32,48},{48,64},{64,80},{80,96},{96,112},{1,17},{17... | collective-permute-start | bytes 786440 | tf_op jit(solution)/shard_map/ppermute | solution.py:332
  36.5 16.7 %collective-permute-start.4 = (bf16[4,4,64,128]{3,2,1,0:T(8,128)(2,1)S(1)}, bf16[4,4,64,128]{3,2,1,0:T(8,128)(2,1)S(1)}, u32[]{:S(2)}, u32[]{:S(2)}) collective-permute-start(bf16[4,4,64,128]{3,2,1,0:T(8,128)(2,1)S(1)} %pad_maximum_fusion.2), channel_id=1, source_target_pairs={{16,0},{32,16},{48,32},{64,48},{80,64},{96,80},{112,96},{17,1},{33... | collective-permute-start | bytes 786440 | tf_op jit(solution)/shard_map/ppermute | solution.py:332
  43.9 18.1 %collective-permute-start.19 = (bf16[4,4,64,128]{3,2,1,0:T(8,128)(2,1)S(1)}, bf16[4,4,64,128]{3,2,1,0:T(8,128)(2,1)S(1)}, u32[]{:S(2)}, u32[]{:S(2)}) collective-permute-start(bf16[4,4,64,128]{3,2,1,0:T(8,128)(2,1)S(1)} %pad_maximum_fusion.3), channel_id=1, source_target_pairs={{0,16},{16,32},{32,48},{48,64},{64,80},{80,96},{96,112},{1,17},{17... | collective-permute-start | bytes 786440 | tf_op jit(solution)/shard_map/ppermute | solution.py:332
  45.3 16.8 %collective-permute-start.20 = (bf16[4,4,64,128]{3,2,1,0:T(8,128)(2,1)S(1)}, bf16[4,4,64,128]{3,2,1,0:T(8,128)(2,1)S(1)}, u32[]{:S(2)}, u32[]{:S(2)}) collective-permute-start(bf16[4,4,64,128]{3,2,1,0:T(8,128)(2,1)S(1)} %pad_maximum_fusion.4), channel_id=1, source_target_pairs={{16,0},{32,16},{48,32},{64,48},{80,64},{96,80},{112,96},{17,1},{33... | collective-permute-start | bytes 786440 | tf_op jit(solution)/shard_map/ppermute | solution.py:332
  60.3 24.9 %collective-permute-start.12 = (f32[2,4,64,512]{3,2,1,0:T(8,128)S(1)}, f32[2,4,64,512]{3,2,1,0:T(8,128)S(1)}, u32[]{:S(2)}, u32[]{:S(2)}) collective-permute-start(f32[2,4,64,512]{3,2,1,0:T(8,128)S(1)} %get-tuple-element.36), channel_id=1, source_target_pairs={{0,4},{4,0},{8,12},{12,8},{1,5},{5,1},{9,13},{13,9},{2,6},{6,2},{1... | collective-permute-start | bytes 3145736 | tf_op jit(solution)/shard_map/ppermute | solution.py:360
  60.4 25.5 %collective-permute-start.14 = (f32[2,4,64,512]{3,2,1,0:T(8,128)S(1)}, f32[2,4,64,512]{3,2,1,0:T(8,128)S(1)}, u32[]{:S(2)}, u32[]{:S(2)}) collective-permute-start(f32[2,4,64,512]{3,2,1,0:T(8,128)S(1)} %get-tuple-element.39), channel_id=1, source_target_pairs={{4,8},{8,4},{12,0},{0,12},{5,9},{9,5},{13,1},{1,13},{6,10},{10,6},... | collective-permute-start | bytes 3145736 | tf_op jit(solution)/shard_map/ppermute | solution.py:361
  78.2 7.8 %collective-permute-start.25 = (f32[4,9,64,128]{3,2,1,0:T(8,128)S(1)}, f32[4,9,64,128]{3,2,1,0:T(8,128)S(1)}, u32[]{:S(2)}, u32[]{:S(2)}) collective-permute-start(f32[4,9,64,128]{3,2,1,0:T(8,128)S(1)} %get-tuple-element.52), channel_id=1, source_target_pairs={{0,16},{16,0},{1,17},{17,1},{2,18},{18,2},{3,19},{19,3},{4,20},{20... | collective-permute-start | bytes 3538952 | tf_op jit(solution)/shard_map/ppermute | solution.py:368
  80.3 26.6 %collective-permute-start.21 = (f32[2,4,64,512]{3,2,1,0:T(8,128)S(1)}, f32[2,4,64,512]{3,2,1,0:T(8,128)S(1)}, u32[]{:S(2)}, u32[]{:S(2)}) collective-permute-start(f32[2,4,64,512]{3,2,1,0:T(8,128)S(1)} %get-tuple-element.45), channel_id=1, source_target_pairs={{0,1},{1,0},{2,3},{3,2},{4,5},{5,4},{6,7},{7,6},{8,9},{9,8},{10,11... | collective-permute-start | bytes 3145736 | tf_op jit(solution)/shard_map/ppermute | solution.py:364
  83.4 25.6 %collective-permute-start.23 = (f32[2,4,64,512]{3,2,1,0:T(8,128)S(1)}, f32[2,4,64,512]{3,2,1,0:T(8,128)S(1)}, u32[]{:S(2)}, u32[]{:S(2)}) collective-permute-start(f32[2,4,64,512]{3,2,1,0:T(8,128)S(1)} %get-tuple-element.48), channel_id=1, source_target_pairs={{1,2},{2,1},{3,0},{0,3},{5,6},{6,5},{7,4},{4,7},{9,10},{10,9},{11,... | collective-permute-start | bytes 3145736 | tf_op jit(solution)/shard_map/ppermute | solution.py:365
  85.2 32.7 %collective-permute-start.13 = (f32[4,64,512]{2,1,0:T(8,128)S(1)}, f32[4,64,512]{2,1,0:T(8,128)S(1)}, u32[]{:S(2)}, u32[]{:S(2)}) collective-permute-start(f32[4,64,512]{2,1,0:T(8,128)S(1)} %fusion.3), channel_id=1, source_target_pairs={{4,8},{8,4},{12,0},{0,12},{5,9},{9,5},{13,1},{1,13},{6,10},{10,6},... | collective-permute-start | bytes 1572872 | tf_op jit(solution)/shard_map/ppermute | solution.py:336
  86.2 23.6 %collective-permute-start.26 = (f32[9,64,128]{2,1,0:T(8,128)S(1)}, f32[9,64,128]{2,1,0:T(8,128)S(1)}, u32[]{:S(2)}, u32[]{:S(2)}) collective-permute-start(f32[9,64,128]{2,1,0:T(8,128)S(1)} %get-tuple-element.55), channel_id=1, source_target_pairs={{0,32},{32,64},{64,96},{96,0},{1,33},{33,65},{65,97},{97,1},{2,34}... | collective-permute-start | bytes 884744 | tf_op jit(solution)/shard_map/ppermute | solution.py:373
  87.3 24.4 %collective-permute-start.28 = (f32[9,64,128]{2,1,0:T(8,128)S(1)}, f32[9,64,128]{2,1,0:T(8,128)S(1)}, u32[]{:S(2)}, u32[]{:S(2)}) collective-permute-start(f32[9,64,128]{2,1,0:T(8,128)S(1)} %get-tuple-element.56), channel_id=1, source_target_pairs={{0,64},{32,96},{64,0},{96,32},{1,65},{33,97},{65,1},{97,33},{2,66}... | collective-permute-start | bytes 884744 | tf_op jit(solution)/shard_map/ppermute | solution.py:373
  106.8 9.1 %collective-permute-start.27 = (f32[9,64,128]{2,1,0:T(8,128)S(1)}, f32[9,64,128]{2,1,0:T(8,128)S(1)}, u32[]{:S(2)}, u32[]{:S(2)}) collective-permute-start(f32[9,64,128]{2,1,0:T(8,128)S(1)} %get-tuple-element.57), channel_id=1, source_target_pairs={{0,96},{32,0},{64,32},{96,64},{1,97},{33,1},{65,33},{97,65},{2,98}... | collective-permute-start | bytes 884744 | tf_op jit(solution)/shard_map/ppermute | solution.py:373
  109.0 12.3 %collective-permute-start.15 = (f32[4,64,512]{2,1,0:T(8,128)S(1)}, f32[4,64,512]{2,1,0:T(8,128)S(1)}, u32[]{:S(2)}, u32[]{:S(2)}) collective-permute-start(f32[4,64,512]{2,1,0:T(8,128)S(1)} %fusion.2), channel_id=1, source_target_pairs={{0,4},{4,0},{8,12},{12,8},{1,5},{5,1},{9,13},{13,9},{2,6},{6,2},{1... | collective-permute-start | bytes 1572872 | tf_op jit(solution)/shard_map/ppermute | solution.py:337
  109.9 13.5 %collective-permute-start.22 = (f32[4,64,512]{2,1,0:T(8,128)S(1)}, f32[4,64,512]{2,1,0:T(8,128)S(1)}, u32[]{:S(2)}, u32[]{:S(2)}) collective-permute-start(f32[4,64,512]{2,1,0:T(8,128)S(1)} %fusion.1), channel_id=1, source_target_pairs={{1,2},{2,1},{3,0},{0,3},{5,6},{6,5},{7,4},{4,7},{9,10},{10,9},{11,... | collective-permute-start | bytes 1572872 | tf_op jit(solution)/shard_map/ppermute | solution.py:336
  111.7 11.7 %collective-permute-start.24 = (f32[4,64,512]{2,1,0:T(8,128)S(1)}, f32[4,64,512]{2,1,0:T(8,128)S(1)}, u32[]{:S(2)}, u32[]{:S(2)}) collective-permute-start(f32[4,64,512]{2,1,0:T(8,128)S(1)} %fusion), channel_id=1, source_target_pairs={{0,1},{1,0},{2,3},{3,2},{4,5},{5,4},{6,7},{7,6},{8,9},{9,8},{10,11... | collective-permute-start | bytes 1572872 | tf_op jit(solution)/shard_map/ppermute | solution.py:337
  116.0 19.8 %collective-permute-start.29 = (f32[9,64,128]{2,1,0:T(8,128)S(1)}, f32[9,64,128]{2,1,0:T(8,128)S(1)}, u32[]{:S(2)}, u32[]{:S(2)}) collective-permute-start(f32[9,64,128]{2,1,0:T(8,128)S(1)} %fusion.6), channel_id=1, source_target_pairs={{0,0},{4,32},{8,64},{12,96},{32,4},{36,36},{40,68},{44,100},{64,8}... | collective-permute-start | bytes 884744 | tf_op jit(solution)/shard_map/ppermute | solution.py:375

commit v5 on v4

--- a/solution.py
+++ b/solution.py
@@ -186,7 +186,7 @@
     )(at, mine, other)
 
 
-def lay_shifted(chunks, top, bottom, rows, shifted):
+def lay_shifted(q, chunks, top, bottom, rows, shifted):
     column = lane_of((64, LANES)) % W
     not_first = jnp.where(column == 0, 0.0, 1.0).astype(BF16)
     not_last = jnp.where(column == W - 1, 0.0, 1.0).astype(BF16)
@@ -194,11 +194,11 @@
         at = k * 64
         for j, h in enumerate(rows):
             if h == -1:
-                tile = top[k, 0]
+                tile = top[k, q]
             elif h == 8:
-                tile = bottom[k, 0]
+                tile = bottom[k, q]
             else:
-                tile = chunks[k][0, :, h * LANES : (h + 1) * LANES]
+                tile = chunks[k][q, :, h * LANES : (h + 1) * LANES]
             lanes = slice(j * LANES, (j + 1) * LANES)
             shifted[at : at + 64, lanes] = pltpu.roll(tile, 1, 1) * not_first
             shifted[256 + at : 320 + at, lanes] = tile
@@ -209,45 +209,48 @@
     edged = 1 in halves
     top, bottom = refs[:2] if edged else (None, None)
     refs = refs[2 * edged :]
-    w_ref, shifted = refs[0], refs[-1]
-    lay_shifted((c0, c1, c2, c3), top, bottom, rows, shifted)
-    for i, half in enumerate(halves):
-        own, following, send = refs[1 + 3 * i : 4 + 3 * i]
-        for n in range(2):
-            part = None
-            for a in range(3):
-                places = [rows.index(h - 1 + a) for h in ROWS[half][2 * n : 2 * n + 2]]
-                source = jnp.concatenate([shifted[:, j * LANES : (j + 1) * LANES] for j in places], axis=1)
-                term = jnp.dot(w_ref[a], source, preferred_element_type=F32)
-                part = term if part is None else part + term
-            lanes = slice(n * 256, (n + 1) * 256)
-            own[0, :, lanes] = part[0:64]
-            pair = (following.at[0], send.at[0, 0]) if half else (send.at[0, 0], following.at[0])
-            pair[0][:, lanes] = part[64:128]
-            pair[1][:, lanes] = part[128:192]
-            send[1, 0, :, lanes] = part[192:256]
+    w_ref, both = refs[0], refs[-1]
+
+    def lay(q, shifted):
+        lay_shifted(q, (c0, c1, c2, c3), top, bottom, rows, shifted)
+
+    def multiply(q, shifted):
+        for i, half in enumerate(halves):
+            own, following, send = refs[1 + 3 * i : 4 + 3 * i]
+            for n in range(2):
+                part = None
+                for a in range(3):
+                    places = [rows.index(h - 1 + a) for h in ROWS[half][2 * n : 2 * n + 2]]
+                    source = jnp.concatenate([shifted[:, j * LANES : (j + 1) * LANES] for j in places], axis=1)
+                    term = jnp.dot(w_ref[a], source, preferred_element_type=F32)
+                    part = term if part is None else part + term
+                lanes = slice(n * 256, (n + 1) * 256)
+                own[q, :, lanes] = part[0:64]
+                pair = (following.at[q], send.at[0, q]) if half else (send.at[0, q], following.at[q])
+                pair[0][:, lanes] = part[64:128]
+                pair[1][:, lanes] = part[128:192]
+                send[1, q, :, lanes] = part[192:256]
+
+    lay(0, both.at[0])
+    for q in range(4):
+        if q < 3:
+            lay(q + 1, both.at[(q + 1) % 2])
+        multiply(q, both.at[q % 2])
 
 
 def conv(halves, at, chunks, sides, weights):
     rows = {(0,): (0, 1, 2, 3, 4, 5), (1,): (4, 5, 6, 7, 8, -1, 0, 1)}.get(halves, tuple(range(-1, 9)))
     single = jax.ShapeDtypeStruct((4, 64, 512), F32)
     double = jax.ShapeDtypeStruct((2, 4, 64, 512), F32)
-    chunk = pl.BlockSpec((1, 64, 1024), lambda q: (q, 0, 0))
-    edge = pl.BlockSpec((4, 1, 64, LANES), lambda q: (0, q, 0, 0))
-    one = pl.BlockSpec((1, 64, 512), lambda q: (q, 0, 0))
-    two = pl.BlockSpec((2, 1, 64, 512), lambda q: (0, q, 0, 0))
+    near = pl.BlockSpec(memory_space=pltpu.VMEM)
     sides = sides if 1 in halves else ()
     return pl.pallas_call(
         functools.partial(conv_kernel, halves, rows),
         out_shape=(single, single, double) * len(halves),
-        grid=(4,),
-        in_specs=[pl.BlockSpec(memory_space=pltpu.SMEM)]
-        + [chunk] * 4
-        + [edge] * len(sides)
-        + [pl.BlockSpec((3, 256, 768), lambda q: (0, 0, 0))],
-        out_specs=[one, one, two] * len(halves),
-        scratch_shapes=[pltpu.VMEM((768, len(rows) * LANES), BF16)],
-        compiler_params=params(16),
+        in_specs=[pl.BlockSpec(memory_space=pltpu.SMEM)] + [near] * (5 + len(sides)),
+        out_specs=[near] * (3 * len(halves)),
+        scratch_shapes=[pltpu.VMEM((2, 768, len(rows) * LANES), BF16)],
+        compiler_params=params(20),
         cost_estimate=pl.CostEstimate(
             flops=2415919104 * len(halves), bytes_accessed=6000000 * len(halves), transcendentals=0
         ),
@@ -256,54 +259,48 @@
 
 def kernel_grad_kernel(at, x0, x1, x2, x3, top, bottom, g0, g1, g2, g3, mine, other, shifted, grads, total):
     z, core, x, y = at[0], at[1], at[2], at[3]
-    q = pl.program_id(0)
-    lay_shifted((x0, x1, x2, x3), top, bottom, range(-1, 9), shifted)
-    for k, g_ref in enumerate((g0, g1, g2, g3)):
-        grads[k * 64 : (k + 1) * 64, :] = g_ref[0]
-
-    @pl.when(q == 0)
-    def _():
-        total[...] = jnp.zeros_like(total)
-
-    for a in range(3):
-        total[a] += lax.dot_general(
-            grads[...],
-            shifted[:, a * LANES : a * LANES + 1024],
-            (((1,), (1,)), ((), ())),
-            preferred_element_type=F32,
-        )
-
-    @pl.when(q == 3)
-    def _():
-        for half, o_ref in ((core, mine), (1 - core, other)):
-            second = jnp.where(half == y // 2, 0, 1)
-            straight = second == lax.rem(y, 2)
-            for k in range(4):
-                member = lax.rem(z + (0, 1, 3, 2)[k], 4)
-                rows = pl.ds(pl.multiple_of(place_of(member, x) * 64, 64), 64)
-                for a in range(3):
-                    for c in range(3):
-                        lanes = pl.ds(pl.multiple_of(c * 256 + second * LANES, LANES), LANES)
-                        tile = total[a, rows, lanes]
-                        o_ref[k, a * 3 + c] = jnp.where(straight, tile, pltpu.roll(tile, W, 1))
+
+    def add(q, first):
+        lay_shifted(q, (x0, x1, x2, x3), top, bottom, range(-1, 9), shifted)
+        for k, g_ref in enumerate((g0, g1, g2, g3)):
+            grads[k * 64 : (k + 1) * 64, :] = g_ref[q]
+        for a in range(3):
+            term = lax.dot_general(
+                grads[...],
+                shifted[:, a * LANES : a * LANES + 1024],
+                (((1,), (1,)), ((), ())),
+                preferred_element_type=F32,
+            )
+            total[a] = term if first else total[a] + term
+
+    add(0, True)
+
+    @pl.loop(1, 4)
+    def _(q):
+        add(q, False)
+
+    for half, o_ref in ((core, mine), (1 - core, other)):
+        second = jnp.where(half == y // 2, 0, 1)
+        straight = second == lax.rem(y, 2)
+        for k in range(4):
+            member = lax.rem(z + (0, 1, 3, 2)[k], 4)
+            rows = pl.ds(pl.multiple_of(place_of(member, x) * 64, 64), 64)
+            for a in range(3):
+                for c in range(3):
+                    lanes = pl.ds(pl.multiple_of(c * 256 + second * LANES, LANES), LANES)
+                    tile = total[a, rows, lanes]
+                    o_ref[k, a * 3 + c] = jnp.where(straight, tile, pltpu.roll(tile, W, 1))
 
 
 def weight_grads(at, chunks, top, bottom, grads):
     shape = jax.ShapeDtypeStruct((4, 9, 64, LANES), F32)
-    chunk = pl.BlockSpec((1, 64, 1024), lambda q: (q, 0, 0))
-    edge = pl.BlockSpec((4, 1, 64, LANES), lambda q: (0, q, 0, 0))
-    whole = pl.BlockSpec((4, 9, 64, LANES), lambda q: (0, 0, 0, 0))
+    near = pl.BlockSpec(memory_space=pltpu.VMEM)
     return pl.pallas_call(
         kernel_grad_kernel,
         out_shape=(shape,) * 2,
-        grid=(4,),
-        in_specs=[pl.BlockSpec(memory_space=pltpu.SMEM)] + [chunk] * 4 + [edge] * 2 + [chunk] * 4,
-        out_specs=[whole] * 2,
-        scratch_shapes=[
-            pltpu.VMEM((768, 1280), BF16),
-            pltpu.VMEM((256, 1024), BF16),
-            pltpu.VMEM((3, 256, 768), F32),
-        ],
+        in_specs=[pl.BlockSpec(memory_space=pltpu.SMEM)] + [near] * 10,
+        out_specs=[near] * 2,
+        scratch_shapes=[pltpu.VMEM((768, 1280), BF16), pltpu.VMEM((256, 1024), BF16), pltpu.VMEM((3, 256, 768), F32)],
         compiler_params=params(20),
         cost_estimate=pl.CostEstimate(flops=4831838208, bytes_accessed=9000000, transcendentals=0),
         name="weight_grads",
@@ -359,9 +356,9 @@
     out_a, out_b = out[:3], out[3:]
     out_one_a = lax.ppermute(out_a[2], "x", FIRST)
     out_one_b = lax.ppermute(out_b[2], "x", SECOND)
-    grad = conv((0, 1), after(at, out_a[0]), g_chunks, g_sides, turned)
-    grad_a, grad_b = grad[:3], grad[3:]
+    grad_a = conv((0,), after(at, out_a[0]), g_chunks, g_sides, turned)
     grad_one_a = lax.ppermute(grad_a[2], "y", FIRST)
+    grad_b = conv((1,), after(at, grad_a[0]), g_chunks, g_sides, turned)
     grad_one_b = lax.ppermute(grad_b[2], "y", SECOND)
 
     near, far = weight_grads(after(at, grad_b[0]), x_chunks, *x_sides, g_chunks)

time: 138 us -> 136 us (0.986)
  the two profiles are of different devices: /device:TPU:97 before, /device:TPU:104 now
where the time goes in v5:
time: 136 us; the launch traced here: 135 us
  waiting for transfers between devices  61.7 us (45%)
  starting transfers between devices  39.9 us (29%)
  Pallas kernels  29.3 us (22%)
  local copies, waits for them, and re-layouts  2.36 us (2%)
    ppermute x1, waiting for transfers between devices, step(): grad_one_b = lax.ppermute(grad_b[2], 'y', SECOND)  14.8 us
    ppermute x3, waiting for transfers between devices, gather(): lax.ppermute(block, axis, SECOND)  12.9 us
    pallas_call x3, Pallas kernels, conv(): pl.pallas_call(functools.partial(conv_kernel, halves, rows), out_shape=(s...  12.7 us
    ppermute x1, waiting for transfers between devices, step(): home = lax.ppermute(total, ('z', 'x'), cross)  10.4 us
    pallas_call x1, Pallas kernels, weight_grads(): pl.pallas_call(kernel_grad_kernel, out_shape=(shape,) * 2, in_specs=[pl.B...  7.66 us
    ppermute x2, starting transfers between devices, edges(): lax.ppermute(first, ('z', 'core'), backward)  5.73 us
    ppermute x3, waiting for transfers between devices, step(): total = total + lax.ppermute(near[k], 'z', ring(turn))  5.21 us
    ppermute x1, waiting for transfers between devices, step(): out_one_a = lax.ppermute(out_a[2], 'x', FIRST)  4.98 us
  transfers between devices with their start and end apart: 30, of which 13 were waited for; matrix products, arithmetic and copies ran while one was open for 1% of the time, Pallas kernels for 20%

profile of v5, /device:TPU:104, one launch (start us, length us, event | category | flops | bytes accessed | tf_op | source)
XLA Modules:
  0.0 135.3 jit_solution(3556905398833980918)
XLA Ops:
  0.6 0.6 collective-permute-start.7
  1.3 2.5 %collective-permute-start.6 = (bf16[9,64,128]{2,1,0:T(8,128)(2,1)}, bf16[9,64,128]{2,1,0:T(8,128)(2,1)S(1)}, u32[]{:S(2)}, u32[]{:S(2)}) collective-permute-start(bf16[9,64,128]{2,1,0:T(8,128)(2,1)} %bitcast.74), channel_id=1, source_target_pairs={{32,64},{64,32},{96,0},{0,96},{33,65},{65,33},{97,1},{1,97},{34,66... | collective-permute-start | bytes 442376 | tf_op jit(solution)/shard_map/ppermute | solution.py:320
  3.8 0.4 collective-permute-start.5
  4.2 1.0 copy-done
  5.2 1.0 copy-done.1
  6.3 2.4 %pack.1 = (bf16[4,64,1024]{2,1,0:T(8,128)(2,1)S(1)}, bf16[4,64,1024]{2,1,0:T(8,128)(2,1)S(1)}) custom-call(bf16[8,8,4096]{2,1,0:T(8,128)(2,1)S(1)} %copy-done, bf16[8,8,4096]{2,1,0:T(8,128)(2,1)S(1)} %copy-done.1), custom_call_target="tpu_custom_call" | custom-call | tf_op jit(solution)/shard_map/pack/pallas_call | solution.py:61
  8.7 2.4 %collective-permute-start.2 = (bf16[4,64,1024]{2,1,0:T(8,128)(2,1)S(1)}, bf16[4,64,1024]{2,1,0:T(8,128)(2,1)S(1)}, u32[]{:S(2)}, u32[]{:S(2)}) collective-permute-start(bf16[4,64,1024]{2,1,0:T(8,128)(2,1)S(1)} %get-tuple-element.30.c0.x0), channel_id=1, source_target_pairs={{0,2},{1,3},{2,0},{3,1},{4,6},{5,7},{6,4},{7,5},{8,10},{9,11},{10,... | collective-permute-start | bytes 1572872 | tf_op jit(solution)/shard_map/ppermute | solution.py:320
  11.2 0.6 route.1
  11.8 1.6 %collective-permute-start.8 = (bf16[9,64,128]{2,1,0:T(8,128)(2,1)S(1)}, bf16[9,64,128]{2,1,0:T(8,128)(2,1)S(1)}, u32[]{:S(2)}, u32[]{:S(2)}) collective-permute-start(bf16[9,64,128]{2,1,0:T(8,128)(2,1)S(1)} %get-tuple-element.32), channel_id=1, source_target_pairs={{0,4},{4,0},{8,12},{12,8},{1,5},{5,1},{9,13},{13,9},{2,6},{6,2},{1... | collective-permute-start | bytes 442376 | tf_op jit(solution)/shard_map/ppermute | solution.py:341
  13.4 2.1 %collective-permute-start.9 = (bf16[9,64,128]{2,1,0:T(8,128)(2,1)S(1)}, bf16[9,64,128]{2,1,0:T(8,128)(2,1)S(1)}, u32[]{:S(2)}, u32[]{:S(2)}) collective-permute-start(bf16[9,64,128]{2,1,0:T(8,128)(2,1)S(1)} %get-tuple-element.33), channel_id=1, source_target_pairs={{4,8},{8,4},{12,0},{0,12},{5,9},{9,5},{13,1},{1,13},{6,10},{10,6},... | collective-permute-start | bytes 442376 | tf_op jit(solution)/shard_map/ppermute | solution.py:341
  15.5 0.6 collective-permute-start.10
  16.2 1.6 %collective-permute-done.8 = bf16[9,64,128]{2,1,0:T(8,128)(2,1)S(1)} collective-permute-done((bf16[9,64,128]{2,1,0:T(8,128)(2,1)S(1)}, bf16[9,64,128]{2,1,0:T(8,128)(2,1)S(1)}, u32[]{:S(2)}, u32[]{:S(2)}) %collective-permute-start.8) | collective-permute-done | bytes 147488 | tf_op jit(solution)/shard_map/ppermute | solution.py:341
  17.8 2.8 %collective-permute-start = (bf16[4,64,1024]{2,1,0:T(8,128)(2,1)S(1)}, bf16[4,64,1024]{2,1,0:T(8,128)(2,1)S(1)}, u32[]{:S(2)}, u32[]{:S(2)}) collective-permute-start(bf16[4,64,1024]{2,1,0:T(8,128)(2,1)S(1)} %get-tuple-element.30.c0.x0), channel_id=1, source_target_pairs={{0,1},{1,0},{2,3},{3,2},{4,5},{5,4},{6,7},{7,6},{8,9},{9,8},{10,11... | collective-permute-start | bytes 1572872 | tf_op jit(solution)/shard_map/ppermute | solution.py:320
  20.6 2.6 %collective-permute-done.9 = bf16[9,64,128]{2,1,0:T(8,128)(2,1)S(1)} collective-permute-done((bf16[9,64,128]{2,1,0:T(8,128)(2,1)S(1)}, bf16[9,64,128]{2,1,0:T(8,128)(2,1)S(1)}, u32[]{:S(2)}, u32[]{:S(2)}) %collective-permute-start.9) | collective-permute-done | bytes 147488 | tf_op jit(solution)/shard_map/ppermute | solution.py:341
  23.2 1.5 %collective-permute-start.18 = (bf16[4,64,1024]{2,1,0:T(8,128)(2,1)S(1)}, bf16[4,64,1024]{2,1,0:T(8,128)(2,1)S(1)}, u32[]{:S(2)}, u32[]{:S(2)}) collective-permute-start(bf16[4,64,1024]{2,1,0:T(8,128)(2,1)S(1)} %get-tuple-element.43.c0.g0), channel_id=1, source_target_pairs={{0,8},{4,12},{8,0},{12,4},{1,9},{5,13},{9,1},{13,5},{2,10},{6,14},... | collective-permute-start | bytes 1572872 | tf_op jit(solution)/shard_map/ppermute | solution.py:320
  24.7 0.6 collective-permute-start.17
  25.4 1.5 %collective-permute-start.16 = (bf16[4,64,1024]{2,1,0:T(8,128)(2,1)S(1)}, bf16[4,64,1024]{2,1,0:T(8,128)(2,1)S(1)}, u32[]{:S(2)}, u32[]{:S(2)}) collective-permute-start(bf16[4,64,1024]{2,1,0:T(8,128)(2,1)S(1)} %get-tuple-element.43.c0.g0), channel_id=1, source_target_pairs={{0,4},{4,0},{8,12},{12,8},{1,5},{5,1},{9,13},{13,9},{2,6},{6,2},{1... | collective-permute-start | bytes 1572872 | tf_op jit(solution)/shard_map/ppermute | solution.py:320
  26.9 7.5 %collective-permute-done.1.c2.x2 = bf16[4,64,1024]{2,1,0:T(8,128)(2,1)S(1)} collective-permute-done((bf16[4,64,1024]{2,1,0:T(8,128)(2,1)S(1)}, bf16[4,64,1024]{2,1,0:T(8,128)(2,1)S(1)}, u32[]{:S(2)}, u32[]{:S(2)}) %collective-permute-start.1) | collective-permute-done | bytes 524320 | tf_op jit(solution)/shard_map/ppermute | solution.py:320
  34.6 2.3 %collective-permute-start.3 = (bf16[4,4,64,128]{3,2,1,0:T(8,128)(2,1)S(1)}, bf16[4,4,64,128]{3,2,1,0:T(8,128)(2,1)S(1)}, u32[]{:S(2)}, u32[]{:S(2)}) collective-permute-start(bf16[4,4,64,128]{3,2,1,0:T(8,128)(2,1)S(1)} %pad_maximum_fusion.1), channel_id=1, source_target_pairs={{0,16},{16,32},{32,48},{48,64},{64,80},{80,96},{96,112},{1,17},{17... | collective-permute-start | bytes 786440 | tf_op jit(solution)/shard_map/ppermute | solution.py:329
  36.9 2.6 %collective-permute-done.18.c3.g3 = bf16[4,64,1024]{2,1,0:T(8,128)(2,1)S(1)} collective-permute-done((bf16[4,64,1024]{2,1,0:T(8,128)(2,1)S(1)}, bf16[4,64,1024]{2,1,0:T(8,128)(2,1)S(1)}, u32[]{:S(2)}, u32[]{:S(2)}) %collective-permute-start.18) | collective-permute-done | bytes 524320 | tf_op jit(solution)/shard_map/ppermute | solution.py:320
  39.5 1.9 %collective-permute-start.4 = (bf16[4,4,64,128]{3,2,1,0:T(8,128)(2,1)S(1)}, bf16[4,4,64,128]{3,2,1,0:T(8,128)(2,1)S(1)}, u32[]{:S(2)}, u32[]{:S(2)}) collective-permute-start(bf16[4,4,64,128]{3,2,1,0:T(8,128)(2,1)S(1)} %pad_maximum_fusion.2), channel_id=1, source_target_pairs={{16,0},{32,16},{48,32},{64,48},{80,64},{96,80},{112,96},{17,1},{33... | collective-permute-start | bytes 786440 | tf_op jit(solution)/shard_map/ppermute | solution.py:329
  41.4 5.5 %collective-permute-done.17.c2.g2 = bf16[4,64,1024]{2,1,0:T(8,128)(2,1)S(1)} collective-permute-done((bf16[4,64,1024]{2,1,0:T(8,128)(2,1)S(1)}, bf16[4,64,1024]{2,1,0:T(8,128)(2,1)S(1)}, u32[]{:S(2)}, u32[]{:S(2)}) %collective-permute-start.17) | collective-permute-done | bytes 524320 | tf_op jit(solution)/shard_map/ppermute | solution.py:320
  46.9 1.2 collective-permute-done.16.c1.g1
  48.2 1.9 %collective-permute-start.21 = (bf16[4,4,64,128]{3,2,1,0:T(8,128)(2,1)S(1)}, bf16[4,4,64,128]{3,2,1,0:T(8,128)(2,1)S(1)}, u32[]{:S(2)}, u32[]{:S(2)}) collective-permute-start(bf16[4,4,64,128]{3,2,1,0:T(8,128)(2,1)S(1)} %pad_maximum_fusion.3), channel_id=1, source_target_pairs={{0,16},{16,32},{32,48},{48,64},{64,80},{80,96},{96,112},{1,17},{17... | collective-permute-start | bytes 786440 | tf_op jit(solution)/shard_map/ppermute | solution.py:329
  50.2 3.8 %collective-permute-start.22 = (bf16[4,4,64,128]{3,2,1,0:T(8,128)(2,1)S(1)}, bf16[4,4,64,128]{3,2,1,0:T(8,128)(2,1)S(1)}, u32[]{:S(2)}, u32[]{:S(2)}) collective-permute-start(bf16[4,4,64,128]{3,2,1,0:T(8,128)(2,1)S(1)} %pad_maximum_fusion.4), channel_id=1, source_target_pairs={{16,0},{32,16},{48,32},{64,48},{80,64},{96,80},{112,96},{17,1},{33... | collective-permute-start | bytes 786440 | tf_op jit(solution)/shard_map/ppermute | solution.py:329
  54.0 1.6 %weights.1 = (bf16[3,256,768]{2,1,0:T(8,128)(2,1)S(1)}, bf16[3,256,768]{2,1,0:T(8,128)(2,1)S(1)}) custom-call(s32[4]{0:T(128)S(1)} %pad_add_fusion.at, bf16[4,9,64,128]{3,2,1,0:T(8,128)(2,1)S(1)} %pad_maximum_fusion.mine, bf16[4,9,64,128]{3,2,1,0:T(8,128)(2,1)S(1)} %collective-permute-done.11.other), custom_call_target="tpu_custom_call" | custom-call | tf_op jit(solution)/shard_map/weights/pallas_call | solution.py:178
  55.6 5.8 %shard_map.58 = (f32[4,64,512]{2,1,0:T(8,128)S(1)}, f32[4,64,512]{2,1,0:T(8,128)S(1)}, f32[2,4,64,512]{3,2,1,0:T(8,128)S(1)}, f32[4,64,512]{2,1,0:T(8,128)S(1)},...) custom-call(s32[4]{0:T(128)S(1)} %pad_add_fusion.at, bf16[4,64,1024]{2,1,0:T(8,128)(2,1)S(1)} %get-tuple-element.30.c0.x0, ...), custom_call_target="tpu_custom_call" | custom-call | flops 4831838208 | bytes 12000000 | tf_op jit(solution)/shard_map/pallas_call | solution.py:247
  61.4 0.4 collective-permute-start.12
  61.8 2.4 %collective-permute-start.14 = (f32[2,4,64,512]{3,2,1,0:T(8,128)S(1)}, f32[2,4,64,512]{3,2,1,0:T(8,128)S(1)}, u32[]{:S(2)}, u32[]{:S(2)}) collective-permute-start(f32[2,4,64,512]{3,2,1,0:T(8,128)S(1)} %get-tuple-element.40), channel_id=1, source_target_pairs={{4,8},{8,4},{12,0},{0,12},{5,9},{9,5},{13,1},{1,13},{6,10},{10,6},... | collective-permute-start | bytes 3145736 | tf_op jit(solution)/shard_map/ppermute | solution.py:358
  64.2 3.4 %shard_map.59 = (f32[4,64,512]{2,1,0:T(8,128)S(1)}, f32[4,64,512]{2,1,0:T(8,128)S(1)}, f32[2,4,64,512]{3,2,1,0:T(8,128)S(1)}) custom-call(s32[4]{0:T(128)S(1)} %pad_add_fusion.at, bf16[4,64,1024]{2,1,0:T(8,128)(2,1)S(1)} %get-tuple-element.43.c0.g0, bf16[4,64,1024]{2,1,0:T(8,128)(2,1)S(1)} %collective-permute-done.16.c1.g1, ...), custom_call_target="tpu_custom_call" | custom-call | flops 2415919104 | bytes 6000000 | tf_op jit(solution)/shard_map/pallas_call | solution.py:247
  67.6 3.5 %shard_map.60 = (f32[4,64,512]{2,1,0:T(8,128)S(1)}, f32[4,64,512]{2,1,0:T(8,128)S(1)}, f32[2,4,64,512]{3,2,1,0:T(8,128)S(1)}) custom-call(s32[4]{0:T(128)S(1)} %pad_add_fusion.at, bf16[4,64,1024]{2,1,0:T(8,128)(2,1)S(1)} %get-tuple-element.43.c0.g0, bf16[4,64,1024]{2,1,0:T(8,128)(2,1)S(1)} %collective-permute-done.16.c1.g1, ...), custom_call_target="tpu_custom_call" | custom-call | flops 2415919104 | bytes 6000000 | tf_op jit(solution)/shard_map/pallas_call | solution.py:247
  71.1 7.7 %weight_grads.1 = (f32[4,9,64,128]{3,2,1,0:T(8,128)S(1)}, f32[4,9,64,128]{3,2,1,0:T(8,128)S(1)}) custom-call(s32[4]{0:T(128)S(1)} %pad_add_fusion.at, bf16[4,64,1024]{2,1,0:T(8,128)(2,1)S(1)} %get-tuple-element.30.c0.x0, bf16[4,64,1024]{2,1,0:T(8,128)(2,1)S(1)} %collective-permute-done.c1.x1, bf16[4,64,1024]{2,1,0:T(8,128)(2,1)S(1)} %collective-permute-done.1.c2.x2, ...), custom_call_target="tpu_custom_call" | custom-call | flops 4831838208 | bytes 9000000 | tf_op jit(solution)/shard_map/weight_grads/pallas_call | solution.py:298
  78.9 1.5 %collective-permute-start.23 = (f32[2,4,64,512]{3,2,1,0:T(8,128)S(1)}, f32[2,4,64,512]{3,2,1,0:T(8,128)S(1)}, u32[]{:S(2)}, u32[]{:S(2)}) collective-permute-start(f32[2,4,64,512]{3,2,1,0:T(8,128)S(1)} %get-tuple-element.50), channel_id=1, source_target_pairs={{1,2},{2,1},{3,0},{0,3},{5,6},{6,5},{7,4},{4,7},{9,10},{10,9},{11,... | collective-permute-start | bytes 3145736 | tf_op jit(solution)/shard_map/ppermute | solution.py:362
  80.4 5.0 %collective-permute-done.12.one_a = f32[2,4,64,512]{3,2,1,0:T(8,128)S(1)} collective-permute-done((f32[2,4,64,512]{3,2,1,0:T(8,128)S(1)}, f32[2,4,64,512]{3,2,1,0:T(8,128)S(1)}, u32[]{:S(2)}, u32[]{:S(2)}) %collective-permute-start.12) | collective-permute-done | bytes 1048608 | tf_op jit(solution)/shard_map/ppermute | solution.py:357
  85.5 2.5 %collective-permute-start.13 = (f32[4,64,512]{2,1,0:T(8,128)S(1)}, f32[4,64,512]{2,1,0:T(8,128)S(1)}, u32[]{:S(2)}, u32[]{:S(2)}) collective-permute-start(f32[4,64,512]{2,1,0:T(8,128)S(1)} %fusion.3), channel_id=1, source_target_pairs={{4,8},{8,4},{12,0},{0,12},{5,9},{9,5},{13,1},{1,13},{6,10},{10,6},... | collective-permute-start | bytes 1572872 | tf_op jit(solution)/shard_map/ppermute | solution.py:333
  88.0 0.2 add.28
  88.4 1.2 collective-permute-start.28
  89.6 14.8 %collective-permute-done.23.one_b = f32[2,4,64,512]{3,2,1,0:T(8,128)S(1)} collective-permute-done((f32[2,4,64,512]{3,2,1,0:T(8,128)S(1)}, f32[2,4,64,512]{3,2,1,0:T(8,128)S(1)}, u32[]{:S(2)}, u32[]{:S(2)}) %collective-permute-start.23) | collective-permute-done | bytes 1048608 | tf_op jit(solution)/shard_map/ppermute | solution.py:362
  104.6 1.0 collective-permute-done.19.one_a
  105.6 1.1 collective-permute-start.15
  106.8 0.6 collective-permute-start.24
  107.4 1.6 %collective-permute-start.20 = (f32[4,64,512]{2,1,0:T(8,128)S(1)}, f32[4,64,512]{2,1,0:T(8,128)S(1)}, u32[]{:S(2)}, u32[]{:S(2)}) collective-permute-start(f32[4,64,512]{2,1,0:T(8,128)S(1)} %fusion.1), channel_id=1, source_target_pairs={{1,2},{2,1},{3,0},{0,3},{5,6},{6,5},{7,4},{4,7},{9,10},{10,9},{11,... | collective-permute-start | bytes 1572872 | tf_op jit(solution)/shard_map/ppermute | solution.py:333
  109.0 5.2 %collective-permute-done.27 = f32[9,64,128]{2,1,0:T(8,128)S(1)} collective-permute-done((f32[9,64,128]{2,1,0:T(8,128)S(1)}, f32[9,64,128]{2,1,0:T(8,128)S(1)}, u32[]{:S(2)}, u32[]{:S(2)}) %collective-permute-start.27) | collective-permute-done | bytes 294944 | tf_op jit(solution)/shard_map/ppermute | solution.py:370
  114.2 1.9 %collective-permute-start.29 = (f32[9,64,128]{2,1,0:T(8,128)S(1)}, f32[9,64,128]{2,1,0:T(8,128)S(1)}, u32[]{:S(2)}, u32[]{:S(2)}) collective-permute-start(f32[9,64,128]{2,1,0:T(8,128)S(1)} %fusion.6), channel_id=1, source_target_pairs={{0,0},{4,32},{8,64},{12,96},{32,4},{36,36},{40,68},{44,100},{64,8}... | collective-permute-start | bytes 884744 | tf_op jit(solution)/shard_map/ppermute | solution.py:372
  116.2 4.2 %collective-permute-done.15.two_b = f32[4,64,512]{2,1,0:T(8,128)S(1)} collective-permute-done((f32[4,64,512]{2,1,0:T(8,128)S(1)}, f32[4,64,512]{2,1,0:T(8,128)S(1)}, u32[]{:S(2)}, u32[]{:S(2)}) %collective-permute-start.15) | collective-permute-done | bytes 524320 | tf_op jit(solution)/shard_map/ppermute | solution.py:334
  120.4 2.2 %finish.2 = bf16[8,8,4096]{2,1,0:T(8,128)(2,1)} custom-call(f32[4,64,512]{2,1,0:T(8,128)S(1)} %get-tuple-element.36.own_a, f32[2,4,64,512]{3,2,1,0:T(8,128)S(1)} %collective-permute-done.12.one_a, f32[4,64,512]{2,1,0:T(8,128)S(1)} %collective-permute-done.13.two_a, f32[4,64,512]{2,1,0:T(8,128)S(1)} %get-tuple-element.39.own_b, ...), custom_call_target="tpu_custom_call" | custom-call | tf_op jit(solution)/shard_map/finish/pallas_call | solution.py:113
  122.6 10.4 %collective-permute-done.29.refs_0_ = f32[9,64,128]{2,1,0:T(8,128)S(1)} collective-permute-done((f32[9,64,128]{2,1,0:T(8,128)S(1)}, f32[9,64,128]{2,1,0:T(8,128)S(1)}, u32[]{:S(2)}, u32[]{:S(2)}) %collective-permute-start.29) | collective-permute-done | bytes 294944 | tf_op jit(solution)/shard_map/ppermute | solution.py:372
  132.9 2.2 %finish.3 = (bf16[8,8,4096]{2,1,0:T(8,128)(2,1)}, f32[9,64,128]{2,1,0:T(8,128)}) custom-call(f32[4,64,512]{2,1,0:T(8,128)S(1)} %get-tuple-element.45.own_a, f32[2,4,64,512]{3,2,1,0:T(8,128)S(1)} %collective-permute-done.19.one_a, f32[4,64,512]{2,1,0:T(8,128)S(1)} %collective-permute-done.20.two_a, f32[4,64,512]{2,1,0:T(8,128)S(1)} %get-tuple-element.49.own_b, ...), custom_call_target="tpu_custom_call" | custom-call | tf_op jit(solution)/shard_map/finish/pallas_call | solution.py:113
  (48 shorter events, 1.3 us)
Async XLA Ops:
  0.6 10.6 %collective-permute-start.7 = (bf16[9,64,128]{2,1,0:T(8,128)(2,1)}, bf16[9,64,128]{2,1,0:T(8,128)(2,1)S(1)}, u32[]{:S(2)}, u32[]{:S(2)}) collective-permute-start(bf16[9,64,128]{2,1,0:T(8,128)(2,1)} %bitcast.73), channel_id=1, source_target_pairs={{0,64},{32,96},{64,0},{96,32},{1,65},{33,97},{65,1},{97,33},{2,66}... | collective-permute-start | bytes 442376 | tf_op jit(solution)/shard_map/ppermute | solution.py:320
  1.3 9.9 %collective-permute-start.6 = (bf16[9,64,128]{2,1,0:T(8,128)(2,1)}, bf16[9,64,128]{2,1,0:T(8,128)(2,1)S(1)}, u32[]{:S(2)}, u32[]{:S(2)}) collective-permute-start(bf16[9,64,128]{2,1,0:T(8,128)(2,1)} %bitcast.74), channel_id=1, source_target_pairs={{32,64},{64,32},{96,0},{0,96},{33,65},{65,33},{97,1},{1,97},{34,66... | collective-permute-start | bytes 442376 | tf_op jit(solution)/shard_map/ppermute | solution.py:320
  3.8 7.4 %collective-permute-start.5 = (bf16[9,64,128]{2,1,0:T(8,128)(2,1)}, bf16[9,64,128]{2,1,0:T(8,128)(2,1)S(1)}, u32[]{:S(2)}, u32[]{:S(2)}) collective-permute-start(bf16[9,64,128]{2,1,0:T(8,128)(2,1)} %bitcast.75), channel_id=1, source_target_pairs={{0,32},{32,0},{64,96},{96,64},{1,33},{33,1},{65,97},{97,65},{2,34}... | collective-permute-start | bytes 442376 | tf_op jit(solution)/shard_map/ppermute | solution.py:320
  4.2 1.0 copy-start
  5.2 1.0 copy-start.1
  6.3 4.9 %copy-start.2 = (bf16[3,3,64,128]{3,2,1,0:T(8,128)(2,1)S(1)}, bf16[3,3,64,128]{3,2,1,0:T(8,128)(2,1)}, u32[]{:S(2)}) copy-start(bf16[3,3,64,128]{3,2,1,0:T(8,128)(2,1)} %param.4) | copy-start | bytes 442372
  8.7 16.7 %collective-permute-start.2 = (bf16[4,64,1024]{2,1,0:T(8,128)(2,1)S(1)}, bf16[4,64,1024]{2,1,0:T(8,128)(2,1)S(1)}, u32[]{:S(2)}, u32[]{:S(2)}) collective-permute-start(bf16[4,64,1024]{2,1,0:T(8,128)(2,1)S(1)} %get-tuple-element.30.c0.x0), channel_id=1, source_target_pairs={{0,2},{1,3},{2,0},{3,1},{4,6},{5,7},{6,4},{7,5},{8,10},{9,11},{10,... | collective-permute-start | bytes 1572872 | tf_op jit(solution)/shard_map/ppermute | solution.py:320
  11.1 23.3 %collective-permute-start.1 = (bf16[4,64,1024]{2,1,0:T(8,128)(2,1)S(1)}, bf16[4,64,1024]{2,1,0:T(8,128)(2,1)S(1)}, u32[]{:S(2)}, u32[]{:S(2)}) collective-permute-start(bf16[4,64,1024]{2,1,0:T(8,128)(2,1)S(1)} %get-tuple-element.30.c0.x0), channel_id=1, source_target_pairs={{1,2},{2,1},{3,0},{0,3},{5,6},{6,5},{7,4},{4,7},{9,10},{10,9},{11,... | collective-permute-start | bytes 1572872 | tf_op jit(solution)/shard_map/ppermute | solution.py:320
  11.8 5.9 %collective-permute-start.8 = (bf16[9,64,128]{2,1,0:T(8,128)(2,1)S(1)}, bf16[9,64,128]{2,1,0:T(8,128)(2,1)S(1)}, u32[]{:S(2)}, u32[]{:S(2)}) collective-permute-start(bf16[9,64,128]{2,1,0:T(8,128)(2,1)S(1)} %get-tuple-element.32), channel_id=1, source_target_pairs={{0,4},{4,0},{8,12},{12,8},{1,5},{5,1},{9,13},{13,9},{2,6},{6,2},{1... | collective-permute-start | bytes 442376 | tf_op jit(solution)/shard_map/ppermute | solution.py:341
  13.4 9.8 %collective-permute-start.9 = (bf16[9,64,128]{2,1,0:T(8,128)(2,1)S(1)}, bf16[9,64,128]{2,1,0:T(8,128)(2,1)S(1)}, u32[]{:S(2)}, u32[]{:S(2)}) collective-permute-start(bf16[9,64,128]{2,1,0:T(8,128)(2,1)S(1)} %get-tuple-element.33), channel_id=1, source_target_pairs={{4,8},{8,4},{12,0},{0,12},{5,9},{9,5},{13,1},{1,13},{6,10},{10,6},... | collective-permute-start | bytes 442376 | tf_op jit(solution)/shard_map/ppermute | solution.py:341
  15.5 9.2 %collective-permute-start.10 = (bf16[9,64,128]{2,1,0:T(8,128)(2,1)S(1)}, bf16[9,64,128]{2,1,0:T(8,128)(2,1)S(1)}, u32[]{:S(2)}, u32[]{:S(2)}) collective-permute-start(bf16[9,64,128]{2,1,0:T(8,128)(2,1)S(1)} %get-tuple-element.34), channel_id=1, source_target_pairs={{0,8},{4,12},{8,0},{12,4},{1,9},{5,13},{9,1},{13,5},{2,10},{6,14},... | collective-permute-start | bytes 442376 | tf_op jit(solution)/shard_map/ppermute | solution.py:341
  17.8 16.7 %collective-permute-start = (bf16[4,64,1024]{2,1,0:T(8,128)(2,1)S(1)}, bf16[4,64,1024]{2,1,0:T(8,128)(2,1)S(1)}, u32[]{:S(2)}, u32[]{:S(2)}) collective-permute-start(bf16[4,64,1024]{2,1,0:T(8,128)(2,1)S(1)} %get-tuple-element.30.c0.x0), channel_id=1, source_target_pairs={{0,1},{1,0},{2,3},{3,2},{4,5},{5,4},{6,7},{7,6},{8,9},{9,8},{10,11... | collective-permute-start | bytes 1572872 | tf_op jit(solution)/shard_map/ppermute | solution.py:320
  23.2 16.3 %collective-permute-start.18 = (bf16[4,64,1024]{2,1,0:T(8,128)(2,1)S(1)}, bf16[4,64,1024]{2,1,0:T(8,128)(2,1)S(1)}, u32[]{:S(2)}, u32[]{:S(2)}) collective-permute-start(bf16[4,64,1024]{2,1,0:T(8,128)(2,1)S(1)} %get-tuple-element.43.c0.g0), channel_id=1, source_target_pairs={{0,8},{4,12},{8,0},{12,4},{1,9},{5,13},{9,1},{13,5},{2,10},{6,14},... | collective-permute-start | bytes 1572872 | tf_op jit(solution)/shard_map/ppermute | solution.py:320
  24.7 22.2 %collective-permute-start.17 = (bf16[4,64,1024]{2,1,0:T(8,128)(2,1)S(1)}, bf16[4,64,1024]{2,1,0:T(8,128)(2,1)S(1)}, u32[]{:S(2)}, u32[]{:S(2)}) collective-permute-start(bf16[4,64,1024]{2,1,0:T(8,128)(2,1)S(1)} %get-tuple-element.43.c0.g0), channel_id=1, source_target_pairs={{4,8},{8,4},{12,0},{0,12},{5,9},{9,5},{13,1},{1,13},{6,10},{10,6},... | collective-permute-start | bytes 1572872 | tf_op jit(solution)/shard_map/ppermute | solution.py:320
  25.4 22.7 %collective-permute-start.16 = (bf16[4,64,1024]{2,1,0:T(8,128)(2,1)S(1)}, bf16[4,64,1024]{2,1,0:T(8,128)(2,1)S(1)}, u32[]{:S(2)}, u32[]{:S(2)}) collective-permute-start(bf16[4,64,1024]{2,1,0:T(8,128)(2,1)S(1)} %get-tuple-element.43.c0.g0), channel_id=1, source_target_pairs={{0,4},{4,0},{8,12},{12,8},{1,5},{5,1},{9,13},{13,9},{2,6},{6,2},{1... | collective-permute-start | bytes 1572872 | tf_op jit(solution)/shard_map/ppermute | solution.py:320
  34.3 19.7 %collective-permute-start.11 = (bf16[4,9,64,128]{3,2,1,0:T(8,128)(2,1)S(1)}, bf16[4,9,64,128]{3,2,1,0:T(8,128)(2,1)S(1)}, u32[]{:S(2)}, u32[]{:S(2)}) collective-permute-start(bf16[4,9,64,128]{3,2,1,0:T(8,128)(2,1)S(1)} %pad_maximum_fusion.mine), channel_id=1, source_target_pairs={{0,16},{16,0},{1,17},{17,1},{2,18},{18,2},{3,19},{19,3},{4,20},{20... | collective-permute-start | bytes 1769480 | tf_op jit(solution)/shard_map/ppermute | solution.py:343
  34.6 21.0 %collective-permute-start.3 = (bf16[4,4,64,128]{3,2,1,0:T(8,128)(2,1)S(1)}, bf16[4,4,64,128]{3,2,1,0:T(8,128)(2,1)S(1)}, u32[]{:S(2)}, u32[]{:S(2)}) collective-permute-start(bf16[4,4,64,128]{3,2,1,0:T(8,128)(2,1)S(1)} %pad_maximum_fusion.1), channel_id=1, source_target_pairs={{0,16},{16,32},{32,48},{48,64},{64,80},{80,96},{96,112},{1,17},{17... | collective-permute-start | bytes 786440 | tf_op jit(solution)/shard_map/ppermute | solution.py:329
  39.5 16.1 %collective-permute-start.4 = (bf16[4,4,64,128]{3,2,1,0:T(8,128)(2,1)S(1)}, bf16[4,4,64,128]{3,2,1,0:T(8,128)(2,1)S(1)}, u32[]{:S(2)}, u32[]{:S(2)}) collective-permute-start(bf16[4,4,64,128]{3,2,1,0:T(8,128)(2,1)S(1)} %pad_maximum_fusion.2), channel_id=1, source_target_pairs={{16,0},{32,16},{48,32},{64,48},{80,64},{96,80},{112,96},{17,1},{33... | collective-permute-start | bytes 786440 | tf_op jit(solution)/shard_map/ppermute | solution.py:329
  48.2 19.4 %collective-permute-start.21 = (bf16[4,4,64,128]{3,2,1,0:T(8,128)(2,1)S(1)}, bf16[4,4,64,128]{3,2,1,0:T(8,128)(2,1)S(1)}, u32[]{:S(2)}, u32[]{:S(2)}) collective-permute-start(bf16[4,4,64,128]{3,2,1,0:T(8,128)(2,1)S(1)} %pad_maximum_fusion.3), channel_id=1, source_target_pairs={{0,16},{16,32},{32,48},{48,64},{64,80},{80,96},{96,112},{1,17},{17... | collective-permute-start | bytes 786440 | tf_op jit(solution)/shard_map/ppermute | solution.py:329
  50.2 17.5 %collective-permute-start.22 = (bf16[4,4,64,128]{3,2,1,0:T(8,128)(2,1)S(1)}, bf16[4,4,64,128]{3,2,1,0:T(8,128)(2,1)S(1)}, u32[]{:S(2)}, u32[]{:S(2)}) collective-permute-start(bf16[4,4,64,128]{3,2,1,0:T(8,128)(2,1)S(1)} %pad_maximum_fusion.4), channel_id=1, source_target_pairs={{16,0},{32,16},{48,32},{64,48},{80,64},{96,80},{112,96},{17,1},{33... | collective-permute-start | bytes 786440 | tf_op jit(solution)/shard_map/ppermute | solution.py:329
  61.4 23.9 %collective-permute-start.12 = (f32[2,4,64,512]{3,2,1,0:T(8,128)S(1)}, f32[2,4,64,512]{3,2,1,0:T(8,128)S(1)}, u32[]{:S(2)}, u32[]{:S(2)}) collective-permute-start(f32[2,4,64,512]{3,2,1,0:T(8,128)S(1)} %get-tuple-element.37), channel_id=1, source_target_pairs={{0,4},{4,0},{8,12},{12,8},{1,5},{5,1},{9,13},{13,9},{2,6},{6,2},{1... | collective-permute-start | bytes 3145736 | tf_op jit(solution)/shard_map/ppermute | solution.py:357
  61.8 26.1 %collective-permute-start.14 = (f32[2,4,64,512]{3,2,1,0:T(8,128)S(1)}, f32[2,4,64,512]{3,2,1,0:T(8,128)S(1)}, u32[]{:S(2)}, u32[]{:S(2)}) collective-permute-start(f32[2,4,64,512]{3,2,1,0:T(8,128)S(1)} %get-tuple-element.40), channel_id=1, source_target_pairs={{4,8},{8,4},{12,0},{0,12},{5,9},{9,5},{13,1},{1,13},{6,10},{10,6},... | collective-permute-start | bytes 3145736 | tf_op jit(solution)/shard_map/ppermute | solution.py:358
  78.8 9.2 %collective-permute-start.25 = (f32[4,9,64,128]{3,2,1,0:T(8,128)S(1)}, f32[4,9,64,128]{3,2,1,0:T(8,128)S(1)}, u32[]{:S(2)}, u32[]{:S(2)}) collective-permute-start(f32[4,9,64,128]{3,2,1,0:T(8,128)S(1)} %get-tuple-element.54), channel_id=1, source_target_pairs={{0,16},{16,0},{1,17},{17,1},{2,18},{18,2},{3,19},{19,3},{4,20},{20... | collective-permute-start | bytes 3538952 | tf_op jit(solution)/shard_map/ppermute | solution.py:365
  78.9 25.6 %collective-permute-start.23 = (f32[2,4,64,512]{3,2,1,0:T(8,128)S(1)}, f32[2,4,64,512]{3,2,1,0:T(8,128)S(1)}, u32[]{:S(2)}, u32[]{:S(2)}) collective-permute-start(f32[2,4,64,512]{3,2,1,0:T(8,128)S(1)} %get-tuple-element.50), channel_id=1, source_target_pairs={{1,2},{2,1},{3,0},{0,3},{5,6},{6,5},{7,4},{4,7},{9,10},{10,9},{11,... | collective-permute-start | bytes 3145736 | tf_op jit(solution)/shard_map/ppermute | solution.py:362
  80.4 25.2 %collective-permute-start.19 = (f32[2,4,64,512]{3,2,1,0:T(8,128)S(1)}, f32[2,4,64,512]{3,2,1,0:T(8,128)S(1)}, u32[]{:S(2)}, u32[]{:S(2)}) collective-permute-start(f32[2,4,64,512]{3,2,1,0:T(8,128)S(1)} %get-tuple-element.46), channel_id=1, source_target_pairs={{0,1},{1,0},{2,3},{3,2},{4,5},{5,4},{6,7},{7,6},{8,9},{9,8},{10,11... | collective-permute-start | bytes 3145736 | tf_op jit(solution)/shard_map/ppermute | solution.py:360
  85.5 30.7 %collective-permute-start.13 = (f32[4,64,512]{2,1,0:T(8,128)S(1)}, f32[4,64,512]{2,1,0:T(8,128)S(1)}, u32[]{:S(2)}, u32[]{:S(2)}) collective-permute-start(f32[4,64,512]{2,1,0:T(8,128)S(1)} %fusion.3), channel_id=1, source_target_pairs={{4,8},{8,4},{12,0},{0,12},{5,9},{9,5},{13,1},{1,13},{6,10},{10,6},... | collective-permute-start | bytes 1572872 | tf_op jit(solution)/shard_map/ppermute | solution.py:333
  88.3 18.5 %collective-permute-start.26 = (f32[9,64,128]{2,1,0:T(8,128)S(1)}, f32[9,64,128]{2,1,0:T(8,128)S(1)}, u32[]{:S(2)}, u32[]{:S(2)}) collective-permute-start(f32[9,64,128]{2,1,0:T(8,128)S(1)} %get-tuple-element.57), channel_id=1, source_target_pairs={{0,32},{32,64},{64,96},{96,0},{1,33},{33,65},{65,97},{97,1},{2,34}... | collective-permute-start | bytes 884744 | tf_op jit(solution)/shard_map/ppermute | solution.py:370
  88.4 19.0 %collective-permute-start.28 = (f32[9,64,128]{2,1,0:T(8,128)S(1)}, f32[9,64,128]{2,1,0:T(8,128)S(1)}, u32[]{:S(2)}, u32[]{:S(2)}) collective-permute-start(f32[9,64,128]{2,1,0:T(8,128)S(1)} %get-tuple-element.58), channel_id=1, source_target_pairs={{0,64},{32,96},{64,0},{96,32},{1,65},{33,97},{65,1},{97,33},{2,66}... | collective-permute-start | bytes 884744 | tf_op jit(solution)/shard_map/ppermute | solution.py:370
  104.5 9.7 %collective-permute-start.27 = (f32[9,64,128]{2,1,0:T(8,128)S(1)}, f32[9,64,128]{2,1,0:T(8,128)S(1)}, u32[]{:S(2)}, u32[]{:S(2)}) collective-permute-start(f32[9,64,128]{2,1,0:T(8,128)S(1)} %get-tuple-element.59), channel_id=1, source_target_pairs={{0,96},{32,0},{64,32},{96,64},{1,97},{33,1},{65,33},{97,65},{2,98}... | collective-permute-start | bytes 884744 | tf_op jit(solution)/shard_map/ppermute | solution.py:370
  105.6 14.8 %collective-permute-start.15 = (f32[4,64,512]{2,1,0:T(8,128)S(1)}, f32[4,64,512]{2,1,0:T(8,128)S(1)}, u32[]{:S(2)}, u32[]{:S(2)}) collective-permute-start(f32[4,64,512]{2,1,0:T(8,128)S(1)} %fusion.2), channel_id=1, source_target_pairs={{0,4},{4,0},{8,12},{12,8},{1,5},{5,1},{9,13},{13,9},{2,6},{6,2},{1... | collective-permute-start | bytes 1572872 | tf_op jit(solution)/shard_map/ppermute | solution.py:334
  106.8 15.8 %collective-permute-start.24 = (f32[4,64,512]{2,1,0:T(8,128)S(1)}, f32[4,64,512]{2,1,0:T(8,128)S(1)}, u32[]{:S(2)}, u32[]{:S(2)}) collective-permute-start(f32[4,64,512]{2,1,0:T(8,128)S(1)} %fusion), channel_id=1, source_target_pairs={{0,1},{1,0},{2,3},{3,2},{4,5},{5,4},{6,7},{7,6},{8,9},{9,8},{10,11... | collective-permute-start | bytes 1572872 | tf_op jit(solution)/shard_map/ppermute | solution.py:334
  107.4 15.2 %collective-permute-start.20 = (f32[4,64,512]{2,1,0:T(8,128)S(1)}, f32[4,64,512]{2,1,0:T(8,128)S(1)}, u32[]{:S(2)}, u32[]{:S(2)}) collective-permute-start(f32[4,64,512]{2,1,0:T(8,128)S(1)} %fusion.1), channel_id=1, source_target_pairs={{1,2},{2,1},{3,0},{0,3},{5,6},{6,5},{7,4},{4,7},{9,10},{10,9},{11,... | collective-permute-start | bytes 1572872 | tf_op jit(solution)/shard_map/ppermute | solution.py:333
  114.2 18.7 %collective-permute-start.29 = (f32[9,64,128]{2,1,0:T(8,128)S(1)}, f32[9,64,128]{2,1,0:T(8,128)S(1)}, u32[]{:S(2)}, u32[]{:S(2)}) collective-permute-start(f32[9,64,128]{2,1,0:T(8,128)S(1)} %fusion.6), channel_id=1, source_target_pairs={{0,0},{4,32},{8,64},{12,96},{32,4},{36,36},{40,68},{44,100},{64,8}... | collective-permute-start | bytes 884744 | tf_op jit(solution)/shard_map/ppermute | solution.py:372

commit v6 on v5

--- a/solution.py
+++ b/solution.py
@@ -37,13 +37,24 @@
     return jnp.where(apart == 0, 0, jnp.where(apart == 2, 3, jnp.where(apart == 1, 1 + odd, 2 - odd)))
 
 
-def pack_kernel(x_ref, g_ref, x_out, g_out, rows_ref, mix_ref):
+def pack_kernel(x_hbm, g_hbm, x_out, g_out, taken, rows_ref, mix_ref, in_sem):
     low = lane_of((32, LANES)) < W
-    for i, (t, q) in enumerate((t, q) for t in range(2) for q in range(4)):
+    pieces = [(t, q) for t in range(2) for q in range(4)]
+
+    def fetch(t, q, side):
+        source = (x_hbm, g_hbm)[t].at[q + 4 * side]
+        return pltpu.make_async_copy(source, taken.at[t, q, side], in_sem.at[t, q, side])
+
+    for t, q in pieces:
+        for side in range(2):
+            fetch(t, q, side).start()
+    for i, (t, q) in enumerate(pieces):
         b = i % 2
-        source, target = ((x_ref, x_out), (g_ref, g_out))[t]
-        for side in range(2):
-            flat = source[q + 4 * side].astype(F32)
+        target = (x_out, g_out)[t]
+        for side in range(2):
+            fetch(t, q, side).wait()
+        for side in range(2):
+            flat = taken[t, q, side].astype(F32)
             for p in range(32):
                 rows_ref[b, side, :, p, :] = flat[:, p * LANES : (p + 1) * LANES]
         for h in range(8):
@@ -57,16 +68,22 @@
 
 def pack(x, g):
     shape = jax.ShapeDtypeStruct((4, 64, 1024), BF16)
+    far = pl.BlockSpec(memory_space=pltpu.HBM)
     near = pl.BlockSpec(memory_space=pltpu.VMEM)
     return pl.pallas_call(
         pack_kernel,
         out_shape=(shape, shape),
-        in_specs=[near] * 2,
+        in_specs=[far] * 2,
         out_specs=[near] * 2,
-        scratch_shapes=[pltpu.VMEM((2, 2, 8, 32, LANES), F32), pltpu.VMEM((2, 8, 64, LANES), F32)],
+        scratch_shapes=[
+            pltpu.VMEM((2, 4, 2, 8, 4096), BF16),
+            pltpu.VMEM((2, 2, 8, 32, LANES), F32),
+            pltpu.VMEM((2, 8, 64, LANES), F32),
+            pltpu.SemaphoreType.DMA((2, 4, 2)),
+        ],
         compiler_params=params(8),
         name="pack",
-    )(x, g)
+    )(*(pltpu.with_memory_space_constraint(a, pltpu.HBM) for a in (x, g)))
 
 
 ROWS = ((1, 2, 3, 4), (5, 6, 7, 0))

time: 136 us -> 136 us (level)
  the two profiles are of different devices: /device:TPU:104 before, /device:TPU:97 now
where the time goes in v6:
time: 136 us; the launch traced here: 135 us
  starting transfers between devices  51.9 us (38%)
  waiting for transfers between devices  50.3 us (37%)
  Pallas kernels  30.9 us (23%)
    ppermute x1, waiting for transfers between devices, step(): grad_one_b = lax.ppermute(grad_b[2], 'y', SECOND)  15.5 us
    ppermute x2, starting transfers between devices, edges(): lax.ppermute(first, ('z', 'core'), backward)  13.9 us
    pallas_call x3, Pallas kernels, conv(): pl.pallas_call(functools.partial(conv_kernel, halves, rows), out_shape=(s...  12.7 us
    ppermute x1, waiting for transfers between devices, step(): home = lax.ppermute(total, ('z', 'x'), cross)  12.6 us
    ppermute x3, waiting for transfers between devices, gather(): lax.ppermute(block, axis, SECOND)  11.2 us
    pallas_call x1, Pallas kernels, weight_grads(): pl.pallas_call(kernel_grad_kernel, out_shape=(shape,) * 2, in_specs=[pl.B...  7.67 us
    ppermute x3, starting transfers between devices, gather(): lax.ppermute(block, axis, OPPOSITE)  5.57 us
    ppermute x3, starting transfers between devices, step(): total = total + lax.ppermute(near[k], 'z', ring(turn))  5.03 us
  transfers between devices with their start and end apart: 30, of which 11 were waited for; matrix products, arithmetic and copies ran while one was open for 1% of the time, Pallas kernels for 21%

profile of v6, /device:TPU:97, one launch (start us, length us, event | category | flops | bytes accessed | tf_op | source)
XLA Modules:
  0.0 135.4 jit_solution(9615453377103539202)
XLA Ops:
  0.6 0.4 collective-permute-start.7
  1.0 2.2 %collective-permute-start.6 = (bf16[9,64,128]{2,1,0:T(8,128)(2,1)}, bf16[9,64,128]{2,1,0:T(8,128)(2,1)S(1)}, u32[]{:S(2)}, u32[]{:S(2)}) collective-permute-start(bf16[9,64,128]{2,1,0:T(8,128)(2,1)} %bitcast.74), channel_id=1, source_target_pairs={{32,64},{64,32},{96,0},{0,96},{33,65},{65,33},{97,1},{1,97},{34,66... | collective-permute-start | bytes 442376 | tf_op jit(solution)/shard_map/ppermute | solution.py:337
  3.2 0.1 collective-permute-start.5
  3.4 3.9 %pack.1 = (bf16[4,64,1024]{2,1,0:T(8,128)(2,1)S(1)}, bf16[4,64,1024]{2,1,0:T(8,128)(2,1)S(1)}) custom-call(bf16[8,8,4096]{2,1,0:T(8,128)(2,1)} %x_hbm.1, bf16[8,8,4096]{2,1,0:T(8,128)(2,1)} %g_hbm.1), custom_call_target="tpu_custom_call" | custom-call | tf_op jit(solution)/shard_map/pack/pallas_call | solution.py:73
  7.3 3.0 %collective-permute-start.2 = (bf16[4,64,1024]{2,1,0:T(8,128)(2,1)S(1)}, bf16[4,64,1024]{2,1,0:T(8,128)(2,1)S(1)}, u32[]{:S(2)}, u32[]{:S(2)}) collective-permute-start(bf16[4,64,1024]{2,1,0:T(8,128)(2,1)S(1)} %get-tuple-element.30.c0.x0), channel_id=1, source_target_pairs={{0,2},{1,3},{2,0},{3,1},{4,6},{5,7},{6,4},{7,5},{8,10},{9,11},{10,... | collective-permute-start | bytes 1572872 | tf_op jit(solution)/shard_map/ppermute | solution.py:337
  10.3 0.8 collective-permute-start.1
  11.3 0.6 route.1
  12.0 1.3 collective-permute-start.8
  13.2 1.8 %collective-permute-start.9 = (bf16[9,64,128]{2,1,0:T(8,128)(2,1)S(1)}, bf16[9,64,128]{2,1,0:T(8,128)(2,1)S(1)}, u32[]{:S(2)}, u32[]{:S(2)}) collective-permute-start(bf16[9,64,128]{2,1,0:T(8,128)(2,1)S(1)} %get-tuple-element.33), channel_id=1, source_target_pairs={{4,8},{8,4},{12,0},{0,12},{5,9},{9,5},{13,1},{1,13},{6,10},{10,6},... | collective-permute-start | bytes 442376 | tf_op jit(solution)/shard_map/ppermute | solution.py:358
  15.1 0.6 collective-permute-start.10
  15.7 0.6 collective-permute-done.8
  16.3 1.9 %collective-permute-start = (bf16[4,64,1024]{2,1,0:T(8,128)(2,1)S(1)}, bf16[4,64,1024]{2,1,0:T(8,128)(2,1)S(1)}, u32[]{:S(2)}, u32[]{:S(2)}) collective-permute-start(bf16[4,64,1024]{2,1,0:T(8,128)(2,1)S(1)} %get-tuple-element.30.c0.x0), channel_id=1, source_target_pairs={{0,1},{1,0},{2,3},{3,2},{4,5},{5,4},{6,7},{7,6},{8,9},{9,8},{10,11... | collective-permute-start | bytes 1572872 | tf_op jit(solution)/shard_map/ppermute | solution.py:337
  18.2 0.5 collective-permute-done.9
  18.7 2.2 %collective-permute-start.18 = (bf16[4,64,1024]{2,1,0:T(8,128)(2,1)S(1)}, bf16[4,64,1024]{2,1,0:T(8,128)(2,1)S(1)}, u32[]{:S(2)}, u32[]{:S(2)}) collective-permute-start(bf16[4,64,1024]{2,1,0:T(8,128)(2,1)S(1)} %get-tuple-element.43.c0.g0), channel_id=1, source_target_pairs={{0,8},{4,12},{8,0},{12,4},{1,9},{5,13},{9,1},{13,5},{2,10},{6,14},... | collective-permute-start | bytes 1572872 | tf_op jit(solution)/shard_map/ppermute | solution.py:337
  21.0 1.4 %collective-permute-done.10 = bf16[9,64,128]{2,1,0:T(8,128)(2,1)S(1)} collective-permute-done((bf16[9,64,128]{2,1,0:T(8,128)(2,1)S(1)}, bf16[9,64,128]{2,1,0:T(8,128)(2,1)S(1)}, u32[]{:S(2)}, u32[]{:S(2)}) %collective-permute-start.10) | collective-permute-done | bytes 147488 | tf_op jit(solution)/shard_map/ppermute | solution.py:358
  22.3 0.4 collective-permute-start.17
  22.9 11.0 %collective-permute-done.1.c2.x2 = bf16[4,64,1024]{2,1,0:T(8,128)(2,1)S(1)} collective-permute-done((bf16[4,64,1024]{2,1,0:T(8,128)(2,1)S(1)}, bf16[4,64,1024]{2,1,0:T(8,128)(2,1)S(1)}, u32[]{:S(2)}, u32[]{:S(2)}) %collective-permute-start.1) | collective-permute-done | bytes 524320 | tf_op jit(solution)/shard_map/ppermute | solution.py:337
  34.0 0.5 collective-permute-start.11
  34.6 1.3 collective-permute-start.3
  35.9 7.4 %collective-permute-start.4 = (bf16[4,4,64,128]{3,2,1,0:T(8,128)(2,1)S(1)}, bf16[4,4,64,128]{3,2,1,0:T(8,128)(2,1)S(1)}, u32[]{:S(2)}, u32[]{:S(2)}) collective-permute-start(bf16[4,4,64,128]{3,2,1,0:T(8,128)(2,1)S(1)} %pad_maximum_fusion.2), channel_id=1, source_target_pairs={{16,0},{32,16},{48,32},{64,48},{80,64},{96,80},{112,96},{17,1},{33... | collective-permute-start | bytes 786440 | tf_op jit(solution)/shard_map/ppermute | solution.py:346
  43.5 1.3 collective-permute-start.21
  44.8 6.5 %collective-permute-start.22 = (bf16[4,4,64,128]{3,2,1,0:T(8,128)(2,1)S(1)}, bf16[4,4,64,128]{3,2,1,0:T(8,128)(2,1)S(1)}, u32[]{:S(2)}, u32[]{:S(2)}) collective-permute-start(bf16[4,4,64,128]{3,2,1,0:T(8,128)(2,1)S(1)} %pad_maximum_fusion.4), channel_id=1, source_target_pairs={{16,0},{32,16},{48,32},{64,48},{80,64},{96,80},{112,96},{17,1},{33... | collective-permute-start | bytes 786440 | tf_op jit(solution)/shard_map/ppermute | solution.py:346
  51.3 1.6 %weights.1 = (bf16[3,256,768]{2,1,0:T(8,128)(2,1)S(1)}, bf16[3,256,768]{2,1,0:T(8,128)(2,1)S(1)}) custom-call(s32[4]{0:T(128)S(1)} %pad_add_fusion.at, bf16[4,9,64,128]{3,2,1,0:T(8,128)(2,1)S(1)} %pad_maximum_fusion.mine, bf16[4,9,64,128]{3,2,1,0:T(8,128)(2,1)S(1)} %collective-permute-done.11.other), custom_call_target="tpu_custom_call" | custom-call | tf_op jit(solution)/shard_map/weights/pallas_call | solution.py:195
  52.9 5.9 %shard_map.58 = (f32[4,64,512]{2,1,0:T(8,128)S(1)}, f32[4,64,512]{2,1,0:T(8,128)S(1)}, f32[2,4,64,512]{3,2,1,0:T(8,128)S(1)}, f32[4,64,512]{2,1,0:T(8,128)S(1)},...) custom-call(s32[4]{0:T(128)S(1)} %pad_add_fusion.at, bf16[4,64,1024]{2,1,0:T(8,128)(2,1)S(1)} %get-tuple-element.30.c0.x0, ...), custom_call_target="tpu_custom_call" | custom-call | flops 4831838208 | bytes 12000000 | tf_op jit(solution)/shard_map/pallas_call | solution.py:264
  58.9 1.7 %collective-permute-start.14 = (f32[2,4,64,512]{3,2,1,0:T(8,128)S(1)}, f32[2,4,64,512]{3,2,1,0:T(8,128)S(1)}, u32[]{:S(2)}, u32[]{:S(2)}) collective-permute-start(f32[2,4,64,512]{3,2,1,0:T(8,128)S(1)} %get-tuple-element.40), channel_id=1, source_target_pairs={{4,8},{8,4},{12,0},{0,12},{5,9},{9,5},{13,1},{1,13},{6,10},{10,6},... | collective-permute-start | bytes 3145736 | tf_op jit(solution)/shard_map/ppermute | solution.py:375
  60.6 3.4 %shard_map.59 = (f32[4,64,512]{2,1,0:T(8,128)S(1)}, f32[4,64,512]{2,1,0:T(8,128)S(1)}, f32[2,4,64,512]{3,2,1,0:T(8,128)S(1)}) custom-call(s32[4]{0:T(128)S(1)} %pad_add_fusion.at, bf16[4,64,1024]{2,1,0:T(8,128)(2,1)S(1)} %get-tuple-element.43.c0.g0, bf16[4,64,1024]{2,1,0:T(8,128)(2,1)S(1)} %collective-permute-done.16.c1.g1, ...), custom_call_target="tpu_custom_call" | custom-call | flops 2415919104 | bytes 6000000 | tf_op jit(solution)/shard_map/pallas_call | solution.py:264
  64.0 3.5 %shard_map.60 = (f32[4,64,512]{2,1,0:T(8,128)S(1)}, f32[4,64,512]{2,1,0:T(8,128)S(1)}, f32[2,4,64,512]{3,2,1,0:T(8,128)S(1)}) custom-call(s32[4]{0:T(128)S(1)} %pad_add_fusion.at, bf16[4,64,1024]{2,1,0:T(8,128)(2,1)S(1)} %get-tuple-element.43.c0.g0, bf16[4,64,1024]{2,1,0:T(8,128)(2,1)S(1)} %collective-permute-done.16.c1.g1, ...), custom_call_target="tpu_custom_call" | custom-call | flops 2415919104 | bytes 6000000 | tf_op jit(solution)/shard_map/pallas_call | solution.py:264
  67.5 7.7 %weight_grads.1 = (f32[4,9,64,128]{3,2,1,0:T(8,128)S(1)}, f32[4,9,64,128]{3,2,1,0:T(8,128)S(1)}) custom-call(s32[4]{0:T(128)S(1)} %pad_add_fusion.at, bf16[4,64,1024]{2,1,0:T(8,128)(2,1)S(1)} %get-tuple-element.30.c0.x0, bf16[4,64,1024]{2,1,0:T(8,128)(2,1)S(1)} %collective-permute-done.c1.x1, bf16[4,64,1024]{2,1,0:T(8,128)(2,1)S(1)} %collective-permute-done.1.c2.x2, ...), custom_call_target="tpu_custom_call" | custom-call | flops 4831838208 | bytes 9000000 | tf_op jit(solution)/shard_map/weight_grads/pallas_call | solution.py:315
  75.2 2.1 %collective-permute-start.25 = (f32[4,9,64,128]{3,2,1,0:T(8,128)S(1)}, f32[4,9,64,128]{3,2,1,0:T(8,128)S(1)}, u32[]{:S(2)}, u32[]{:S(2)}) collective-permute-start(f32[4,9,64,128]{3,2,1,0:T(8,128)S(1)} %get-tuple-element.54), channel_id=1, source_target_pairs={{0,16},{16,0},{1,17},{17,1},{2,18},{18,2},{3,19},{19,3},{4,20},{20... | collective-permute-start | bytes 3538952 | tf_op jit(solution)/shard_map/ppermute | solution.py:382
  77.3 3.3 %collective-permute-start.23 = (f32[2,4,64,512]{3,2,1,0:T(8,128)S(1)}, f32[2,4,64,512]{3,2,1,0:T(8,128)S(1)}, u32[]{:S(2)}, u32[]{:S(2)}) collective-permute-start(f32[2,4,64,512]{3,2,1,0:T(8,128)S(1)} %get-tuple-element.50), channel_id=1, source_target_pairs={{1,2},{2,1},{3,0},{0,3},{5,6},{6,5},{7,4},{4,7},{9,10},{10,9},{11,... | collective-permute-start | bytes 3145736 | tf_op jit(solution)/shard_map/ppermute | solution.py:379
  80.5 1.7 %collective-permute-start.19 = (f32[2,4,64,512]{3,2,1,0:T(8,128)S(1)}, f32[2,4,64,512]{3,2,1,0:T(8,128)S(1)}, u32[]{:S(2)}, u32[]{:S(2)}) collective-permute-start(f32[2,4,64,512]{3,2,1,0:T(8,128)S(1)} %get-tuple-element.46), channel_id=1, source_target_pairs={{0,1},{1,0},{2,3},{3,2},{4,5},{5,4},{6,7},{7,6},{8,9},{9,8},{10,11... | collective-permute-start | bytes 3145736 | tf_op jit(solution)/shard_map/ppermute | solution.py:377
  82.3 1.1 collective-permute-start.13
  83.5 0.2 add.28
  83.8 1.9 %collective-permute-start.26 = (f32[9,64,128]{2,1,0:T(8,128)S(1)}, f32[9,64,128]{2,1,0:T(8,128)S(1)}, u32[]{:S(2)}, u32[]{:S(2)}) collective-permute-start(f32[9,64,128]{2,1,0:T(8,128)S(1)} %get-tuple-element.57), channel_id=1, source_target_pairs={{0,32},{32,64},{64,96},{96,0},{1,33},{33,65},{65,97},{97,1},{2,34}... | collective-permute-start | bytes 884744 | tf_op jit(solution)/shard_map/ppermute | solution.py:387
  85.7 2.7 %collective-permute-start.28 = (f32[9,64,128]{2,1,0:T(8,128)S(1)}, f32[9,64,128]{2,1,0:T(8,128)S(1)}, u32[]{:S(2)}, u32[]{:S(2)}) collective-permute-start(f32[9,64,128]{2,1,0:T(8,128)S(1)} %get-tuple-element.58), channel_id=1, source_target_pairs={{0,64},{32,96},{64,0},{96,32},{1,65},{33,97},{65,1},{97,33},{2,66}... | collective-permute-start | bytes 884744 | tf_op jit(solution)/shard_map/ppermute | solution.py:387
  88.4 15.5 %collective-permute-done.23.one_b = f32[2,4,64,512]{3,2,1,0:T(8,128)S(1)} collective-permute-done((f32[2,4,64,512]{3,2,1,0:T(8,128)S(1)}, f32[2,4,64,512]{3,2,1,0:T(8,128)S(1)}, u32[]{:S(2)}, u32[]{:S(2)}) %collective-permute-start.23) | collective-permute-done | bytes 1048608 | tf_op jit(solution)/shard_map/ppermute | solution.py:379
  104.0 0.4 collective-permute-start.27
  104.5 0.8 collective-permute-done.19.one_a
  105.3 0.8 collective-permute-start.15
  106.2 1.3 collective-permute-start.24
  107.6 1.1 collective-permute-start.20
  108.6 4.4 %collective-permute-done.27 = f32[9,64,128]{2,1,0:T(8,128)S(1)} collective-permute-done((f32[9,64,128]{2,1,0:T(8,128)S(1)}, f32[9,64,128]{2,1,0:T(8,128)S(1)}, u32[]{:S(2)}, u32[]{:S(2)}) %collective-permute-start.27) | collective-permute-done | bytes 294944 | tf_op jit(solution)/shard_map/ppermute | solution.py:387
  113.2 1.9 %collective-permute-start.29 = (f32[9,64,128]{2,1,0:T(8,128)S(1)}, f32[9,64,128]{2,1,0:T(8,128)S(1)}, u32[]{:S(2)}, u32[]{:S(2)}) collective-permute-start(f32[9,64,128]{2,1,0:T(8,128)S(1)} %fusion.6), channel_id=1, source_target_pairs={{0,0},{4,32},{8,64},{12,96},{32,4},{36,36},{40,68},{44,100},{64,8}... | collective-permute-start | bytes 884744 | tf_op jit(solution)/shard_map/ppermute | solution.py:389
  115.1 2.7 %collective-permute-done.15.two_b = f32[4,64,512]{2,1,0:T(8,128)S(1)} collective-permute-done((f32[4,64,512]{2,1,0:T(8,128)S(1)}, f32[4,64,512]{2,1,0:T(8,128)S(1)}, u32[]{:S(2)}, u32[]{:S(2)}) %collective-permute-start.15) | collective-permute-done | bytes 524320 | tf_op jit(solution)/shard_map/ppermute | solution.py:351
  117.7 2.2 %finish.2 = bf16[8,8,4096]{2,1,0:T(8,128)(2,1)} custom-call(f32[4,64,512]{2,1,0:T(8,128)S(1)} %get-tuple-element.36.own_a, f32[2,4,64,512]{3,2,1,0:T(8,128)S(1)} %collective-permute-done.12.one_a, f32[4,64,512]{2,1,0:T(8,128)S(1)} %collective-permute-done.13.two_a, f32[4,64,512]{2,1,0:T(8,128)S(1)} %get-tuple-element.39.own_b, ...), custom_call_target="tpu_custom_call" | custom-call | tf_op jit(solution)/shard_map/finish/pallas_call | solution.py:130
  119.9 0.5 collective-permute-done.20.two_a
  120.5 12.6 %collective-permute-done.29.refs_0_ = f32[9,64,128]{2,1,0:T(8,128)S(1)} collective-permute-done((f32[9,64,128]{2,1,0:T(8,128)S(1)}, f32[9,64,128]{2,1,0:T(8,128)S(1)}, u32[]{:S(2)}, u32[]{:S(2)}) %collective-permute-start.29) | collective-permute-done | bytes 294944 | tf_op jit(solution)/shard_map/ppermute | solution.py:389
  133.0 2.2 %finish.3 = (bf16[8,8,4096]{2,1,0:T(8,128)(2,1)}, f32[9,64,128]{2,1,0:T(8,128)}) custom-call(f32[4,64,512]{2,1,0:T(8,128)S(1)} %get-tuple-element.45.own_a, f32[2,4,64,512]{3,2,1,0:T(8,128)S(1)} %collective-permute-done.19.one_a, f32[4,64,512]{2,1,0:T(8,128)S(1)} %collective-permute-done.20.two_a, f32[4,64,512]{2,1,0:T(8,128)S(1)} %get-tuple-element.49.own_b, ...), custom_call_target="tpu_custom_call" | custom-call | tf_op jit(solution)/shard_map/finish/pallas_call | solution.py:130
  (44 shorter events, 1.3 us)
Async XLA Ops:
  0.6 10.7 %copy-start = (bf16[3,3,64,128]{3,2,1,0:T(8,128)(2,1)S(1)}, bf16[3,3,64,128]{3,2,1,0:T(8,128)(2,1)}, u32[]{:S(2)}) copy-start(bf16[3,3,64,128]{3,2,1,0:T(8,128)(2,1)} %param.4) | copy-start | bytes 442372
  0.6 10.6 %collective-permute-start.7 = (bf16[9,64,128]{2,1,0:T(8,128)(2,1)}, bf16[9,64,128]{2,1,0:T(8,128)(2,1)S(1)}, u32[]{:S(2)}, u32[]{:S(2)}) collective-permute-start(bf16[9,64,128]{2,1,0:T(8,128)(2,1)} %bitcast.73), channel_id=1, source_target_pairs={{0,64},{32,96},{64,0},{96,32},{1,65},{33,97},{65,1},{97,33},{2,66}... | collective-permute-start | bytes 442376 | tf_op jit(solution)/shard_map/ppermute | solution.py:337
  1.0 10.3 %collective-permute-start.6 = (bf16[9,64,128]{2,1,0:T(8,128)(2,1)}, bf16[9,64,128]{2,1,0:T(8,128)(2,1)S(1)}, u32[]{:S(2)}, u32[]{:S(2)}) collective-permute-start(bf16[9,64,128]{2,1,0:T(8,128)(2,1)} %bitcast.74), channel_id=1, source_target_pairs={{32,64},{64,32},{96,0},{0,96},{33,65},{65,33},{97,1},{1,97},{34,66... | collective-permute-start | bytes 442376 | tf_op jit(solution)/shard_map/ppermute | solution.py:337
  3.2 8.1 %collective-permute-start.5 = (bf16[9,64,128]{2,1,0:T(8,128)(2,1)}, bf16[9,64,128]{2,1,0:T(8,128)(2,1)S(1)}, u32[]{:S(2)}, u32[]{:S(2)}) collective-permute-start(bf16[9,64,128]{2,1,0:T(8,128)(2,1)} %bitcast.75), channel_id=1, source_target_pairs={{0,32},{32,0},{64,96},{96,64},{1,33},{33,1},{65,97},{97,65},{2,34}... | collective-permute-start | bytes 442376 | tf_op jit(solution)/shard_map/ppermute | solution.py:337
  7.3 15.5 %collective-permute-start.2 = (bf16[4,64,1024]{2,1,0:T(8,128)(2,1)S(1)}, bf16[4,64,1024]{2,1,0:T(8,128)(2,1)S(1)}, u32[]{:S(2)}, u32[]{:S(2)}) collective-permute-start(bf16[4,64,1024]{2,1,0:T(8,128)(2,1)S(1)} %get-tuple-element.30.c0.x0), channel_id=1, source_target_pairs={{0,2},{1,3},{2,0},{3,1},{4,6},{5,7},{6,4},{7,5},{8,10},{9,11},{10,... | collective-permute-start | bytes 1572872 | tf_op jit(solution)/shard_map/ppermute | solution.py:337
  10.3 23.7 %collective-permute-start.1 = (bf16[4,64,1024]{2,1,0:T(8,128)(2,1)S(1)}, bf16[4,64,1024]{2,1,0:T(8,128)(2,1)S(1)}, u32[]{:S(2)}, u32[]{:S(2)}) collective-permute-start(bf16[4,64,1024]{2,1,0:T(8,128)(2,1)S(1)} %get-tuple-element.30.c0.x0), channel_id=1, source_target_pairs={{1,2},{2,1},{3,0},{0,3},{5,6},{6,5},{7,4},{4,7},{9,10},{10,9},{11,... | collective-permute-start | bytes 1572872 | tf_op jit(solution)/shard_map/ppermute | solution.py:337
  12.0 4.4 %collective-permute-start.8 = (bf16[9,64,128]{2,1,0:T(8,128)(2,1)S(1)}, bf16[9,64,128]{2,1,0:T(8,128)(2,1)S(1)}, u32[]{:S(2)}, u32[]{:S(2)}) collective-permute-start(bf16[9,64,128]{2,1,0:T(8,128)(2,1)S(1)} %get-tuple-element.32), channel_id=1, source_target_pairs={{0,4},{4,0},{8,12},{12,8},{1,5},{5,1},{9,13},{13,9},{2,6},{6,2},{1... | collective-permute-start | bytes 442376 | tf_op jit(solution)/shard_map/ppermute | solution.py:358
  13.2 5.5 %collective-permute-start.9 = (bf16[9,64,128]{2,1,0:T(8,128)(2,1)S(1)}, bf16[9,64,128]{2,1,0:T(8,128)(2,1)S(1)}, u32[]{:S(2)}, u32[]{:S(2)}) collective-permute-start(bf16[9,64,128]{2,1,0:T(8,128)(2,1)S(1)} %get-tuple-element.33), channel_id=1, source_target_pairs={{4,8},{8,4},{12,0},{0,12},{5,9},{9,5},{13,1},{1,13},{6,10},{10,6},... | collective-permute-start | bytes 442376 | tf_op jit(solution)/shard_map/ppermute | solution.py:358
  15.1 7.3 %collective-permute-start.10 = (bf16[9,64,128]{2,1,0:T(8,128)(2,1)S(1)}, bf16[9,64,128]{2,1,0:T(8,128)(2,1)S(1)}, u32[]{:S(2)}, u32[]{:S(2)}) collective-permute-start(bf16[9,64,128]{2,1,0:T(8,128)(2,1)S(1)} %get-tuple-element.34), channel_id=1, source_target_pairs={{0,8},{4,12},{8,0},{12,4},{1,9},{5,13},{9,1},{13,5},{2,10},{6,14},... | collective-permute-start | bytes 442376 | tf_op jit(solution)/shard_map/ppermute | solution.py:358
  16.3 18.2 %collective-permute-start = (bf16[4,64,1024]{2,1,0:T(8,128)(2,1)S(1)}, bf16[4,64,1024]{2,1,0:T(8,128)(2,1)S(1)}, u32[]{:S(2)}, u32[]{:S(2)}) collective-permute-start(bf16[4,64,1024]{2,1,0:T(8,128)(2,1)S(1)} %get-tuple-element.30.c0.x0), channel_id=1, source_target_pairs={{0,1},{1,0},{2,3},{3,2},{4,5},{5,4},{6,7},{7,6},{8,9},{9,8},{10,11... | collective-permute-start | bytes 1572872 | tf_op jit(solution)/shard_map/ppermute | solution.py:337
  18.7 17.2 %collective-permute-start.18 = (bf16[4,64,1024]{2,1,0:T(8,128)(2,1)S(1)}, bf16[4,64,1024]{2,1,0:T(8,128)(2,1)S(1)}, u32[]{:S(2)}, u32[]{:S(2)}) collective-permute-start(bf16[4,64,1024]{2,1,0:T(8,128)(2,1)S(1)} %get-tuple-element.43.c0.g0), channel_id=1, source_target_pairs={{0,8},{4,12},{8,0},{12,4},{1,9},{5,13},{9,1},{13,5},{2,10},{6,14},... | collective-permute-start | bytes 1572872 | tf_op jit(solution)/shard_map/ppermute | solution.py:337
  22.3 21.0 %collective-permute-start.17 = (bf16[4,64,1024]{2,1,0:T(8,128)(2,1)S(1)}, bf16[4,64,1024]{2,1,0:T(8,128)(2,1)S(1)}, u32[]{:S(2)}, u32[]{:S(2)}) collective-permute-start(bf16[4,64,1024]{2,1,0:T(8,128)(2,1)S(1)} %get-tuple-element.43.c0.g0), channel_id=1, source_target_pairs={{4,8},{8,4},{12,0},{0,12},{5,9},{9,5},{13,1},{1,13},{6,10},{10,6},... | collective-permute-start | bytes 1572872 | tf_op jit(solution)/shard_map/ppermute | solution.py:337
  22.8 20.6 %collective-permute-start.16 = (bf16[4,64,1024]{2,1,0:T(8,128)(2,1)S(1)}, bf16[4,64,1024]{2,1,0:T(8,128)(2,1)S(1)}, u32[]{:S(2)}, u32[]{:S(2)}) collective-permute-start(bf16[4,64,1024]{2,1,0:T(8,128)(2,1)S(1)} %get-tuple-element.43.c0.g0), channel_id=1, source_target_pairs={{0,4},{4,0},{8,12},{12,8},{1,5},{5,1},{9,13},{13,9},{2,6},{6,2},{1... | collective-permute-start | bytes 1572872 | tf_op jit(solution)/shard_map/ppermute | solution.py:337
  34.0 17.4 %collective-permute-start.11 = (bf16[4,9,64,128]{3,2,1,0:T(8,128)(2,1)S(1)}, bf16[4,9,64,128]{3,2,1,0:T(8,128)(2,1)S(1)}, u32[]{:S(2)}, u32[]{:S(2)}) collective-permute-start(bf16[4,9,64,128]{3,2,1,0:T(8,128)(2,1)S(1)} %pad_maximum_fusion.mine), channel_id=1, source_target_pairs={{0,16},{16,0},{1,17},{17,1},{2,18},{18,2},{3,19},{19,3},{4,20},{20... | collective-permute-start | bytes 1769480 | tf_op jit(solution)/shard_map/ppermute | solution.py:360
  34.6 18.3 %collective-permute-start.3 = (bf16[4,4,64,128]{3,2,1,0:T(8,128)(2,1)S(1)}, bf16[4,4,64,128]{3,2,1,0:T(8,128)(2,1)S(1)}, u32[]{:S(2)}, u32[]{:S(2)}) collective-permute-start(bf16[4,4,64,128]{3,2,1,0:T(8,128)(2,1)S(1)} %pad_maximum_fusion.1), channel_id=1, source_target_pairs={{0,16},{16,32},{32,48},{48,64},{64,80},{80,96},{96,112},{1,17},{17... | collective-permute-start | bytes 786440 | tf_op jit(solution)/shard_map/ppermute | solution.py:346
  35.9 17.0 %collective-permute-start.4 = (bf16[4,4,64,128]{3,2,1,0:T(8,128)(2,1)S(1)}, bf16[4,4,64,128]{3,2,1,0:T(8,128)(2,1)S(1)}, u32[]{:S(2)}, u32[]{:S(2)}) collective-permute-start(bf16[4,4,64,128]{3,2,1,0:T(8,128)(2,1)S(1)} %pad_maximum_fusion.2), channel_id=1, source_target_pairs={{16,0},{32,16},{48,32},{64,48},{80,64},{96,80},{112,96},{17,1},{33... | collective-permute-start | bytes 786440 | tf_op jit(solution)/shard_map/ppermute | solution.py:346
  43.5 20.5 %collective-permute-start.21 = (bf16[4,4,64,128]{3,2,1,0:T(8,128)(2,1)S(1)}, bf16[4,4,64,128]{3,2,1,0:T(8,128)(2,1)S(1)}, u32[]{:S(2)}, u32[]{:S(2)}) collective-permute-start(bf16[4,4,64,128]{3,2,1,0:T(8,128)(2,1)S(1)} %pad_maximum_fusion.3), channel_id=1, source_target_pairs={{0,16},{16,32},{32,48},{48,64},{64,80},{80,96},{96,112},{1,17},{17... | collective-permute-start | bytes 786440 | tf_op jit(solution)/shard_map/ppermute | solution.py:346
  44.8 19.1 %collective-permute-start.22 = (bf16[4,4,64,128]{3,2,1,0:T(8,128)(2,1)S(1)}, bf16[4,4,64,128]{3,2,1,0:T(8,128)(2,1)S(1)}, u32[]{:S(2)}, u32[]{:S(2)}) collective-permute-start(bf16[4,4,64,128]{3,2,1,0:T(8,128)(2,1)S(1)} %pad_maximum_fusion.4), channel_id=1, source_target_pairs={{16,0},{32,16},{48,32},{64,48},{80,64},{96,80},{112,96},{17,1},{33... | collective-permute-start | bytes 786440 | tf_op jit(solution)/shard_map/ppermute | solution.py:346
  58.8 23.4 %collective-permute-start.12 = (f32[2,4,64,512]{3,2,1,0:T(8,128)S(1)}, f32[2,4,64,512]{3,2,1,0:T(8,128)S(1)}, u32[]{:S(2)}, u32[]{:S(2)}) collective-permute-start(f32[2,4,64,512]{3,2,1,0:T(8,128)S(1)} %get-tuple-element.37), channel_id=1, source_target_pairs={{0,4},{4,0},{8,12},{12,8},{1,5},{5,1},{9,13},{13,9},{2,6},{6,2},{1... | collective-permute-start | bytes 3145736 | tf_op jit(solution)/shard_map/ppermute | solution.py:374
  58.9 24.5 %collective-permute-start.14 = (f32[2,4,64,512]{3,2,1,0:T(8,128)S(1)}, f32[2,4,64,512]{3,2,1,0:T(8,128)S(1)}, u32[]{:S(2)}, u32[]{:S(2)}) collective-permute-start(f32[2,4,64,512]{3,2,1,0:T(8,128)S(1)} %get-tuple-element.40), channel_id=1, source_target_pairs={{4,8},{8,4},{12,0},{0,12},{5,9},{9,5},{13,1},{1,13},{6,10},{10,6},... | collective-permute-start | bytes 3145736 | tf_op jit(solution)/shard_map/ppermute | solution.py:375
  75.2 8.3 %collective-permute-start.25 = (f32[4,9,64,128]{3,2,1,0:T(8,128)S(1)}, f32[4,9,64,128]{3,2,1,0:T(8,128)S(1)}, u32[]{:S(2)}, u32[]{:S(2)}) collective-permute-start(f32[4,9,64,128]{3,2,1,0:T(8,128)S(1)} %get-tuple-element.54), channel_id=1, source_target_pairs={{0,16},{16,0},{1,17},{17,1},{2,18},{18,2},{3,19},{19,3},{4,20},{20... | collective-permute-start | bytes 3538952 | tf_op jit(solution)/shard_map/ppermute | solution.py:382
  77.3 26.7 %collective-permute-start.23 = (f32[2,4,64,512]{3,2,1,0:T(8,128)S(1)}, f32[2,4,64,512]{3,2,1,0:T(8,128)S(1)}, u32[]{:S(2)}, u32[]{:S(2)}) collective-permute-start(f32[2,4,64,512]{3,2,1,0:T(8,128)S(1)} %get-tuple-element.50), channel_id=1, source_target_pairs={{1,2},{2,1},{3,0},{0,3},{5,6},{6,5},{7,4},{4,7},{9,10},{10,9},{11,... | collective-permute-start | bytes 3145736 | tf_op jit(solution)/shard_map/ppermute | solution.py:379
  80.5 24.8 %collective-permute-start.19 = (f32[2,4,64,512]{3,2,1,0:T(8,128)S(1)}, f32[2,4,64,512]{3,2,1,0:T(8,128)S(1)}, u32[]{:S(2)}, u32[]{:S(2)}) collective-permute-start(f32[2,4,64,512]{3,2,1,0:T(8,128)S(1)} %get-tuple-element.46), channel_id=1, source_target_pairs={{0,1},{1,0},{2,3},{3,2},{4,5},{5,4},{6,7},{7,6},{8,9},{9,8},{10,11... | collective-permute-start | bytes 3145736 | tf_op jit(solution)/shard_map/ppermute | solution.py:377
  82.3 32.8 %collective-permute-start.13 = (f32[4,64,512]{2,1,0:T(8,128)S(1)}, f32[4,64,512]{2,1,0:T(8,128)S(1)}, u32[]{:S(2)}, u32[]{:S(2)}) collective-permute-start(f32[4,64,512]{2,1,0:T(8,128)S(1)} %fusion.3), channel_id=1, source_target_pairs={{4,8},{8,4},{12,0},{0,12},{5,9},{9,5},{13,1},{1,13},{6,10},{10,6},... | collective-permute-start | bytes 1572872 | tf_op jit(solution)/shard_map/ppermute | solution.py:350
  83.8 22.4 %collective-permute-start.26 = (f32[9,64,128]{2,1,0:T(8,128)S(1)}, f32[9,64,128]{2,1,0:T(8,128)S(1)}, u32[]{:S(2)}, u32[]{:S(2)}) collective-permute-start(f32[9,64,128]{2,1,0:T(8,128)S(1)} %get-tuple-element.57), channel_id=1, source_target_pairs={{0,32},{32,64},{64,96},{96,0},{1,33},{33,65},{65,97},{97,1},{2,34}... | collective-permute-start | bytes 884744 | tf_op jit(solution)/shard_map/ppermute | solution.py:387
  85.7 21.9 %collective-permute-start.28 = (f32[9,64,128]{2,1,0:T(8,128)S(1)}, f32[9,64,128]{2,1,0:T(8,128)S(1)}, u32[]{:S(2)}, u32[]{:S(2)}) collective-permute-start(f32[9,64,128]{2,1,0:T(8,128)S(1)} %get-tuple-element.58), channel_id=1, source_target_pairs={{0,64},{32,96},{64,0},{96,32},{1,65},{33,97},{65,1},{97,33},{2,66}... | collective-permute-start | bytes 884744 | tf_op jit(solution)/shard_map/ppermute | solution.py:387
  104.0 9.1 %collective-permute-start.27 = (f32[9,64,128]{2,1,0:T(8,128)S(1)}, f32[9,64,128]{2,1,0:T(8,128)S(1)}, u32[]{:S(2)}, u32[]{:S(2)}) collective-permute-start(f32[9,64,128]{2,1,0:T(8,128)S(1)} %get-tuple-element.59), channel_id=1, source_target_pairs={{0,96},{32,0},{64,32},{96,64},{1,97},{33,1},{65,33},{97,65},{2,98}... | collective-permute-start | bytes 884744 | tf_op jit(solution)/shard_map/ppermute | solution.py:387
  105.3 12.5 %collective-permute-start.15 = (f32[4,64,512]{2,1,0:T(8,128)S(1)}, f32[4,64,512]{2,1,0:T(8,128)S(1)}, u32[]{:S(2)}, u32[]{:S(2)}) collective-permute-start(f32[4,64,512]{2,1,0:T(8,128)S(1)} %fusion.2), channel_id=1, source_target_pairs={{0,4},{4,0},{8,12},{12,8},{1,5},{5,1},{9,13},{13,9},{2,6},{6,2},{1... | collective-permute-start | bytes 1572872 | tf_op jit(solution)/shard_map/ppermute | solution.py:351
  106.2 13.7 %collective-permute-start.24 = (f32[4,64,512]{2,1,0:T(8,128)S(1)}, f32[4,64,512]{2,1,0:T(8,128)S(1)}, u32[]{:S(2)}, u32[]{:S(2)}) collective-permute-start(f32[4,64,512]{2,1,0:T(8,128)S(1)} %fusion), channel_id=1, source_target_pairs={{0,1},{1,0},{2,3},{3,2},{4,5},{5,4},{6,7},{7,6},{8,9},{9,8},{10,11... | collective-permute-start | bytes 1572872 | tf_op jit(solution)/shard_map/ppermute | solution.py:351
  107.6 12.9 %collective-permute-start.20 = (f32[4,64,512]{2,1,0:T(8,128)S(1)}, f32[4,64,512]{2,1,0:T(8,128)S(1)}, u32[]{:S(2)}, u32[]{:S(2)}) collective-permute-start(f32[4,64,512]{2,1,0:T(8,128)S(1)} %fusion.1), channel_id=1, source_target_pairs={{1,2},{2,1},{3,0},{0,3},{5,6},{6,5},{7,4},{4,7},{9,10},{10,9},{11,... | collective-permute-start | bytes 1572872 | tf_op jit(solution)/shard_map/ppermute | solution.py:350
  113.2 19.9 %collective-permute-start.29 = (f32[9,64,128]{2,1,0:T(8,128)S(1)}, f32[9,64,128]{2,1,0:T(8,128)S(1)}, u32[]{:S(2)}, u32[]{:S(2)}) collective-permute-start(f32[9,64,128]{2,1,0:T(8,128)S(1)} %fusion.6), channel_id=1, source_target_pairs={{0,0},{4,32},{8,64},{12,96},{32,4},{36,36},{40,68},{44,100},{64,8}... | collective-permute-start | bytes 884744 | tf_op jit(solution)/shard_map/ppermute | solution.py:389

commit v7 on v6

--- a/solution.py
+++ b/solution.py
@@ -357,7 +357,8 @@
     own, first, second, far = route_weights(at, along_z)
     got = (own, lax.ppermute(first, "x", FIRST), lax.ppermute(second, "x", SECOND), lax.ppermute(far, "x", OPPOSITE))
     got = jnp.stack(got)
-    return arrange_weights(at, got, lax.ppermute(got, "core", SWAP))
+    other = lax.ppermute(got, "core", SWAP)
+    return arrange_weights(at, got, other)
 
 
 def step(images, kernel, upstream):
@@ -369,11 +370,11 @@
 
     x_sides = edges(x_chunks)
     g_sides = edges(g_chunks)
-    out = conv((0, 1), at, x_chunks, x_sides, weights)
-    out_a, out_b = out[:3], out[3:]
+    out_a = conv((0,), at, x_chunks, x_sides, weights)
     out_one_a = lax.ppermute(out_a[2], "x", FIRST)
+    out_b = conv((1,), after(at, out_a[0]), x_chunks, x_sides, weights)
     out_one_b = lax.ppermute(out_b[2], "x", SECOND)
-    grad_a = conv((0,), after(at, out_a[0]), g_chunks, g_sides, turned)
+    grad_a = conv((0,), after(at, out_b[0]), g_chunks, g_sides, turned)
     grad_one_a = lax.ppermute(grad_a[2], "y", FIRST)
     grad_b = conv((1,), after(at, grad_a[0]), g_chunks, g_sides, turned)
     grad_one_b = lax.ppermute(grad_b[2], "y", SECOND)

time: 136 us -> 138 us (1.015)
  the two profiles are of different devices: /device:TPU:97 before, /device:TPU:14 now
where the time goes in v7:
time: 138 us; the launch traced here: 137 us
  starting transfers between devices  60.4 us (44%)
  waiting for transfers between devices  42.8 us (31%)
  Pallas kernels  31.9 us (23%)
    ppermute x3, starting transfers between devices, step(): total = total + lax.ppermute(near[k], 'z', ring(turn))  16.1 us
    pallas_call x4, Pallas kernels, conv(): pl.pallas_call(functools.partial(conv_kernel, halves, rows), out_shape=(s...  13.8 us
    ppermute x1, waiting for transfers between devices, step(): grad_one_b = lax.ppermute(grad_b[2], 'y', SECOND)  7.7 us
    pallas_call x1, Pallas kernels, weight_grads(): pl.pallas_call(kernel_grad_kernel, out_shape=(shape,) * 2, in_specs=[pl.B...  7.67 us
    ppermute x2, waiting for transfers between devices, reduce_second(): two_a = lax.ppermute(a[1] + one_a[1], axis, SECOND)  7.54 us
    ppermute x1, starting transfers between devices, step(): home = lax.ppermute(total, ('z', 'x'), cross)  7.42 us
    ppermute x1, waiting for transfers between devices, fetch_weights(): lax.ppermute(second, 'x', SECOND)  7.24 us
    ppermute x3, waiting for transfers between devices, gather(): lax.ppermute(block, axis, SECOND)  7.11 us
  transfers between devices with their start and end apart: 30, of which 13 were waited for; matrix products, arithmetic and copies ran while one was open for 1% of the time, Pallas kernels for 22%

profile of v7, /device:TPU:14, one launch (start us, length us, event | category | flops | bytes accessed | tf_op | source)
XLA Modules:
  0.0 137.5 jit_solution(15913992540848255620)
XLA Ops:
  0.6 4.0 %collective-permute-start.5 = (bf16[9,64,128]{2,1,0:T(8,128)(2,1)}, bf16[9,64,128]{2,1,0:T(8,128)(2,1)S(1)}, u32[]{:S(2)}, u32[]{:S(2)}) collective-permute-start(bf16[9,64,128]{2,1,0:T(8,128)(2,1)} %bitcast.73), channel_id=1, source_target_pairs={{0,64},{32,96},{64,0},{96,32},{1,65},{33,97},{65,1},{97,33},{2,66}... | collective-permute-start | bytes 442376 | tf_op jit(solution)/shard_map/ppermute | solution.py:337
  4.6 0.7 collective-permute-start.4
  5.3 0.3 collective-permute-start.3
  5.6 3.9 %pack.1 = (bf16[4,64,1024]{2,1,0:T(8,128)(2,1)S(1)}, bf16[4,64,1024]{2,1,0:T(8,128)(2,1)S(1)}) custom-call(bf16[8,8,4096]{2,1,0:T(8,128)(2,1)} %x_hbm.1, bf16[8,8,4096]{2,1,0:T(8,128)(2,1)} %g_hbm.1), custom_call_target="tpu_custom_call" | custom-call | tf_op jit(solution)/shard_map/pack/pallas_call | solution.py:73
  9.6 2.4 %collective-permute-start.2 = (bf16[4,64,1024]{2,1,0:T(8,128)(2,1)S(1)}, bf16[4,64,1024]{2,1,0:T(8,128)(2,1)S(1)}, u32[]{:S(2)}, u32[]{:S(2)}) collective-permute-start(bf16[4,64,1024]{2,1,0:T(8,128)(2,1)S(1)} %get-tuple-element.31.c0.x0), channel_id=1, source_target_pairs={{0,2},{1,3},{2,0},{3,1},{4,6},{5,7},{6,4},{7,5},{8,10},{9,11},{10,... | collective-permute-start | bytes 1572872 | tf_op jit(solution)/shard_map/ppermute | solution.py:337
  12.1 0.5 collective-permute-done.3.b1
  12.6 0.6 route.1
  13.2 0.9 collective-permute-start.6
  14.1 1.1 collective-permute-start.7
  15.3 2.1 %collective-permute-start.8 = (bf16[9,64,128]{2,1,0:T(8,128)(2,1)S(1)}, bf16[9,64,128]{2,1,0:T(8,128)(2,1)S(1)}, u32[]{:S(2)}, u32[]{:S(2)}) collective-permute-start(bf16[9,64,128]{2,1,0:T(8,128)(2,1)S(1)} %get-tuple-element.35), channel_id=1, source_target_pairs={{0,8},{4,12},{8,0},{12,4},{1,9},{5,13},{9,1},{13,5},{2,10},{6,14},... | collective-permute-start | bytes 442376 | tf_op jit(solution)/shard_map/ppermute | solution.py:358
  17.4 2.2 %collective-permute-done.6 = bf16[9,64,128]{2,1,0:T(8,128)(2,1)S(1)} collective-permute-done((bf16[9,64,128]{2,1,0:T(8,128)(2,1)S(1)}, bf16[9,64,128]{2,1,0:T(8,128)(2,1)S(1)}, u32[]{:S(2)}, u32[]{:S(2)}) %collective-permute-start.6) | collective-permute-done | bytes 147488 | tf_op jit(solution)/shard_map/ppermute | solution.py:358
  19.6 2.2 %collective-permute-start = (bf16[4,64,1024]{2,1,0:T(8,128)(2,1)S(1)}, bf16[4,64,1024]{2,1,0:T(8,128)(2,1)S(1)}, u32[]{:S(2)}, u32[]{:S(2)}) collective-permute-start(bf16[4,64,1024]{2,1,0:T(8,128)(2,1)S(1)} %get-tuple-element.31.c0.x0), channel_id=1, source_target_pairs={{0,1},{1,0},{2,3},{3,2},{4,5},{5,4},{6,7},{7,6},{8,9},{9,8},{10,11... | collective-permute-start | bytes 1572872 | tf_op jit(solution)/shard_map/ppermute | solution.py:337
  21.8 7.2 %collective-permute-done.7 = bf16[9,64,128]{2,1,0:T(8,128)(2,1)S(1)} collective-permute-done((bf16[9,64,128]{2,1,0:T(8,128)(2,1)S(1)}, bf16[9,64,128]{2,1,0:T(8,128)(2,1)S(1)}, u32[]{:S(2)}, u32[]{:S(2)}) %collective-permute-start.7) | collective-permute-done | bytes 147488 | tf_op jit(solution)/shard_map/ppermute | solution.py:358
  29.1 2.9 %collective-permute-start.17 = (bf16[4,64,1024]{2,1,0:T(8,128)(2,1)S(1)}, bf16[4,64,1024]{2,1,0:T(8,128)(2,1)S(1)}, u32[]{:S(2)}, u32[]{:S(2)}) collective-permute-start(bf16[4,64,1024]{2,1,0:T(8,128)(2,1)S(1)} %get-tuple-element.45.c0.g0), channel_id=1, source_target_pairs={{4,8},{8,4},{12,0},{0,12},{5,9},{9,5},{13,1},{1,13},{6,10},{10,6},... | collective-permute-start | bytes 1572872 | tf_op jit(solution)/shard_map/ppermute | solution.py:337
  32.1 0.7 collective-permute-start.16
  32.8 2.7 %collective-permute-done.1.c2.x2 = bf16[4,64,1024]{2,1,0:T(8,128)(2,1)S(1)} collective-permute-done((bf16[4,64,1024]{2,1,0:T(8,128)(2,1)S(1)}, bf16[4,64,1024]{2,1,0:T(8,128)(2,1)S(1)}, u32[]{:S(2)}, u32[]{:S(2)}) %collective-permute-start.1) | collective-permute-done | bytes 524320 | tf_op jit(solution)/shard_map/ppermute | solution.py:337
  35.5 0.1 collective-permute-done.c1.x1
  35.7 2.3 %collective-permute-start.12 = (bf16[4,4,64,128]{3,2,1,0:T(8,128)(2,1)S(1)}, bf16[4,4,64,128]{3,2,1,0:T(8,128)(2,1)S(1)}, u32[]{:S(2)}, u32[]{:S(2)}) collective-permute-start(bf16[4,4,64,128]{3,2,1,0:T(8,128)(2,1)S(1)} %pad_maximum_fusion.1), channel_id=1, source_target_pairs={{0,16},{16,32},{32,48},{48,64},{64,80},{80,96},{96,112},{1,17},{17... | collective-permute-start | bytes 786440 | tf_op jit(solution)/shard_map/ppermute | solution.py:346
  38.1 1.8 %collective-permute-done.18.c3.g3 = bf16[4,64,1024]{2,1,0:T(8,128)(2,1)S(1)} collective-permute-done((bf16[4,64,1024]{2,1,0:T(8,128)(2,1)S(1)}, bf16[4,64,1024]{2,1,0:T(8,128)(2,1)S(1)}, u32[]{:S(2)}, u32[]{:S(2)}) %collective-permute-start.18) | collective-permute-done | bytes 524320 | tf_op jit(solution)/shard_map/ppermute | solution.py:337
  39.9 1.3 collective-permute-start.13
  41.2 4.4 %collective-permute-done.17.c2.g2 = bf16[4,64,1024]{2,1,0:T(8,128)(2,1)S(1)} collective-permute-done((bf16[4,64,1024]{2,1,0:T(8,128)(2,1)S(1)}, bf16[4,64,1024]{2,1,0:T(8,128)(2,1)S(1)}, u32[]{:S(2)}, u32[]{:S(2)}) %collective-permute-start.17) | collective-permute-done | bytes 524320 | tf_op jit(solution)/shard_map/ppermute | solution.py:337
  45.7 1.3 collective-permute-start.21
  47.0 1.5 %collective-permute-start.22 = (bf16[4,4,64,128]{3,2,1,0:T(8,128)(2,1)S(1)}, bf16[4,4,64,128]{3,2,1,0:T(8,128)(2,1)S(1)}, u32[]{:S(2)}, u32[]{:S(2)}) collective-permute-start(bf16[4,4,64,128]{3,2,1,0:T(8,128)(2,1)S(1)} %pad_maximum_fusion.4), channel_id=1, source_target_pairs={{16,0},{32,16},{48,32},{64,48},{80,64},{96,80},{112,96},{17,1},{33... | collective-permute-start | bytes 786440 | tf_op jit(solution)/shard_map/ppermute | solution.py:346
  48.5 1.6 %weights.1 = (bf16[3,256,768]{2,1,0:T(8,128)(2,1)S(1)}, bf16[3,256,768]{2,1,0:T(8,128)(2,1)S(1)}) custom-call(s32[4]{0:T(128)S(1)} %pad_add_fusion.at, bf16[4,9,64,128]{3,2,1,0:T(8,128)(2,1)S(1)} %pad_maximum_fusion.mine, bf16[4,9,64,128]{3,2,1,0:T(8,128)(2,1)S(1)} %collective-permute-done.9.other), custom_call_target="tpu_custom_call" | custom-call | tf_op jit(solution)/shard_map/weights/pallas_call | solution.py:195
  50.1 3.4 %shard_map.58 = (f32[4,64,512]{2,1,0:T(8,128)S(1)}, f32[4,64,512]{2,1,0:T(8,128)S(1)}, f32[2,4,64,512]{3,2,1,0:T(8,128)S(1)}) custom-call(s32[4]{0:T(128)S(1)} %pad_add_fusion.at, bf16[4,64,1024]{2,1,0:T(8,128)(2,1)S(1)} %get-tuple-element.31.c0.x0, bf16[4,64,1024]{2,1,0:T(8,128)(2,1)S(1)} %collective-permute-done.c1.x1, ...), custom_call_target="tpu_custom_call" | custom-call | flops 2415919104 | bytes 6000000 | tf_op jit(solution)/shard_map/pallas_call | solution.py:264
  53.5 3.5 %shard_map.59 = (f32[4,64,512]{2,1,0:T(8,128)S(1)}, f32[4,64,512]{2,1,0:T(8,128)S(1)}, f32[2,4,64,512]{3,2,1,0:T(8,128)S(1)}) custom-call(s32[4]{0:T(128)S(1)} %pad_add_fusion.at, bf16[4,64,1024]{2,1,0:T(8,128)(2,1)S(1)} %get-tuple-element.31.c0.x0, bf16[4,64,1024]{2,1,0:T(8,128)(2,1)S(1)} %collective-permute-done.c1.x1, ...), custom_call_target="tpu_custom_call" | custom-call | flops 2415919104 | bytes 6000000 | tf_op jit(solution)/shard_map/pallas_call | solution.py:264
  57.0 1.7 %collective-permute-start.14 = (f32[2,4,64,512]{3,2,1,0:T(8,128)S(1)}, f32[2,4,64,512]{3,2,1,0:T(8,128)S(1)}, u32[]{:S(2)}, u32[]{:S(2)}) collective-permute-start(f32[2,4,64,512]{3,2,1,0:T(8,128)S(1)} %get-tuple-element.42), channel_id=1, source_target_pairs={{4,8},{8,4},{12,0},{0,12},{5,9},{9,5},{13,1},{1,13},{6,10},{10,6},... | collective-permute-start | bytes 3145736 | tf_op jit(solution)/shard_map/ppermute | solution.py:376
  58.7 3.4 %shard_map.60 = (f32[4,64,512]{2,1,0:T(8,128)S(1)}, f32[4,64,512]{2,1,0:T(8,128)S(1)}, f32[2,4,64,512]{3,2,1,0:T(8,128)S(1)}) custom-call(s32[4]{0:T(128)S(1)} %pad_add_fusion.at, bf16[4,64,1024]{2,1,0:T(8,128)(2,1)S(1)} %get-tuple-element.45.c0.g0, bf16[4,64,1024]{2,1,0:T(8,128)(2,1)S(1)} %collective-permute-done.16.c1.g1, ...), custom_call_target="tpu_custom_call" | custom-call | flops 2415919104 | bytes 6000000 | tf_op jit(solution)/shard_map/pallas_call | solution.py:264
  62.1 3.5 %shard_map.61 = (f32[4,64,512]{2,1,0:T(8,128)S(1)}, f32[4,64,512]{2,1,0:T(8,128)S(1)}, f32[2,4,64,512]{3,2,1,0:T(8,128)S(1)}) custom-call(s32[4]{0:T(128)S(1)} %pad_add_fusion.at, bf16[4,64,1024]{2,1,0:T(8,128)(2,1)S(1)} %get-tuple-element.45.c0.g0, bf16[4,64,1024]{2,1,0:T(8,128)(2,1)S(1)} %collective-permute-done.16.c1.g1, ...), custom_call_target="tpu_custom_call" | custom-call | flops 2415919104 | bytes 6000000 | tf_op jit(solution)/shard_map/pallas_call | solution.py:264
  65.7 7.7 %weight_grads.1 = (f32[4,9,64,128]{3,2,1,0:T(8,128)S(1)}, f32[4,9,64,128]{3,2,1,0:T(8,128)S(1)}) custom-call(s32[4]{0:T(128)S(1)} %pad_add_fusion.at, bf16[4,64,1024]{2,1,0:T(8,128)(2,1)S(1)} %get-tuple-element.31.c0.x0, bf16[4,64,1024]{2,1,0:T(8,128)(2,1)S(1)} %collective-permute-done.c1.x1, bf16[4,64,1024]{2,1,0:T(8,128)(2,1)S(1)} %collective-permute-done.1.c2.x2, ...), custom_call_target="tpu_custom_call" | custom-call | flops 4831838208 | bytes 9000000 | tf_op jit(solution)/shard_map/weight_grads/pallas_call | solution.py:315
  73.4 2.6 %collective-permute-start.25 = (f32[4,9,64,128]{3,2,1,0:T(8,128)S(1)}, f32[4,9,64,128]{3,2,1,0:T(8,128)S(1)}, u32[]{:S(2)}, u32[]{:S(2)}) collective-permute-start(f32[4,9,64,128]{3,2,1,0:T(8,128)S(1)} %get-tuple-element.56), channel_id=1, source_target_pairs={{0,16},{16,0},{1,17},{17,1},{2,18},{18,2},{3,19},{19,3},{4,20},{20... | collective-permute-start | bytes 3538952 | tf_op jit(solution)/shard_map/ppermute | solution.py:383
  76.0 1.6 %collective-permute-start.23 = (f32[2,4,64,512]{3,2,1,0:T(8,128)S(1)}, f32[2,4,64,512]{3,2,1,0:T(8,128)S(1)}, u32[]{:S(2)}, u32[]{:S(2)}) collective-permute-start(f32[2,4,64,512]{3,2,1,0:T(8,128)S(1)} %get-tuple-element.52), channel_id=1, source_target_pairs={{1,2},{2,1},{3,0},{0,3},{5,6},{6,5},{7,4},{4,7},{9,10},{10,9},{11,... | collective-permute-start | bytes 3145736 | tf_op jit(solution)/shard_map/ppermute | solution.py:380
  77.6 2.2 %collective-permute-start.19 = (f32[2,4,64,512]{3,2,1,0:T(8,128)S(1)}, f32[2,4,64,512]{3,2,1,0:T(8,128)S(1)}, u32[]{:S(2)}, u32[]{:S(2)}) collective-permute-start(f32[2,4,64,512]{3,2,1,0:T(8,128)S(1)} %get-tuple-element.48), channel_id=1, source_target_pairs={{0,1},{1,0},{2,3},{3,2},{4,5},{5,4},{6,7},{7,6},{8,9},{9,8},{10,11... | collective-permute-start | bytes 3145736 | tf_op jit(solution)/shard_map/ppermute | solution.py:378
  79.9 1.8 %collective-permute-done.14.one_b = f32[2,4,64,512]{3,2,1,0:T(8,128)S(1)} collective-permute-done((f32[2,4,64,512]{3,2,1,0:T(8,128)S(1)}, f32[2,4,64,512]{3,2,1,0:T(8,128)S(1)}, u32[]{:S(2)}, u32[]{:S(2)}) %collective-permute-start.14) | collective-permute-done | bytes 1048608 | tf_op jit(solution)/shard_map/ppermute | solution.py:376
  81.9 1.3 collective-permute-done.10.one_a
  83.3 0.2 add.28
  83.6 4.8 %collective-permute-start.26 = (f32[9,64,128]{2,1,0:T(8,128)S(1)}, f32[9,64,128]{2,1,0:T(8,128)S(1)}, u32[]{:S(2)}, u32[]{:S(2)}) collective-permute-start(f32[9,64,128]{2,1,0:T(8,128)S(1)} %get-tuple-element.59), channel_id=1, source_target_pairs={{0,32},{32,64},{64,96},{96,0},{1,33},{33,65},{65,97},{97,1},{2,34}... | collective-permute-start | bytes 884744 | tf_op jit(solution)/shard_map/ppermute | solution.py:388
  88.4 5.1 %collective-permute-start.28 = (f32[9,64,128]{2,1,0:T(8,128)S(1)}, f32[9,64,128]{2,1,0:T(8,128)S(1)}, u32[]{:S(2)}, u32[]{:S(2)}) collective-permute-start(f32[9,64,128]{2,1,0:T(8,128)S(1)} %get-tuple-element.60), channel_id=1, source_target_pairs={{0,64},{32,96},{64,0},{96,32},{1,65},{33,97},{65,1},{97,33},{2,66}... | collective-permute-start | bytes 884744 | tf_op jit(solution)/shard_map/ppermute | solution.py:388
  93.4 7.7 %collective-permute-done.23.one_b = f32[2,4,64,512]{3,2,1,0:T(8,128)S(1)} collective-permute-done((f32[2,4,64,512]{3,2,1,0:T(8,128)S(1)}, f32[2,4,64,512]{3,2,1,0:T(8,128)S(1)}, u32[]{:S(2)}, u32[]{:S(2)}) %collective-permute-start.23) | collective-permute-done | bytes 1048608 | tf_op jit(solution)/shard_map/ppermute | solution.py:380
  101.2 6.2 %collective-permute-start.27 = (f32[9,64,128]{2,1,0:T(8,128)S(1)}, f32[9,64,128]{2,1,0:T(8,128)S(1)}, u32[]{:S(2)}, u32[]{:S(2)}) collective-permute-start(f32[9,64,128]{2,1,0:T(8,128)S(1)} %get-tuple-element.61), channel_id=1, source_target_pairs={{0,96},{32,0},{64,32},{96,64},{1,97},{33,1},{65,33},{97,65},{2,98}... | collective-permute-start | bytes 884744 | tf_op jit(solution)/shard_map/ppermute | solution.py:388
  107.5 2.5 %collective-permute-start.11 = (f32[4,64,512]{2,1,0:T(8,128)S(1)}, f32[4,64,512]{2,1,0:T(8,128)S(1)}, u32[]{:S(2)}, u32[]{:S(2)}) collective-permute-start(f32[4,64,512]{2,1,0:T(8,128)S(1)} %fusion.3), channel_id=1, source_target_pairs={{4,8},{8,4},{12,0},{0,12},{5,9},{9,5},{13,1},{1,13},{6,10},{10,6},... | collective-permute-start | bytes 1572872 | tf_op jit(solution)/shard_map/ppermute | solution.py:350
  110.2 2.2 %collective-permute-start.20 = (f32[4,64,512]{2,1,0:T(8,128)S(1)}, f32[4,64,512]{2,1,0:T(8,128)S(1)}, u32[]{:S(2)}, u32[]{:S(2)}) collective-permute-start(f32[4,64,512]{2,1,0:T(8,128)S(1)} %fusion.1), channel_id=1, source_target_pairs={{1,2},{2,1},{3,0},{0,3},{5,6},{6,5},{7,4},{4,7},{9,10},{10,9},{11,... | collective-permute-start | bytes 1572872 | tf_op jit(solution)/shard_map/ppermute | solution.py:350
  112.4 1.0 collective-permute-done.27
  113.5 7.4 %collective-permute-start.29 = (f32[9,64,128]{2,1,0:T(8,128)S(1)}, f32[9,64,128]{2,1,0:T(8,128)S(1)}, u32[]{:S(2)}, u32[]{:S(2)}) collective-permute-start(f32[9,64,128]{2,1,0:T(8,128)S(1)} %fusion.6), channel_id=1, source_target_pairs={{0,0},{4,32},{8,64},{12,96},{32,4},{36,36},{40,68},{44,100},{64,8}... | collective-permute-start | bytes 884744 | tf_op jit(solution)/shard_map/ppermute | solution.py:390
  120.9 7.5 %collective-permute-done.11.two_a = f32[4,64,512]{2,1,0:T(8,128)S(1)} collective-permute-done((f32[4,64,512]{2,1,0:T(8,128)S(1)}, f32[4,64,512]{2,1,0:T(8,128)S(1)}, u32[]{:S(2)}, u32[]{:S(2)}) %collective-permute-start.11) | collective-permute-done | bytes 524320 | tf_op jit(solution)/shard_map/ppermute | solution.py:350
  128.5 2.2 %finish.2 = bf16[8,8,4096]{2,1,0:T(8,128)(2,1)} custom-call(f32[4,64,512]{2,1,0:T(8,128)S(1)} %get-tuple-element.37.own_a, f32[2,4,64,512]{3,2,1,0:T(8,128)S(1)} %collective-permute-done.10.one_a, f32[4,64,512]{2,1,0:T(8,128)S(1)} %collective-permute-done.11.two_a, f32[4,64,512]{2,1,0:T(8,128)S(1)} %get-tuple-element.41.own_b, ...), custom_call_target="tpu_custom_call" | custom-call | tf_op jit(solution)/shard_map/finish/pallas_call | solution.py:130
  130.6 4.4 %collective-permute-done.29.refs_0_ = f32[9,64,128]{2,1,0:T(8,128)S(1)} collective-permute-done((f32[9,64,128]{2,1,0:T(8,128)S(1)}, f32[9,64,128]{2,1,0:T(8,128)S(1)}, u32[]{:S(2)}, u32[]{:S(2)}) %collective-permute-start.29) | collective-permute-done | bytes 294944 | tf_op jit(solution)/shard_map/ppermute | solution.py:390
  135.1 2.2 %finish.3 = (bf16[8,8,4096]{2,1,0:T(8,128)(2,1)}, f32[9,64,128]{2,1,0:T(8,128)}) custom-call(f32[4,64,512]{2,1,0:T(8,128)S(1)} %get-tuple-element.47.own_a, f32[2,4,64,512]{3,2,1,0:T(8,128)S(1)} %collective-permute-done.19.one_a, f32[4,64,512]{2,1,0:T(8,128)S(1)} %collective-permute-done.20.two_a, f32[4,64,512]{2,1,0:T(8,128)S(1)} %get-tuple-element.51.own_b, ...), custom_call_target="tpu_custom_call" | custom-call | tf_op jit(solution)/shard_map/finish/pallas_call | solution.py:130
  (45 shorter events, 1.2 us)
Async XLA Ops:
  0.6 12.0 %copy-start = (bf16[3,3,64,128]{3,2,1,0:T(8,128)(2,1)S(1)}, bf16[3,3,64,128]{3,2,1,0:T(8,128)(2,1)}, u32[]{:S(2)}) copy-start(bf16[3,3,64,128]{3,2,1,0:T(8,128)(2,1)} %param.4) | copy-start | bytes 442372
  0.6 11.4 %collective-permute-start.5 = (bf16[9,64,128]{2,1,0:T(8,128)(2,1)}, bf16[9,64,128]{2,1,0:T(8,128)(2,1)S(1)}, u32[]{:S(2)}, u32[]{:S(2)}) collective-permute-start(bf16[9,64,128]{2,1,0:T(8,128)(2,1)} %bitcast.73), channel_id=1, source_target_pairs={{0,64},{32,96},{64,0},{96,32},{1,65},{33,97},{65,1},{97,33},{2,66}... | collective-permute-start | bytes 442376 | tf_op jit(solution)/shard_map/ppermute | solution.py:337
  4.6 7.5 %collective-permute-start.4 = (bf16[9,64,128]{2,1,0:T(8,128)(2,1)}, bf16[9,64,128]{2,1,0:T(8,128)(2,1)S(1)}, u32[]{:S(2)}, u32[]{:S(2)}) collective-permute-start(bf16[9,64,128]{2,1,0:T(8,128)(2,1)} %bitcast.74), channel_id=1, source_target_pairs={{32,64},{64,32},{96,0},{0,96},{33,65},{65,33},{97,1},{1,97},{34,66... | collective-permute-start | bytes 442376 | tf_op jit(solution)/shard_map/ppermute | solution.py:337
  5.3 7.3 %collective-permute-start.3 = (bf16[9,64,128]{2,1,0:T(8,128)(2,1)}, bf16[9,64,128]{2,1,0:T(8,128)(2,1)S(1)}, u32[]{:S(2)}, u32[]{:S(2)}) collective-permute-start(bf16[9,64,128]{2,1,0:T(8,128)(2,1)} %bitcast.75), channel_id=1, source_target_pairs={{0,32},{32,0},{64,96},{96,64},{1,33},{33,1},{65,97},{97,65},{2,34}... | collective-permute-start | bytes 442376 | tf_op jit(solution)/shard_map/ppermute | solution.py:337
  9.6 22.5 %collective-permute-start.2 = (bf16[4,64,1024]{2,1,0:T(8,128)(2,1)S(1)}, bf16[4,64,1024]{2,1,0:T(8,128)(2,1)S(1)}, u32[]{:S(2)}, u32[]{:S(2)}) collective-permute-start(bf16[4,64,1024]{2,1,0:T(8,128)(2,1)S(1)} %get-tuple-element.31.c0.x0), channel_id=1, source_target_pairs={{0,2},{1,3},{2,0},{3,1},{4,6},{5,7},{6,4},{7,5},{8,10},{9,11},{10,... | collective-permute-start | bytes 1572872 | tf_op jit(solution)/shard_map/ppermute | solution.py:337
  11.9 23.5 %collective-permute-start.1 = (bf16[4,64,1024]{2,1,0:T(8,128)(2,1)S(1)}, bf16[4,64,1024]{2,1,0:T(8,128)(2,1)S(1)}, u32[]{:S(2)}, u32[]{:S(2)}) collective-permute-start(bf16[4,64,1024]{2,1,0:T(8,128)(2,1)S(1)} %get-tuple-element.31.c0.x0), channel_id=1, source_target_pairs={{1,2},{2,1},{3,0},{0,3},{5,6},{6,5},{7,4},{4,7},{9,10},{10,9},{11,... | collective-permute-start | bytes 1572872 | tf_op jit(solution)/shard_map/ppermute | solution.py:337
  13.2 6.4 %collective-permute-start.6 = (bf16[9,64,128]{2,1,0:T(8,128)(2,1)S(1)}, bf16[9,64,128]{2,1,0:T(8,128)(2,1)S(1)}, u32[]{:S(2)}, u32[]{:S(2)}) collective-permute-start(bf16[9,64,128]{2,1,0:T(8,128)(2,1)S(1)} %get-tuple-element.33), channel_id=1, source_target_pairs={{0,4},{4,0},{8,12},{12,8},{1,5},{5,1},{9,13},{13,9},{2,6},{6,2},{1... | collective-permute-start | bytes 442376 | tf_op jit(solution)/shard_map/ppermute | solution.py:358
  14.1 14.9 %collective-permute-start.7 = (bf16[9,64,128]{2,1,0:T(8,128)(2,1)S(1)}, bf16[9,64,128]{2,1,0:T(8,128)(2,1)S(1)}, u32[]{:S(2)}, u32[]{:S(2)}) collective-permute-start(bf16[9,64,128]{2,1,0:T(8,128)(2,1)S(1)} %get-tuple-element.34), channel_id=1, source_target_pairs={{4,8},{8,4},{12,0},{0,12},{5,9},{9,5},{13,1},{1,13},{6,10},{10,6},... | collective-permute-start | bytes 442376 | tf_op jit(solution)/shard_map/ppermute | solution.py:358
  15.3 13.8 %collective-permute-start.8 = (bf16[9,64,128]{2,1,0:T(8,128)(2,1)S(1)}, bf16[9,64,128]{2,1,0:T(8,128)(2,1)S(1)}, u32[]{:S(2)}, u32[]{:S(2)}) collective-permute-start(bf16[9,64,128]{2,1,0:T(8,128)(2,1)S(1)} %get-tuple-element.35), channel_id=1, source_target_pairs={{0,8},{4,12},{8,0},{12,4},{1,9},{5,13},{9,1},{13,5},{2,10},{6,14},... | collective-permute-start | bytes 442376 | tf_op jit(solution)/shard_map/ppermute | solution.py:358
  19.6 16.0 %collective-permute-start = (bf16[4,64,1024]{2,1,0:T(8,128)(2,1)S(1)}, bf16[4,64,1024]{2,1,0:T(8,128)(2,1)S(1)}, u32[]{:S(2)}, u32[]{:S(2)}) collective-permute-start(bf16[4,64,1024]{2,1,0:T(8,128)(2,1)S(1)} %get-tuple-element.31.c0.x0), channel_id=1, source_target_pairs={{0,1},{1,0},{2,3},{3,2},{4,5},{5,4},{6,7},{7,6},{8,9},{9,8},{10,11... | collective-permute-start | bytes 1572872 | tf_op jit(solution)/shard_map/ppermute | solution.py:337
  29.1 10.8 %collective-permute-start.18 = (bf16[4,64,1024]{2,1,0:T(8,128)(2,1)S(1)}, bf16[4,64,1024]{2,1,0:T(8,128)(2,1)S(1)}, u32[]{:S(2)}, u32[]{:S(2)}) collective-permute-start(bf16[4,64,1024]{2,1,0:T(8,128)(2,1)S(1)} %get-tuple-element.45.c0.g0), channel_id=1, source_target_pairs={{0,8},{4,12},{8,0},{12,4},{1,9},{5,13},{9,1},{13,5},{2,10},{6,14},... | collective-permute-start | bytes 1572872 | tf_op jit(solution)/shard_map/ppermute | solution.py:337
  29.1 16.5 %collective-permute-start.17 = (bf16[4,64,1024]{2,1,0:T(8,128)(2,1)S(1)}, bf16[4,64,1024]{2,1,0:T(8,128)(2,1)S(1)}, u32[]{:S(2)}, u32[]{:S(2)}) collective-permute-start(bf16[4,64,1024]{2,1,0:T(8,128)(2,1)S(1)} %get-tuple-element.45.c0.g0), channel_id=1, source_target_pairs={{4,8},{8,4},{12,0},{0,12},{5,9},{9,5},{13,1},{1,13},{6,10},{10,6},... | collective-permute-start | bytes 1572872 | tf_op jit(solution)/shard_map/ppermute | solution.py:337
  32.1 13.5 %collective-permute-start.16 = (bf16[4,64,1024]{2,1,0:T(8,128)(2,1)S(1)}, bf16[4,64,1024]{2,1,0:T(8,128)(2,1)S(1)}, u32[]{:S(2)}, u32[]{:S(2)}) collective-permute-start(bf16[4,64,1024]{2,1,0:T(8,128)(2,1)S(1)} %get-tuple-element.45.c0.g0), channel_id=1, source_target_pairs={{0,4},{4,0},{8,12},{12,8},{1,5},{5,1},{9,13},{13,9},{2,6},{6,2},{1... | collective-permute-start | bytes 1572872 | tf_op jit(solution)/shard_map/ppermute | solution.py:337
  35.5 13.0 %collective-permute-start.9 = (bf16[4,9,64,128]{3,2,1,0:T(8,128)(2,1)S(1)}, bf16[4,9,64,128]{3,2,1,0:T(8,128)(2,1)S(1)}, u32[]{:S(2)}, u32[]{:S(2)}) collective-permute-start(bf16[4,9,64,128]{3,2,1,0:T(8,128)(2,1)S(1)} %pad_maximum_fusion.mine), channel_id=1, source_target_pairs={{0,16},{16,0},{1,17},{17,1},{2,18},{18,2},{3,19},{19,3},{4,20},{20... | collective-permute-start | bytes 1769480 | tf_op jit(solution)/shard_map/ppermute | solution.py:360
  35.7 17.8 %collective-permute-start.12 = (bf16[4,4,64,128]{3,2,1,0:T(8,128)(2,1)S(1)}, bf16[4,4,64,128]{3,2,1,0:T(8,128)(2,1)S(1)}, u32[]{:S(2)}, u32[]{:S(2)}) collective-permute-start(bf16[4,4,64,128]{3,2,1,0:T(8,128)(2,1)S(1)} %pad_maximum_fusion.1), channel_id=1, source_target_pairs={{0,16},{16,32},{32,48},{48,64},{64,80},{80,96},{96,112},{1,17},{17... | collective-permute-start | bytes 786440 | tf_op jit(solution)/shard_map/ppermute | solution.py:346
  39.9 13.6 %collective-permute-start.13 = (bf16[4,4,64,128]{3,2,1,0:T(8,128)(2,1)S(1)}, bf16[4,4,64,128]{3,2,1,0:T(8,128)(2,1)S(1)}, u32[]{:S(2)}, u32[]{:S(2)}) collective-permute-start(bf16[4,4,64,128]{3,2,1,0:T(8,128)(2,1)S(1)} %pad_maximum_fusion.2), channel_id=1, source_target_pairs={{16,0},{32,16},{48,32},{64,48},{80,64},{96,80},{112,96},{17,1},{33... | collective-permute-start | bytes 786440 | tf_op jit(solution)/shard_map/ppermute | solution.py:346
  45.7 16.4 %collective-permute-start.21 = (bf16[4,4,64,128]{3,2,1,0:T(8,128)(2,1)S(1)}, bf16[4,4,64,128]{3,2,1,0:T(8,128)(2,1)S(1)}, u32[]{:S(2)}, u32[]{:S(2)}) collective-permute-start(bf16[4,4,64,128]{3,2,1,0:T(8,128)(2,1)S(1)} %pad_maximum_fusion.3), channel_id=1, source_target_pairs={{0,16},{16,32},{32,48},{48,64},{64,80},{80,96},{96,112},{1,17},{17... | collective-permute-start | bytes 786440 | tf_op jit(solution)/shard_map/ppermute | solution.py:346
  47.0 15.1 %collective-permute-start.22 = (bf16[4,4,64,128]{3,2,1,0:T(8,128)(2,1)S(1)}, bf16[4,4,64,128]{3,2,1,0:T(8,128)(2,1)S(1)}, u32[]{:S(2)}, u32[]{:S(2)}) collective-permute-start(bf16[4,4,64,128]{3,2,1,0:T(8,128)(2,1)S(1)} %pad_maximum_fusion.4), channel_id=1, source_target_pairs={{16,0},{32,16},{48,32},{64,48},{80,64},{96,80},{112,96},{17,1},{33... | collective-permute-start | bytes 786440 | tf_op jit(solution)/shard_map/ppermute | solution.py:346
  57.0 24.7 %collective-permute-start.14 = (f32[2,4,64,512]{3,2,1,0:T(8,128)S(1)}, f32[2,4,64,512]{3,2,1,0:T(8,128)S(1)}, u32[]{:S(2)}, u32[]{:S(2)}) collective-permute-start(f32[2,4,64,512]{3,2,1,0:T(8,128)S(1)} %get-tuple-element.42), channel_id=1, source_target_pairs={{4,8},{8,4},{12,0},{0,12},{5,9},{9,5},{13,1},{1,13},{6,10},{10,6},... | collective-permute-start | bytes 3145736 | tf_op jit(solution)/shard_map/ppermute | solution.py:376
  58.7 24.4 %collective-permute-start.10 = (f32[2,4,64,512]{3,2,1,0:T(8,128)S(1)}, f32[2,4,64,512]{3,2,1,0:T(8,128)S(1)}, u32[]{:S(2)}, u32[]{:S(2)}) collective-permute-start(f32[2,4,64,512]{3,2,1,0:T(8,128)S(1)} %get-tuple-element.38), channel_id=1, source_target_pairs={{0,4},{4,0},{8,12},{12,8},{1,5},{5,1},{9,13},{13,9},{2,6},{6,2},{1... | collective-permute-start | bytes 3145736 | tf_op jit(solution)/shard_map/ppermute | solution.py:374
  73.4 9.9 %collective-permute-start.25 = (f32[4,9,64,128]{3,2,1,0:T(8,128)S(1)}, f32[4,9,64,128]{3,2,1,0:T(8,128)S(1)}, u32[]{:S(2)}, u32[]{:S(2)}) collective-permute-start(f32[4,9,64,128]{3,2,1,0:T(8,128)S(1)} %get-tuple-element.56), channel_id=1, source_target_pairs={{0,16},{16,0},{1,17},{17,1},{2,18},{18,2},{3,19},{19,3},{4,20},{20... | collective-permute-start | bytes 3538952 | tf_op jit(solution)/shard_map/ppermute | solution.py:383
  76.0 25.2 %collective-permute-start.23 = (f32[2,4,64,512]{3,2,1,0:T(8,128)S(1)}, f32[2,4,64,512]{3,2,1,0:T(8,128)S(1)}, u32[]{:S(2)}, u32[]{:S(2)}) collective-permute-start(f32[2,4,64,512]{3,2,1,0:T(8,128)S(1)} %get-tuple-element.52), channel_id=1, source_target_pairs={{1,2},{2,1},{3,0},{0,3},{5,6},{6,5},{7,4},{4,7},{9,10},{10,9},{11,... | collective-permute-start | bytes 3145736 | tf_op jit(solution)/shard_map/ppermute | solution.py:380
  77.6 29.8 %collective-permute-start.19 = (f32[2,4,64,512]{3,2,1,0:T(8,128)S(1)}, f32[2,4,64,512]{3,2,1,0:T(8,128)S(1)}, u32[]{:S(2)}, u32[]{:S(2)}) collective-permute-start(f32[2,4,64,512]{3,2,1,0:T(8,128)S(1)} %get-tuple-element.48), channel_id=1, source_target_pairs={{0,1},{1,0},{2,3},{3,2},{4,5},{5,4},{6,7},{7,6},{8,9},{9,8},{10,11... | collective-permute-start | bytes 3145736 | tf_op jit(solution)/shard_map/ppermute | solution.py:378
  81.8 39.1 %collective-permute-start.15 = (f32[4,64,512]{2,1,0:T(8,128)S(1)}, f32[4,64,512]{2,1,0:T(8,128)S(1)}, u32[]{:S(2)}, u32[]{:S(2)}) collective-permute-start(f32[4,64,512]{2,1,0:T(8,128)S(1)} %fusion.2), channel_id=1, source_target_pairs={{0,4},{4,0},{8,12},{12,8},{1,5},{5,1},{9,13},{13,9},{2,6},{6,2},{1... | collective-permute-start | bytes 1572872 | tf_op jit(solution)/shard_map/ppermute | solution.py:351
  83.6 26.5 %collective-permute-start.26 = (f32[9,64,128]{2,1,0:T(8,128)S(1)}, f32[9,64,128]{2,1,0:T(8,128)S(1)}, u32[]{:S(2)}, u32[]{:S(2)}) collective-permute-start(f32[9,64,128]{2,1,0:T(8,128)S(1)} %get-tuple-element.59), channel_id=1, source_target_pairs={{0,32},{32,64},{64,96},{96,0},{1,33},{33,65},{65,97},{97,1},{2,34}... | collective-permute-start | bytes 884744 | tf_op jit(solution)/shard_map/ppermute | solution.py:388
  88.4 21.8 %collective-permute-start.28 = (f32[9,64,128]{2,1,0:T(8,128)S(1)}, f32[9,64,128]{2,1,0:T(8,128)S(1)}, u32[]{:S(2)}, u32[]{:S(2)}) collective-permute-start(f32[9,64,128]{2,1,0:T(8,128)S(1)} %get-tuple-element.60), channel_id=1, source_target_pairs={{0,64},{32,96},{64,0},{96,32},{1,65},{33,97},{65,1},{97,33},{2,66}... | collective-permute-start | bytes 884744 | tf_op jit(solution)/shard_map/ppermute | solution.py:388
  101.2 12.2 %collective-permute-start.27 = (f32[9,64,128]{2,1,0:T(8,128)S(1)}, f32[9,64,128]{2,1,0:T(8,128)S(1)}, u32[]{:S(2)}, u32[]{:S(2)}) collective-permute-start(f32[9,64,128]{2,1,0:T(8,128)S(1)} %get-tuple-element.61), channel_id=1, source_target_pairs={{0,96},{32,0},{64,32},{96,64},{1,97},{33,1},{65,33},{97,65},{2,98}... | collective-permute-start | bytes 884744 | tf_op jit(solution)/shard_map/ppermute | solution.py:388
  107.5 21.0 %collective-permute-start.11 = (f32[4,64,512]{2,1,0:T(8,128)S(1)}, f32[4,64,512]{2,1,0:T(8,128)S(1)}, u32[]{:S(2)}, u32[]{:S(2)}) collective-permute-start(f32[4,64,512]{2,1,0:T(8,128)S(1)} %fusion.3), channel_id=1, source_target_pairs={{4,8},{8,4},{12,0},{0,12},{5,9},{9,5},{13,1},{1,13},{6,10},{10,6},... | collective-permute-start | bytes 1572872 | tf_op jit(solution)/shard_map/ppermute | solution.py:350
  110.1 20.6 %collective-permute-start.24 = (f32[4,64,512]{2,1,0:T(8,128)S(1)}, f32[4,64,512]{2,1,0:T(8,128)S(1)}, u32[]{:S(2)}, u32[]{:S(2)}) collective-permute-start(f32[4,64,512]{2,1,0:T(8,128)S(1)} %fusion), channel_id=1, source_target_pairs={{0,1},{1,0},{2,3},{3,2},{4,5},{5,4},{6,7},{7,6},{8,9},{9,8},{10,11... | collective-permute-start | bytes 1572872 | tf_op jit(solution)/shard_map/ppermute | solution.py:351
  110.2 20.5 %collective-permute-start.20 = (f32[4,64,512]{2,1,0:T(8,128)S(1)}, f32[4,64,512]{2,1,0:T(8,128)S(1)}, u32[]{:S(2)}, u32[]{:S(2)}) collective-permute-start(f32[4,64,512]{2,1,0:T(8,128)S(1)} %fusion.1), channel_id=1, source_target_pairs={{1,2},{2,1},{3,0},{0,3},{5,6},{6,5},{7,4},{4,7},{9,10},{10,9},{11,... | collective-permute-start | bytes 1572872 | tf_op jit(solution)/shard_map/ppermute | solution.py:350
  113.5 21.6 %collective-permute-start.29 = (f32[9,64,128]{2,1,0:T(8,128)S(1)}, f32[9,64,128]{2,1,0:T(8,128)S(1)}, u32[]{:S(2)}, u32[]{:S(2)}) collective-permute-start(f32[9,64,128]{2,1,0:T(8,128)S(1)} %fusion.6), channel_id=1, source_target_pairs={{0,0},{4,32},{8,64},{12,96},{32,4},{36,36},{40,68},{44,100},{64,8}... | collective-permute-start | bytes 884744 | tf_op jit(solution)/shard_map/ppermute | solution.py:390
